TPU v7x, 32 devices: a whole 2x2x4 slice. The times are simulated.
32 devices in a mesh: fsdp: 32 (over z, y, x, core).
Axes of the slice: x: 2, y: 2, z: 4, core: 2. Of those that a mesh axis runs over, the one named last changes fastest.
Arguments:
- images: bfloat16 [2, 64, 197, 384], P(None, 'fsdp'), may hold values from -6 to 6
- counts: int32 [2, 32], P(None, 'fsdp'), may hold values from 1 to 2, as said below
- out_grad: bfloat16 [2, 64, 197, 384], P(None, 'fsdp'), may hold values from -6 to 6
- qkv_weight: bfloat16 [442368], P('fsdp'), may hold values from -0.3125 to 0.3125
- out_weight: bfloat16 [147456], P('fsdp'), may hold values from -1.75 to 1.75
- fc1_weight: bfloat16 [589824], P('fsdp'), may hold values from -0.3125 to 0.3125
- fc2_weight: bfloat16 [589824], P('fsdp'), may hold values from -0.15625 to 0.15625
- norm_gains: bfloat16 [768], P('fsdp'), may hold values from 0.5 to 1.5
- biases: bfloat16 [3840], P('fsdp'), may hold values from -3 to 3
Outputs:
- block_out: float32 [2, 64, 197, 384], P(None, 'fsdp')
- input_grad: float32 [2, 64, 197, 384], P(None, 'fsdp')
- qkv_grad: float32 [442368], P('fsdp')
- out_grad_weight: float32 [147456], P('fsdp')
- fc1_grad: float32 [589824], P('fsdp')
- fc2_grad: float32 [589824], P('fsdp')
- gain_grad: float32 [768], P('fsdp')
- bias_grad: float32 [3840], P('fsdp')
Inputs may be any that keep to these rules, and one draw needn't show every extreme that they name: Device d holds counts[m, d] live images of micro-batch m in its first slots; its other slots of the 2 are empty. In every micro-batch some device holds 2 and some holds 1.
All inputs are finite; a program needn't handle non-finite values.
Results may differ from a plain program's by a relative error of at most 0.0098.
Values may be sent and summed in bfloat16 or wider, within the bound.
No kernel may reach another device: no remote copies, remote signals or barrier semaphores. Data moves between devices by JAX's collectives and lax.ppermute only.
A program may use at most 128 MiB of HBM per device.

v0:
```python
import math

import jax
import jax.numpy as jnp
from jax import lax
from jax.sharding import PartitionSpec as P

D = 384
H = 6
FF = 1536
HD = 64
S = 197
MB = 2


eps_norm = 1e-06


def norm_fwd(rows_in, gain_vec, shift_vec):
    row_mean = jnp.mean(rows_in, axis=-1, keepdims=True)
    centred = rows_in - row_mean
    variance = jnp.mean(centred * centred, axis=-1, keepdims=True)
    inverse = lax.rsqrt(variance + eps_norm)
    normal_rows = centred * inverse
    return (normal_rows * gain_vec + shift_vec, normal_rows, inverse)


def norm_back(grad_normed, normal_rows, inverse, gain_vec):
    scaled = grad_normed * gain_vec
    return inverse * (
        scaled
        - jnp.mean(scaled, axis=-1, keepdims=True)
        - normal_rows * jnp.mean(scaled * normal_rows, axis=-1, keepdims=True)
    )


def unpack(gathered):
    qkv_flat, out_flat, fc1_flat, fc2_flat, gain_flat, bias_flat = gathered
    return (
        qkv_flat.reshape(D, 3 * D),
        out_flat.reshape(D, D),
        fc1_flat.reshape(D, FF),
        fc2_flat.reshape(FF, D),
        gain_flat.astype(jnp.float32),
        bias_flat.astype(jnp.float32),
    )


def head_scores(query_low, key_low):
    return jnp.einsum("bqhd,bkhd->bhqk", query_low, key_low, preferred_element_type=jnp.float32) * (
        1.0 / math.sqrt(HD)
    )


def forward(image_slots, params):
    w_qkv, w_out, w_fc1, w_fc2, gain_all, bias_all = params
    count_img = image_slots.shape[0]
    row_count = count_img * S
    shape_heads = (count_img, S, H, HD)
    rows_in = image_slots.astype(jnp.float32).reshape(row_count, D)
    normed, normal_one, inverse_one = norm_fwd(rows_in, gain_all[:D], bias_all[:D])
    normed_low = normed.astype(jnp.bfloat16)
    mixed = jnp.dot(normed_low, w_qkv, preferred_element_type=jnp.float32)
    query_low = (mixed[:, :D] + bias_all[4 * D : 5 * D]).astype(jnp.bfloat16).reshape(shape_heads)
    key_low = mixed[:, D : 2 * D].astype(jnp.bfloat16).reshape(shape_heads)
    value_low = (
        (mixed[:, 2 * D :] + bias_all[5 * D : 6 * D]).astype(jnp.bfloat16).reshape(shape_heads)
    )
    scores = head_scores(query_low, key_low)
    row_peak = jnp.max(scores, axis=-1, keepdims=True)
    exp_scores = jnp.exp(scores - row_peak)
    row_total = jnp.sum(exp_scores, axis=-1, keepdims=True)
    prob_low = (exp_scores / row_total).astype(jnp.bfloat16)
    log_total = row_peak + jnp.log(row_total)
    attended = jnp.einsum(
        "bhqk,bkhd->bqhd", prob_low, value_low, preferred_element_type=jnp.float32
    )
    attended = attended.reshape(row_count, D).astype(jnp.bfloat16)
    residual = (
        rows_in
        + jnp.dot(attended, w_out, preferred_element_type=jnp.float32)
        + bias_all[2 * D : 3 * D]
    )
    normed_two, normal_two, inverse_two = norm_fwd(residual, gain_all[D:], bias_all[D : 2 * D])
    normed_two_low = normed_two.astype(jnp.bfloat16)
    hidden_in = (
        jnp.dot(normed_two_low, w_fc1, preferred_element_type=jnp.float32) + bias_all[6 * D :]
    )
    active_low = jax.nn.gelu(hidden_in, approximate=False).astype(jnp.bfloat16)
    block_rows = (
        residual
        + jnp.dot(active_low, w_fc2, preferred_element_type=jnp.float32)
        + bias_all[3 * D : 4 * D]
    )
    kept = (
        normal_one,
        inverse_one,
        normed_low,
        query_low,
        key_low,
        value_low,
        log_total,
        attended,
        normal_two,
        inverse_two,
        normed_two_low,
        hidden_in,
        active_low,
    )
    return (block_rows, kept)


def backward(grad_rows, kept, params):
    w_qkv, w_out, w_fc1, w_fc2, gain_all, bias_all = params
    (
        normal_one,
        inverse_one,
        normed_low,
        query_low,
        key_low,
        value_low,
        log_total,
        attended,
        normal_two,
        inverse_two,
        normed_two_low,
        hidden_in,
        active_low,
    ) = kept
    shape_heads = query_low.shape
    row_count = grad_rows.shape[0]
    grad_low = grad_rows.astype(jnp.bfloat16)
    gb_fc2 = jnp.sum(grad_low.astype(jnp.float32), axis=0)
    grad_active = jnp.einsum("rd,fd->rf", grad_low, w_fc2, preferred_element_type=jnp.float32)
    cumulative = 0.5 * (1.0 + lax.erf(hidden_in * (1.0 / math.sqrt(2.0))))
    density = jnp.exp(-0.5 * hidden_in * hidden_in) * (1.0 / math.sqrt(2.0 * math.pi))
    grad_hidden = (grad_active * (cumulative + hidden_in * density)).astype(jnp.bfloat16)
    gb_fc1 = jnp.sum(grad_hidden.astype(jnp.float32), axis=0)
    grad_normed_two = jnp.einsum(
        "rf,df->rd", grad_hidden, w_fc1, preferred_element_type=jnp.float32
    )
    g_gain_two = jnp.sum(grad_normed_two * normal_two, axis=0)
    gb_norm_two = jnp.sum(grad_normed_two, axis=0)
    grad_residual = grad_rows + norm_back(grad_normed_two, normal_two, inverse_two, gain_all[D:])
    grad_res_low = grad_residual.astype(jnp.bfloat16)
    gb_out = jnp.sum(grad_res_low.astype(jnp.float32), axis=0)
    grad_att = jnp.einsum("re,de->rd", grad_res_low, w_out, preferred_element_type=jnp.float32)
    grad_att_low = grad_att.astype(jnp.bfloat16).reshape(shape_heads)
    probs = jnp.exp(head_scores(query_low, key_low) - log_total)
    prob_low = probs.astype(jnp.bfloat16)
    grad_probs = jnp.einsum(
        "bqhd,bkhd->bhqk", grad_att_low, value_low, preferred_element_type=jnp.float32
    )
    grad_value = jnp.einsum(
        "bhqk,bqhd->bkhd", prob_low, grad_att_low, preferred_element_type=jnp.float32
    ).astype(jnp.bfloat16)
    row_dot = jnp.sum(probs * grad_probs, axis=-1, keepdims=True)
    grad_scores = (probs * (grad_probs - row_dot)).astype(jnp.bfloat16)
    head_scale = 1.0 / math.sqrt(HD)
    grad_query = (
        jnp.einsum("bhqk,bkhd->bqhd", grad_scores, key_low, preferred_element_type=jnp.float32)
        * head_scale
    ).astype(jnp.bfloat16)
    grad_key = (
        jnp.einsum("bhqk,bqhd->bkhd", grad_scores, query_low, preferred_element_type=jnp.float32)
        * head_scale
    ).astype(jnp.bfloat16)
    grad_mixed = jnp.concatenate(
        [
            grad_query.reshape(row_count, D),
            grad_key.reshape(row_count, D),
            grad_value.reshape(row_count, D),
        ],
        axis=1,
    )
    gb_query = jnp.sum(grad_query.reshape(row_count, D).astype(jnp.float32), axis=0)
    gb_value = jnp.sum(grad_value.reshape(row_count, D).astype(jnp.float32), axis=0)
    grad_normed = jnp.einsum("re,de->rd", grad_mixed, w_qkv, preferred_element_type=jnp.float32)
    g_gain_one = jnp.sum(grad_normed * normal_one, axis=0)
    gb_norm_one = jnp.sum(grad_normed, axis=0)
    grad_input = grad_residual + norm_back(grad_normed, normal_one, inverse_one, gain_all[:D])
    g_gains = jnp.concatenate([g_gain_one, g_gain_two])
    g_biases = jnp.concatenate(
        [gb_norm_one, gb_norm_two, gb_out, gb_fc2, gb_query, gb_value, gb_fc1]
    )
    operands = (
        normed_low,
        grad_mixed,
        attended,
        grad_res_low,
        normed_two_low,
        grad_hidden,
        active_low,
        grad_low,
    )
    return (grad_input, g_gains, g_biases, operands)


def local(
    images, counts, out_grad, qkv_weight, out_weight, fc1_weight, fc2_weight, norm_gains, biases
):
    gain_total = jnp.zeros((2 * D,), jnp.float32)
    bias_total = jnp.zeros((6 * D + FF,), jnp.float32)
    outputs = []
    input_grads = []
    operand_list = []
    slot_count = images.shape[1]
    for micro in range(MB):
        fwd_set = (
            lax.all_gather(qkv_weight, "fsdp", axis=0, tiled=True),
            lax.all_gather(out_weight, "fsdp", axis=0, tiled=True),
            lax.all_gather(fc1_weight, "fsdp", axis=0, tiled=True),
            lax.all_gather(fc2_weight, "fsdp", axis=0, tiled=True),
            lax.all_gather(norm_gains, "fsdp", axis=0, tiled=True),
            lax.all_gather(biases, "fsdp", axis=0, tiled=True),
        )
        live = (jnp.arange(slot_count, dtype=jnp.int32) < counts[micro, 0]).astype(jnp.float32)
        block_rows, kept = forward(images[micro], unpack(fwd_set))
        outputs.append(block_rows.reshape(slot_count, S, D) * live[:, None, None])
        grad_rows = (out_grad[micro].astype(jnp.float32) * live[:, None, None]).reshape(
            slot_count * S, D
        )
        bwd_set = (
            lax.all_gather(qkv_weight, "fsdp", axis=0, tiled=True),
            lax.all_gather(out_weight, "fsdp", axis=0, tiled=True),
            lax.all_gather(fc1_weight, "fsdp", axis=0, tiled=True),
            lax.all_gather(fc2_weight, "fsdp", axis=0, tiled=True),
            lax.all_gather(norm_gains, "fsdp", axis=0, tiled=True),
            lax.all_gather(biases, "fsdp", axis=0, tiled=True),
        )
        grad_input, g_gains, g_biases, operands = backward(grad_rows, kept, unpack(bwd_set))
        input_grads.append(grad_input.reshape(slot_count, S, D))
        gain_total = gain_total + g_gains
        bias_total = bias_total + g_biases
        operand_list.append(operands)

    def joined(position):
        return jnp.concatenate([entry[position] for entry in operand_list], axis=0)

    g_qkv = jnp.einsum("rd,re->de", joined(0), joined(1), preferred_element_type=jnp.float32)
    g_out = jnp.einsum("rd,re->de", joined(2), joined(3), preferred_element_type=jnp.float32)
    g_fc1 = jnp.einsum("rd,rf->df", joined(4), joined(5), preferred_element_type=jnp.float32)
    g_fc2 = jnp.einsum("rf,rd->fd", joined(6), joined(7), preferred_element_type=jnp.float32)
    summed = (
        lax.psum_scatter(g_qkv.reshape(-1), "fsdp", scatter_dimension=0, tiled=True),
        lax.psum_scatter(g_out.reshape(-1), "fsdp", scatter_dimension=0, tiled=True),
        lax.psum_scatter(g_fc1.reshape(-1), "fsdp", scatter_dimension=0, tiled=True),
        lax.psum_scatter(g_fc2.reshape(-1), "fsdp", scatter_dimension=0, tiled=True),
        lax.psum_scatter(gain_total, "fsdp", scatter_dimension=0, tiled=True),
        lax.psum_scatter(bias_total, "fsdp", scatter_dimension=0, tiled=True),
    )
    return (
        jnp.stack(outputs),
        jnp.stack(input_grads),
        summed[0],
        summed[1],
        summed[2],
        summed[3],
        summed[4],
        summed[5],
    )


def solution(mesh):
    placed = (
        P(None, "fsdp", None, None),
        P(None, "fsdp"),
        P(None, "fsdp", None, None),
        P("fsdp"),
        P("fsdp"),
        P("fsdp"),
        P("fsdp"),
        P("fsdp"),
        P("fsdp"),
    )
    return jax.shard_map(
        local,
        mesh=mesh,
        in_specs=placed,
        out_specs=(
            P(None, "fsdp", None, None),
            P(None, "fsdp", None, None),
            P("fsdp"),
            P("fsdp"),
            P("fsdp"),
            P("fsdp"),
            P("fsdp"),
            P("fsdp"),
        ),
        check_vma=False,
    )
```

profile of v0, /device:TPU:0, one launch (start us, length us, event | category | flops | bytes accessed | tf_op | source)
XLA Modules:
  0.0 500.7 jit_solution(9114908147450705660)
XLA Ops:
  8.8 2.3 slice_convert_fusion.3
  11.1 1.6 convert_reduce_fusion.11
  13.2 42.2 %all-reduce.10 = (bf16[768]{0:T(1024)(128)(2,1)S(1)}, bf16[3840]{0:T(1024)(128)(2,1)S(1)}) all-reduce(bf16[768]{0:T(1024)(128)(2,1)S(1)} %dynamic-update-slice, bf16[3840]{0:T(1024)(128)(2,1)S(1)} %dynamic-update-slice.1), channel_id=1, replica_groups=mesh['fsdp'=32] {'fsdp'}, use_global_device_ids=true, to_apply=%add | all-reduce | flops 4608 | bytes 18432
  57.2 5.4 %multiply_reduce_fusion.15 = (f32[2,197]{0,1:T(8,128)S(1)}, f32[2,197]{0,1:T(8,128)S(1)}) fusion(f32[2,197]{0,1:T(8,128)S(1)} %broadcast_multiply_fusion.3, bf16[2,2,197,384]{3,1,2,0:T(2,128)(2,1)S(1)} %copy-done.3, f32[2,197]{0,1:T(8,128)S(1)} %broadcast_multiply_fusion.2), kind=kLoop, calls=%fused_computation.179 | loop fusion | flops 1209580 | bytes 611488 | tf_op jit(solution)/shard_map/reduce_sum | solution.py:22
  70.7 46.5 %all-gather = bf16[32,1,13824]{2,1,0:T(2,128)(2,1)S(1)} all-gather(bf16[1,1,13824]{2,1,0:T(2,128)(2,1)S(1)} %reshape.419), channel_id=1, replica_groups=mesh['fsdp'=32] {'fsdp'}, dimensions={0}, use_global_device_ids=true | all-gather | bytes 912384 | tf_op jit(solution)/shard_map/all_gather | solution.py:210
  117.2 5.3 %reduce.10 = bf16[32,13824]{1,0:T(8,128)(2,1)S(1)} reduce(bf16[32,1,13824]{2,1,0:T(2,128)(2,1)S(1)} %all-gather, bf16[]{:T(256)} %constant.121), dimensions={1}, to_apply=%all-gather.reduce_sub_computation | reduce | bytes 1769474 | tf_op jit(solution)/shard_map/all_gather | solution.py:210
  135.0 38.3 %all-gather.1 = bf16[32,1,4608]{2,1,0:T(2,128)(2,1)S(1)} all-gather(bf16[1,1,4608]{2,1,0:T(2,128)(2,1)S(1)} %reshape.421), channel_id=1, replica_groups=mesh['fsdp'=32] {'fsdp'}, dimensions={0}, use_global_device_ids=true | all-gather | bytes 304128 | tf_op jit(solution)/shard_map/all_gather | solution.py:211
  173.2 1.7 reduce.11
  177.4 2.4 reshape.425
  179.8 2.3 copy.164
  191.2 1.8 fusion.104
  193.2 2.4 fusion.105
  197.5 2.0 reshape.414
  199.6 2.0 reshape.413
  206.3 2.2 add_convert_fusion.3
  208.5 3.5 reshape.392
  212.0 8.1 %fusion.7 = (bf16[394,1536]{1,0:T(8,128)(2,1)}, f32[394,1536]{1,0:T(8,128)}) fusion(f32[1536]{0:T(1024)S(1)} %copy-done.84, bf16[394,384]{1,0:T(8,128)(2,1)} %get-tuple-element.98, bf16[384,1536]{1,0:T(8,128)(2,1)} %reshape.392), kind=kOutput, calls=%fused_computation.15 | convolution fusion | flops 504723456 | bytes 5119488 | tf_op jit(solution)/shard_map/dot_general | solution.py:87
  220.1 3.1 reshape.393
  223.2 3.5 fusion.46
  226.7 1.9 reshape.398
  228.6 8.1 %fusion.4 = (bf16[394,1536]{1,0:T(8,128)(2,1)S(1)}, f32[394,1536]{1,0:T(8,128)}) fusion(f32[1536]{0:T(1024)S(1)} %copy-done.84, bf16[394,384]{1,0:T(8,128)(2,1)} %get-tuple-element.97, bf16[384,1536]{1,0:T(8,128)(2,1)} %reshape.392), kind=kOutput, calls=%fused_computation.12 | convolution fusion | flops 504723456 | bytes 5119488 | tf_op jit(solution)/shard_map/dot_general | solution.py:87
  237.8 1.7 fusion.47
  239.5 2.0 reshape.394
  241.5 3.5 convert_reduce_fusion.6
  244.9 1.8 convert_element_type.310
  246.7 4.2 convert_reduce_fusion
  250.9 1.6 fusion.109
  252.6 1.7 convert_element_type.294
  254.3 4.3 convert_reduce_fusion.1
  258.7 1.6 multiply_reduce_fusion.6
  260.3 2.7 convert_reduce_fusion.7
  266.9 2.6 multiply_reduce_fusion.1
  270.6 1.7 convert_reduce_fusion.5
  273.6 1.9 convert_reduce_fusion.4
  285.1 2.8 fusion.30
  292.3 3.0 fusion.108
  303.5 3.2 multiply_reduce_fusion.5
  306.7 2.8 fusion.40
  309.5 2.6 reshape.407
  313.0 3.2 reshape.409
  316.2 4.9 fusion.34
  321.1 3.2 reshape.410
  325.6 1.6 copy.207
  328.2 1.6 copy.208
  330.5 38.7 %all-reduce.8 = (f32[768]{0:T(1024)S(1)}, f32[3840]{0:T(1024)S(1)}) all-reduce(f32[768]{0:T(1024)S(1)} %maximum_add_fusion, f32[3840]{0:T(1024)S(1)} %add.255), channel_id=6, replica_groups=mesh['fsdp'=32] {'fsdp'}, use_global_device_ids=true, to_apply=%region_30.0.clone | all-reduce | flops 4608 | bytes 36864
  370.4 117.4 %all-reduce.13.cloned.1.call-done = (f32[442368]{0:T(1024)}, f32[147456]{0:T(1024)}, f32[589824]{0:T(1024)}, f32[589824]{0:T(1024)}) async-done(((f32[442368]{0:T(1024)}, f32[147456]{0:T(1024)}, f32[589824]{0:T(1024)}, f32[589824]{0:T(1024)}), (f32[442368]{0:T(1024)}, f32[147456]{0:T(1024)}, f32[589824]{0:T(1024)}, f32[589824]{0:T(1024)})) %all-reduce.13.cloned.1.call-update) | async-done | bytes 7077904
  487.7 1.5 dynamic-slice.2
  490.8 1.5 dynamic-slice
  (352 shorter events, 79.1 us)
Async XLA Ops:
  7.2 50.1 %copy-start.3 = (bf16[2,2,197,384]{3,1,2,0:T(2,128)(2,1)S(1)}, bf16[2,2,197,384]{3,1,2,0:T(2,128)(2,1)}, u32[]{:S(2)}) copy-start(bf16[2,2,197,384]{3,1,2,0:T(2,128)(2,1)} %param.9) | copy-start | bytes 1815556
  7.2 5.5 %copy-start.92 = (bf16[24]{0:T(256)(128)(2,1)S(1)}, bf16[24]{0:T(256)(128)(2,1)}, u32[]{:S(2)}) copy-start(bf16[24]{0:T(256)(128)(2,1)} %param.16) | copy-start | bytes 148
  7.2 5.7 %copy-start.93 = (bf16[120]{0:T(256)(128)(2,1)S(1)}, bf16[120]{0:T(256)(128)(2,1)}, u32[]{:S(2)}) copy-start(bf16[120]{0:T(256)(128)(2,1)} %param.17) | copy-start | bytes 724
  7.2 56.1 %copy-start.89 = (s32[2,1]{0,1:T(1,128)S(1)}, s32[2,1]{0,1:T(1,128)}, u32[]{:S(2)}) copy-start(s32[2,1]{0,1:T(1,128)} %param.10) | copy-start | bytes 28
  7.2 57.8 %copy-start.46 = (bf16[2,2,197,384]{3,1,2,0:T(2,128)(2,1)S(1)}, bf16[2,2,197,384]{3,1,2,0:T(2,128)(2,1)}, u32[]{:S(2)}) copy-start(bf16[2,2,197,384]{3,1,2,0:T(2,128)(2,1)} %param.11) | copy-start | bytes 1815556
  7.2 201.3 %all-gather.5.cloned.1.call-start = ((), (), s32[]{:S(2)}) async-start(), calls=%async_computation | async-start | bytes 1216512 | tf_op jit(solution)/shard_map/all_gather | solution.py:212
  8.0 212.2 %all-gather.7.cloned.1.call-start = ((), (), s32[]{:S(2)}) async-start(), calls=%async_computation.1 | async-start | bytes 1216512 | tf_op jit(solution)/shard_map/all_gather | solution.py:213
  8.7 479.0 %all-reduce.13.cloned.1.call-start = ((), (), s32[]{:S(2)}) async-start(), calls=%async_computation.2 | async-start | bytes 14155776
  55.9 13.3 %copy-start.67 = (f32[384]{0:T(512)}, f32[384]{0:T(512)S(1)}, u32[]{:S(2)}) copy-start(f32[384]{0:T(512)S(1)} %get-tuple-element.89) | copy-start | bytes 4612
  66.4 4.2 copy-start.59
  177.4 4.6 copy-start.40
  177.4 7.4 %copy-start.35 = (bf16[394,384]{1,0:T(8,128)(2,1)S(1)}, bf16[394,384]{1,0:T(8,128)(2,1)}, u32[]{:S(2)}) copy-start(bf16[394,384]{1,0:T(8,128)(2,1)} %slice.135) | copy-start | bytes 907780
  184.9 3.4 copy-start.12
  191.2 5.2 %copy-start.16 = (bf16[1,2,197,384]{3,1,2,0:T(2,128)(2,1)S(1)}, bf16[1,2,197,384]{3,1,2,0:T(2,128)(2,1)}, u32[]{:S(2)}) copy-start(bf16[1,2,197,384]{3,1,2,0:T(2,128)(2,1)} %get-tuple-element.80) | copy-start | bytes 907780
  191.2 5.2 %copy-start.17 = (bf16[1,2,197,384]{3,1,2,0:T(2,128)(2,1)S(1)}, bf16[1,2,197,384]{3,1,2,0:T(2,128)(2,1)}, u32[]{:S(2)}) copy-start(bf16[1,2,197,384]{3,1,2,0:T(2,128)(2,1)} %get-tuple-element.81) | copy-start | bytes 907780
  193.2 6.3 %copy-start.85 = (f32[2]{0:T(128)S(1)}, f32[2]{0:T(128)}, u32[]{:S(2)}) copy-start(f32[2]{0:T(128)} %compare_convert_fusion) | copy-start | bytes 28
  195.6 6.1 %copy-start.79 = (f32[2,197]{1,0:T(2,128)S(1)}, f32[2,197]{1,0:T(2,128)}, u32[]{:S(2)}) copy-start(f32[2,197]{1,0:T(2,128)} %copy.237) | copy-start | bytes 4732
  195.6 6.8 %copy-start.81 = (f32[2,197]{1,0:T(2,128)S(1)}, f32[2,197]{1,0:T(2,128)}, u32[]{:S(2)}) copy-start(f32[2,197]{1,0:T(2,128)} %copy.238) | copy-start | bytes 4732
  195.6 7.5 %copy-start.80 = (f32[2,197]{1,0:T(2,128)S(1)}, f32[2,197]{1,0:T(2,128)}, u32[]{:S(2)}) copy-start(f32[2,197]{1,0:T(2,128)} %copy.236) | copy-start | bytes 4732
  195.6 8.1 %copy-start.78 = (f32[2,197]{1,0:T(2,128)S(1)}, f32[2,197]{1,0:T(2,128)}, u32[]{:S(2)}) copy-start(f32[2,197]{1,0:T(2,128)} %copy.235) | copy-start | bytes 4732
  196.3 9.3 %copy-start.54 = (f32[2,6,197]{2,1,0:T(8,128)S(1)}, f32[2,6,197]{2,1,0:T(8,128)}, u32[]{:S(2)}) copy-start(f32[2,6,197]{2,1,0:T(8,128)} %copy-done.53) | copy-start | bytes 28372
  196.3 9.3 %copy-start.58 = (f32[2,6,197]{2,1,0:T(8,128)S(1)}, f32[2,6,197]{2,1,0:T(8,128)}, u32[]{:S(2)}) copy-start(f32[2,6,197]{2,1,0:T(8,128)} %copy-done.57) | copy-start | bytes 28372
  196.4 9.9 %copy-start.62 = (f32[384]{0:T(512)S(1)}, f32[384]{0:T(512)}, u32[]{:S(2)}) copy-start(f32[384]{0:T(512)} %get-tuple-element.109) | copy-start | bytes 4612
  196.4 9.9 %copy-start.69 = (f32[384]{0:T(512)S(1)}, f32[384]{0:T(512)}, u32[]{:S(2)}) copy-start(f32[384]{0:T(512)} %get-tuple-element.85) | copy-start | bytes 4612
  201.6 10.4 %copy-start.84 = (f32[1536]{0:T(1024)S(1)}, f32[1536]{0:T(1024)}, u32[]{:S(2)}) copy-start(f32[1536]{0:T(1024)} %slice.107) | copy-start | bytes 18436
  212.0 11.2 %copy-start.86 = (f32[384]{0:T(512)S(1)}, f32[384]{0:T(512)}, u32[]{:S(2)}) copy-start(f32[384]{0:T(512)} %get-tuple-element.84) | copy-start | bytes 4612
  228.6 9.2 %copy-start.43 = (bf16[1536,384]{1,0:T(8,128)(2,1)S(1)}, bf16[1536,384]{1,0:T(8,128)(2,1)}, u32[]{:S(2)}) copy-start(bf16[1536,384]{1,0:T(8,128)(2,1)} %reshape.393) | copy-start | bytes 3538948
  246.7 4.2 copy-start.41
  254.3 4.3 copy-start.2
  254.3 4.3 copy-start.42
  254.3 4.3 copy-start.45
  263.0 3.9 copy-start.27
  272.3 3.2 copy-start.36
  273.6 5.2 %copy-start.25 = (bf16[2,197,6,64]{1,3,2,0:T(8,128)(2,1)S(1)}, bf16[2,197,6,64]{1,3,2,0:T(8,128)(2,1)}, u32[]{:S(2)}) copy-start(bf16[2,197,6,64]{1,3,2,0:T(8,128)(2,1)} %copy.178) | copy-start | bytes 907780
  275.5 3.3 copy-start.52
  291.5 3.8 copy-start.34
  292.3 4.7 copy-start.33
  297.0 6.4 %copy-start.6 = (f32[394,384]{1,0:T(8,128)S(1)}, f32[394,384]{1,0:T(8,128)}, u32[]{:S(2)}) copy-start(f32[394,384]{1,0:T(8,128)} %reshape.412) | copy-start | bytes 1815556
  297.0 6.4 %copy-start.7 = (f32[394,384]{1,0:T(8,128)S(1)}, f32[394,384]{1,0:T(8,128)}, u32[]{:S(2)}) copy-start(f32[394,384]{1,0:T(8,128)} %reshape.411) | copy-start | bytes 1815556
  297.0 6.4 %copy-start.61 = (f32[384]{0:T(512)S(1)}, f32[384]{0:T(512)}, u32[]{:S(2)}) copy-start(f32[384]{0:T(512)} %copy-done.60) | copy-start | bytes 4612
  297.0 6.4 %copy-start.68 = (f32[384]{0:T(512)S(1)}, f32[384]{0:T(512)}, u32[]{:S(2)}) copy-start(f32[384]{0:T(512)} %copy-done.67) | copy-start | bytes 4612
  297.0 6.4 %copy-start.71 = (f32[394]{0:T(512)S(1)}, f32[394]{0:T(512)}, u32[]{:S(2)}) copy-start(f32[394]{0:T(512)} %div.88) | copy-start | bytes 4732
  297.0 6.4 %copy-start.72 = (f32[394]{0:T(512)S(1)}, f32[394]{0:T(512)}, u32[]{:S(2)}) copy-start(f32[394]{0:T(512)} %rsqrt.45) | copy-start | bytes 4732
  297.0 6.4 %copy-start.73 = (f32[394]{0:T(512)S(1)}, f32[394]{0:T(512)}, u32[]{:S(2)}) copy-start(f32[394]{0:T(512)} %rsqrt.44) | copy-start | bytes 4732
  297.1 6.4 %copy-start.74 = (f32[394]{0:T(512)S(1)}, f32[394]{0:T(512)}, u32[]{:S(2)}) copy-start(f32[394]{0:T(512)} %div.83) | copy-start | bytes 4732
  303.4 3.2 copy-start.55
  313.0 3.2 copy-start.50
  313.0 3.2 copy-start.51
  (54 other events, 103.5 us)
Sparse Core Ops, SparseCore 0:
  10.9 56.7 all-gather.4
  70.6 53.6 all-gather.6
  324.4 163.2 all-reduce.12
where the time goes:
time: 507 us; the launch traced here: 501 us
  blocking collectives  166 us (33%)
  waiting for transfers between devices  119 us (23%)
  local copies, waits for them, and re-layouts  93.5 us (18%)
  matrix products  71.6 us (14%)
  other arithmetic  35.4 us (7%)
  between operations  15.6 us (3%)
    unnamed x4, waiting for transfers between devices  119 us
    unnamed x2, blocking collectives  80.9 us
    all_gather x1, blocking collectives, local(): lax.all_gather(qkv_weight, 'fsdp', axis=0, tiled=True)  46.5 us
    all_gather x1, blocking collectives, local(): lax.all_gather(out_weight, 'fsdp', axis=0, tiled=True)  38.3 us
    unnamed x232, local copies, waits for them, and re-layouts  22 us
    dot_general x2, matrix products, forward(): jnp.dot(normed_two_low, w_fc1, preferred_element_type=jnp.float32)  16.2 us
  transfers between devices with their start and end apart: 3, of which 1 were waited for; matrix products, arithmetic and copies ran while one was open for 18% of the time, Pallas kernels for 0%

commit v1 on v0

v1 whole, which is shorter than its diff:
```python
import functools
import math

import jax
import jax.numpy as jnp
from jax import lax
from jax.experimental import pallas as pl
from jax.experimental.pallas import tpu as pltpu
from jax.sharding import PartitionSpec as P

D = 384
H = 6
FF = 1536
HD = 64
S = 197
SP = 208
SQ = 256
EPS = 1e-06
f32 = jnp.float32
bf16 = jnp.bfloat16
G1, G2, B1, B2, BO, BF2, BQ, BV, BF1 = 0, 384, 768, 1152, 1536, 1920, 2304, 2688, 3072
NV = 4608
VMEM_LIMIT = 60 * 1024 * 1024


def params(**kw):
    return pltpu.CompilerParams(vmem_limit_bytes=VMEM_LIMIT, **kw)


def full(shape):
    return pl.BlockSpec(shape, lambda *_: (0,) * len(shape))


def any_spec():
    return pl.BlockSpec(memory_space=pl.ANY)


def nn(a, b):
    return jnp.dot(a, b, preferred_element_type=f32)


def nt(a, b):
    return lax.dot_general(a, b, (((1,), (1,)), ((), ())), preferred_element_type=f32)


def tr(a):
    return a.astype(f32).T.astype(a.dtype)


def norm_stats(rows):
    mean = jnp.mean(rows, axis=-1, keepdims=True)
    cen = rows - mean
    var = jnp.mean(cen * cen, axis=-1, keepdims=True)
    inv = lax.rsqrt(var + EPS)
    return cen * inv, inv


def pad_rows(ref_val):
    return jnp.concatenate([ref_val, jnp.zeros((SP - S, ref_val.shape[1]), ref_val.dtype)], axis=0)


def head_masks():
    lane = lax.broadcasted_iota(jnp.int32, (SP, 128), 1)
    return lane < HD


def pick(block, first, head):
    zero = jnp.zeros_like(block)
    return jnp.where(first, block, zero) if head == 0 else jnp.where(first, zero, block)


def attn_fwd_body(x_ref, w, vec, a1_ref, qkv_ref, o_ref, lse_ref):
    rows = pad_rows(x_ref[0].astype(f32))
    n1, _ = norm_stats(rows)
    a1 = (n1 * vec[:, G1 : G1 + D] + vec[:, B1 : B1 + D]).astype(bf16)
    a1_ref[0] = a1
    mixed = nn(a1, w)
    q = (mixed[:, :D] + vec[:, BQ : BQ + D]).astype(bf16)
    k = mixed[:, D : 2 * D].astype(bf16)
    v = (mixed[:, 2 * D :] + vec[:, BV : BV + D]).astype(bf16)
    qkv_ref[0, :, :D] = q
    qkv_ref[0, :, D : 2 * D] = k
    qkv_ref[0, :, 2 * D :] = v
    first = head_masks()
    key_ok = lax.broadcasted_iota(jnp.int32, (SP, SQ), 0) < S
    for j in range(H // 2):
        cols = slice(128 * j, 128 * j + 128)
        q2t = jnp.concatenate([tr(q[:, cols]), jnp.zeros((128, SQ - SP), bf16)], axis=1)
        v2t = tr(v[:, cols])
        outs = []
        for h in range(2):
            z = nn(pick(k[:, cols], first, h), q2t) * 0.125
            z = jnp.where(key_ok, z, -1e30)
            peak = jnp.max(z, axis=0, keepdims=True)
            e = jnp.exp(z - peak)
            total = jnp.sum(e, axis=0, keepdims=True)
            pb = (e * (1.0 / total)).astype(bf16)
            lse_ref[0, pl.ds(2 * j + h, 1), :] = peak + jnp.log(total)
            outs.append(nn(v2t[HD * h : HD * h + HD, :], pb))
        o_ref[0, :, cols] = jnp.concatenate(outs, axis=0).T[:SP].astype(bf16)


def k1_kernel(x_ref, w_ref, vec_ref, a1_ref, qkv_ref, o_ref, lse_ref):
    attn_fwd_body(x_ref, w_ref[...], vec_ref[...], a1_ref, qkv_ref, o_ref, lse_ref)


def k1(x, w, vec):
    n = x.shape[0]
    blk = lambda r, c: pl.BlockSpec((1, r, c), lambda i: (i, 0, 0))
    return pl.pallas_call(
        k1_kernel,
        name="k1",
        grid=(n,),
        in_specs=[blk(S, D), full((D, 3 * D)), full((1, NV))],
        out_specs=[blk(SP, D), blk(SP, 3 * D), blk(SP, D), blk(8, SQ)],
        out_shape=[
            jax.ShapeDtypeStruct((n, SP, D), bf16),
            jax.ShapeDtypeStruct((n, SP, 3 * D), bf16),
            jax.ShapeDtypeStruct((n, SP, D), bf16),
            jax.ShapeDtypeStruct((n, 8, SQ), f32),
        ],
        compiler_params=params(),
    )(x, w, vec)


CH = 768


def gelu_parts(u):
    cum = 0.5 * (1.0 + lax.erf(u * (1.0 / math.sqrt(2.0))))
    den = jnp.exp(-0.5 * u * u) * (1.0 / math.sqrt(2.0 * math.pi))
    return u * cum, cum + u * den


def k2_kernel(live_ref, x_ref, g_ref, o_ref, oall_ref, wo_ref, w1_ref, w2_ref, vec_ref,
              out_ref, dr_ref, go_ref, g1_ref, g2_ref, sums_ref, a2_s, du_s, gl_s, eb_s, drb_s):
    i = pl.program_id(0)
    n = pl.num_programs(0)
    vec = vec_ref[...]
    live = live_ref[i]
    rows = pl.ds(i * SP, SP)

    @pl.when(i == 0)
    def _():
        sums_ref[...] = jnp.zeros_like(sums_ref)

    res = pad_rows(x_ref[0].astype(f32)) + nn(o_ref[0], wo_ref[...]) + vec[:, BO : BO + D]
    n2, r2 = norm_stats(res)
    a2 = (n2 * vec[:, G2 : G2 + D] + vec[:, B2 : B2 + D]).astype(bf16)
    a2_s[rows, :] = a2
    e = pad_rows(g_ref[0].astype(f32)) * live
    eb = e.astype(bf16)
    eb_s[rows, :] = eb
    acc = res + vec[:, BF2 : BF2 + D]
    dn = jnp.zeros((SP, D), f32)
    for c in range(FF // CH):
        cs = slice(CH * c, CH * c + CH)
        u = nn(a2, w1_ref[:, cs]) + vec[:, BF1 + CH * c : BF1 + CH * c + CH]
        dg = nt(eb, w2_ref[cs, :])
        gel, slope = gelu_parts(u)
        gb = gel.astype(bf16)
        du = (dg * slope).astype(bf16)
        gl_s[rows, cs] = gb
        du_s[rows, cs] = du
        acc = acc + nn(gb, w2_ref[cs, :])
        dn = dn + nt(du, w1_ref[:, cs])
    out_ref[0] = (acc * live)[:S]
    t = dn * vec[:, G2 : G2 + D]
    dr = e + r2 * (
        t - jnp.mean(t, axis=-1, keepdims=True) - n2 * jnp.mean(t * n2, axis=-1, keepdims=True)
    )
    dr_ref[0] = dr
    drb_s[rows, :] = dr.astype(bf16)
    sums_ref[0:1, G2 : G2 + D] += jnp.sum(dn * n2, axis=0, keepdims=True)
    sums_ref[0:1, B2 : B2 + D] += jnp.sum(dn, axis=0, keepdims=True)

    @pl.when(i == n - 1)
    def _():
        ones = jnp.ones((8, a2_s.shape[0]), bf16)
        eball = eb_s[...]
        drball = drb_s[...]
        g1_ref[...] = nn(tr(a2_s[...]), du_s[...])
        g2_ref[...] = nn(tr(eball), gl_s[...]).T
        go_ref[...] = nn(tr(oall_ref[...].reshape(-1, D)), drball)
        sums_ref[:, BF1 : BF1 + FF] = nn(ones, du_s[...])
        sums_ref[:, BF2 : BF2 + D] = nn(ones, eball)
        sums_ref[:, BO : BO + D] = nn(ones, drball)


def k2(live, x, g, o, wo, w1, w2, vec):
    n = x.shape[0]
    blk = lambda r, c: pl.BlockSpec((1, r, c), lambda i: (i, 0, 0))
    return pl.pallas_call(
        k2_kernel,
        name="k2",
        grid=(n,),
        in_specs=[pl.BlockSpec(memory_space=pltpu.SMEM), blk(S, D), blk(S, D), blk(SP, D), full((n, SP, D)),
                  full((D, D)), full((D, FF)), full((FF, D)), full((1, NV))],
        out_specs=[blk(S, D), blk(SP, D), full((D, D)), full((D, FF)), full((FF, D)), full((8, NV))],
        out_shape=[
            jax.ShapeDtypeStruct((n, S, D), f32),
            jax.ShapeDtypeStruct((n, SP, D), f32),
            jax.ShapeDtypeStruct((D, D), f32),
            jax.ShapeDtypeStruct((D, FF), f32),
            jax.ShapeDtypeStruct((FF, D), f32),
            jax.ShapeDtypeStruct((8, NV), f32),
        ],
        scratch_shapes=[
            pltpu.VMEM((n * SP, D), bf16),
            pltpu.VMEM((n * SP, FF), bf16),
            pltpu.VMEM((n * SP, FF), bf16),
            pltpu.VMEM((n * SP, D), bf16),
            pltpu.VMEM((n * SP, D), bf16),
        ],
        compiler_params=params(),
    )(live, x, g, o, o, wo, w1, w2, vec)


def k3_kernel(x_ref, qkv_ref, lse_ref, dr_ref, a1_ref, w_ref, wo_ref, vec_ref,
              dx_ref, gq_ref, sums_ref, dp_s):
    i = pl.program_id(0)
    n = pl.num_programs(0)
    vec = vec_ref[...]
    rows = pl.ds(i * SP, SP)

    @pl.when(i == 0)
    def _():
        sums_ref[...] = jnp.zeros_like(sums_ref)

    dr = dr_ref[0]
    do = nt(dr.astype(bf16), wo_ref[...]).astype(bf16)
    first = head_masks()
    key_ok = lax.broadcasted_iota(jnp.int32, (SP, SQ), 0) < S
    lanes0 = jnp.zeros((128, SQ - SP), bf16)
    rows0 = jnp.zeros((SQ - SP, 128), bf16)
    for j in range(H // 2):
        q2 = qkv_ref[0, :, 128 * j : 128 * j + 128]
        k2_ = qkv_ref[0, :, D + 128 * j : D + 128 * j + 128]
        v2 = qkv_ref[0, :, 2 * D + 128 * j : 2 * D + 128 * j + 128]
        do2 = do[:, 128 * j : 128 * j + 128]
        q2t = jnp.concatenate([tr(q2), lanes0], axis=1)
        do2t = jnp.concatenate([tr(do2), lanes0], axis=1)
        k2t = tr(k2_)
        dqs = []
        dk = jnp.zeros((SP, 128), f32)
        dv = jnp.zeros((SP, 128), f32)
        for h in range(2):
            z = nn(pick(k2_, first, h), q2t) * 0.125
            z = jnp.where(key_ok, z, -1e30)
            p = jnp.exp(z - lse_ref[0, pl.ds(2 * j + h, 1), :])
            dpr = nn(pick(v2, first, h), do2t)
            dot_row = jnp.sum(p * dpr, axis=0, keepdims=True)
            dz = (p * (dpr - dot_row)).astype(bf16)
            pb = p.astype(bf16)
            dv = dv + nn(pb, jnp.concatenate([pick(do2, first, h), rows0], axis=0))
            dk = dk + nn(dz, jnp.concatenate([pick(q2, first, h), rows0], axis=0))
            dqs.append(nn(k2t[HD * h : HD * h + HD, :], dz))
        dp_s[rows, 128 * j : 128 * j + 128] = (jnp.concatenate(dqs, axis=0).T[:SP] * 0.125).astype(bf16)
        dp_s[rows, D + 128 * j : D + 128 * j + 128] = (dk * 0.125).astype(bf16)
        dp_s[rows, 2 * D + 128 * j : 2 * D + 128 * j + 128] = dv.astype(bf16)
    dn = nt(dp_s[rows, :], w_ref[...])
    n1, r1 = norm_stats(pad_rows(x_ref[0].astype(f32)))
    t = dn * vec[:, G1 : G1 + D]
    dx = dr + r1 * (
        t - jnp.mean(t, axis=-1, keepdims=True) - n1 * jnp.mean(t * n1, axis=-1, keepdims=True)
    )
    dx_ref[0] = dx[:S]
    sums_ref[0:1, G1 : G1 + D] += jnp.sum(dn * n1, axis=0, keepdims=True)
    sums_ref[0:1, B1 : B1 + D] += jnp.sum(dn, axis=0, keepdims=True)

    @pl.when(i == n - 1)
    def _():
        dpall = dp_s[...]
        gq_ref[...] = nn(tr(a1_ref[...].reshape(-1, D)), dpall)
        bsum = nn(jnp.ones((8, dpall.shape[0]), bf16), dpall)
        sums_ref[:, BQ : BQ + D] = bsum[:, :D]
        sums_ref[:, BV : BV + D] = bsum[:, 2 * D :]


def k3(x, qkv, lse, dr, a1, w, wo, vec):
    n = x.shape[0]
    blk = lambda r, c: pl.BlockSpec((1, r, c), lambda i: (i, 0, 0))
    return pl.pallas_call(
        k3_kernel,
        name="k3",
        grid=(n,),
        in_specs=[blk(S, D), blk(SP, 3 * D), blk(8, SQ), blk(SP, D), full((n, SP, D)),
                  full((D, 3 * D)), full((D, D)), full((1, NV))],
        out_specs=[blk(S, D), full((D, 3 * D)), full((8, NV))],
        out_shape=[
            jax.ShapeDtypeStruct((n, S, D), f32),
            jax.ShapeDtypeStruct((D, 3 * D), f32),
            jax.ShapeDtypeStruct((8, NV), f32),
        ],
        scratch_shapes=[pltpu.VMEM((n * SP, 3 * D), bf16)],
        compiler_params=params(),
    )(x, qkv, lse, dr, a1, w, wo, vec)


def local(images, counts, out_grad, qkv_weight, out_weight, fc1_weight, fc2_weight, norm_gains, biases):
    ag = lambda v: lax.all_gather(v, "fsdp", axis=0, tiled=True)
    w = ag(qkv_weight).reshape(D, 3 * D)
    wo = ag(out_weight).reshape(D, D)
    w1 = ag(fc1_weight).reshape(D, FF)
    w2 = ag(fc2_weight).reshape(FF, D)
    vec = jnp.concatenate([ag(norm_gains), ag(biases)]).astype(f32)[None, :]
    mb, cap = images.shape[:2]
    x = images.reshape(mb * cap, S, D)
    g = out_grad.reshape(mb * cap, S, D)
    live = (jnp.arange(cap, dtype=jnp.int32)[None, :] < counts[:, :1]).astype(f32).reshape(-1)
    a1, qkv, o, lse = k1(x, w, vec)
    out, dr, go, g1, g2, sums2 = k2(live, x, g, o, wo, w1, w2, vec)
    dx, gq, sums3 = k3(x, qkv, lse, dr, a1, w, wo, vec)
    sums = jnp.where((jnp.arange(NV) < G2) | ((jnp.arange(NV) >= B1) & (jnp.arange(NV) < B2)) | ((jnp.arange(NV) >= BQ) & (jnp.arange(NV) < BF1)), sums3[0], sums2[0])
    rs = lambda v: lax.psum_scatter(v.reshape(-1), "fsdp", scatter_dimension=0, tiled=True)
    return (out.reshape(images.shape), dx.reshape(images.shape), rs(gq), rs(go), rs(g1), rs(g2), rs(sums[: 2 * D]), rs(sums[2 * D :]))


def solution(mesh):
    placed = (
        P(None, "fsdp", None, None),
        P(None, "fsdp"),
        P(None, "fsdp", None, None),
        P("fsdp"),
        P("fsdp"),
        P("fsdp"),
        P("fsdp"),
        P("fsdp"),
        P("fsdp"),
    )
    return jax.shard_map(
        local,
        mesh=mesh,
        in_specs=placed,
        out_specs=(placed[0], placed[2]) + (P("fsdp"),) * 6,
        check_vma=False,
    )
```

time: 507 us -> 389 us (0.77); the launches traced: 501 us -> 388 us
  matrix products: 71.6 us -> 0 us
  local copies, waits for them, and re-layouts: 93.5 us -> 36.7 us
  Pallas kernels: 0 us -> 44.2 us
  other arithmetic: 35.4 us -> 8.41 us
    dot_general x32 -> x0, matrix products: 71.6 us -> none  [the longest x2 16.2 us: forward(): jnp.dot(normed_two_low, w_fc1, preferred_element_type=jnp.float32)]
    pallas_call x0 -> x3, Pallas kernels: none -> 44.2 us  [the longest x1 17.2 us: k2(): pl.pallas_call(k2_kernel, name='k2', grid=(n,), in_specs=[pl.BlockSpec(me...]
    reshape x32 -> x8, local copies, waits for them, and re-layouts: 44.8 us -> 19.3 us  [the longest x4 9.4 us: local(): v.reshape(-1)]
    convert_element_type x22 -> x1, local copies, waits for them, and re-layouts: 17.4 us -> 0.59 us  [local(): (jnp.arange(cap, dtype=jnp.int32)[None, :] < counts[:, :1]).astype(f32)]
    reduce_sum x8 -> x0, other arithmetic: 16.1 us -> none  [the longest x3 6.96 us: norm_fwd(): variance = jnp.mean(centred * centred, axis=-1, keepdims=True)]
    convert_element_type x9 -> x2, other arithmetic: 10.8 us -> 1.35 us  [the longest x1 0.73 us: local(): (jnp.arange(cap, dtype=jnp.int32)[None, :] < counts[:, :1]).astype(f32)]
    unnamed x232 -> x26, local copies, waits for them, and re-layouts: 22 us -> 15.6 us
  transfers between devices with their start and end apart: 3 -> 3, of which waited for: 1 -> 1; matrix products, arithmetic and copies ran while one was open for 18% -> 7% of each run, Pallas kernels for 0% -> 3%
where the time goes in v1:
time: 389 us; the launch traced here: 388 us
  blocking collectives  165 us (42%)
  waiting for transfers between devices  120 us (31%)
  Pallas kernels  44.2 us (11%)
  local copies, waits for them, and re-layouts  36.7 us (9%)
  between operations  13.9 us (4%)
  other arithmetic  8.41 us (2%)
    unnamed x4, waiting for transfers between devices  120 us
    all_gather x2, blocking collectives, local(): ag = lambda v: lax.all_gather(v, 'fsdp', axis=0, tiled=True)  84 us
    unnamed x2, blocking collectives  80.9 us
    pallas_call x1, Pallas kernels, k2(): pl.pallas_call(k2_kernel, name='k2', grid=(n,), in_specs=[pl.BlockSpec(me...  17.2 us
    unnamed x26, local copies, waits for them, and re-layouts  15.6 us
    pallas_call x1, Pallas kernels, k3(): pl.pallas_call(k3_kernel, name='k3', grid=(n,), in_specs=[blk(S, D), blk(...  15.2 us
    pallas_call x1, Pallas kernels, k1(): pl.pallas_call(k1_kernel, name='k1', grid=(n,), in_specs=[blk(S, D), full...  11.7 us
    reshape x4, local copies, waits for them, and re-layouts, local(): v.reshape(-1)  9.4 us
  transfers between devices with their start and end apart: 3, of which 1 were waited for; matrix products, arithmetic and copies ran while one was open for 7% of the time, Pallas kernels for 3%

profile of v1, /device:TPU:0, one launch (start us, length us, event | category | flops | bytes accessed | tf_op | source)
XLA Modules:
  0.0 388.0 jit_solution(10195212259339000671)
XLA Ops:
  7.2 0.0 copy-start.3
  7.2 0.0 all-gather.5.cloned.1.call-start
  7.2 0.7 all-gather.5.cloned.1.call-update
  7.9 0.0 copy-start.4
  7.9 0.0 all-gather.7.cloned.1.call-start
  8.0 0.7 all-gather.7.cloned.1.call-update
  8.7 0.0 all-reduce.13.cloned.1.call-start
  8.7 0.7 compare_convert_fusion
  9.4 0.6 reshape.99.live_ref
  10.0 0.8 dynamic-update-slice
  10.9 0.8 dynamic-update-slice.1
  11.7 42.2 %all-reduce.10 = (bf16[3840]{0:T(1024)(128)(2,1)S(1)}, bf16[768]{0:T(1024)(128)(2,1)S(1)}) all-reduce(bf16[3840]{0:T(1024)(128)(2,1)S(1)} %dynamic-update-slice.1, bf16[768]{0:T(1024)(128)(2,1)S(1)} %dynamic-update-slice), channel_id=1, replica_groups=mesh['fsdp'=32] {'fsdp'}, use_global_device_ids=true, to_apply=%add.1 | all-reduce | flops 4608 | bytes 18432
  53.9 0.7 reshape.106
  54.6 0.8 reshape.104
  55.4 42.0 %all-gather.1 = bf16[32,1,4608]{2,1,0:T(2,128)(2,1)S(1)} all-gather(bf16[1,1,4608]{2,1,0:T(2,128)(2,1)S(1)} %reshape.106), channel_id=1, replica_groups=mesh['fsdp'=32] {'fsdp'}, dimensions={0}, use_global_device_ids=true | all-gather | bytes 304128 | tf_op jit(solution)/shard_map/all_gather | solution.py:301
  97.4 1.7 reduce.1
  99.2 1.1 reshape.90.wo_ref
  100.2 0.0 copy-done.3
  100.2 0.9 copy.25
  101.1 0.0 copy-done.4
  101.2 0.9 copy.26
  102.0 42.0 %all-gather = bf16[32,1,13824]{2,1,0:T(2,128)(2,1)S(1)} all-gather(bf16[1,1,13824]{2,1,0:T(2,128)(2,1)S(1)} %reshape.104), channel_id=1, replica_groups=mesh['fsdp'=32] {'fsdp'}, dimensions={0}, use_global_device_ids=true | all-gather | bytes 912384 | tf_op jit(solution)/shard_map/all_gather | solution.py:301
  144.0 5.3 %reduce = bf16[32,13824]{1,0:T(8,128)(2,1)S(1)} reduce(bf16[32,1,13824]{2,1,0:T(2,128)(2,1)S(1)} %all-gather, bf16[]{:T(256)} %constant.41), dimensions={1}, to_apply=%all-gather.reduce_sub_computation | reduce | bytes 1769474 | tf_op jit(solution)/shard_map/all_gather | solution.py:301
  149.4 2.3 reshape.89.w_ref
  151.6 0.6 maximum_convert_fusion.vec_ref
  152.3 11.7 %k1.1 = (bf16[4,208,384]{2,1,0:T(8,128)(2,1)}, bf16[4,208,1152]{2,1,0:T(8,128)(2,1)}, bf16[4,208,384]{2,1,0:T(8,128)(2,1)}, f32[4,8,256]{2,1,0:T(8,128)}) custom-call(bf16[4,197,384]{2,1,0:T(8,128)(2,1)} %bitcast.5, bf16[384,1152]{1,0:T(8,128)(2,1)} %reshape.89.w_ref, f32[1,4608]{1,0:T(1,128)} %maximum_convert_fusion.vec_ref), custom_call_target="tpu_custom_call" | custom-call | tf_op jit(solution)/shard_map/k1/pallas_call | solution.py:110
  164.0 3.5 reshape.91.w1_ref
  167.5 3.1 reshape.92.w2_ref
  170.5 17.2 %k2.1 = (f32[4,197,384]{2,1,0:T(8,128)}, f32[4,208,384]{2,1,0:T(8,128)}, f32[384,384]{1,0:T(8,128)}, f32[384,1536]{1,0:T(8,128)}, f32[1536,384]{1,0:T(8,128)}, /*index=5*/f32[8,4608]{1,0:T(8,128)}) custom-call(f32[4]{0:T(128)} %reshape.99.live_ref, bf16[4,197,384]{2,1,0:T(8,128)(2,1)} %bitcast.6, bf16[4,197,384]{2,1,0:T(8,128)(2,1)} %bitcast.8, ...), custom_call_target="tpu_custom_call" | custom-call | tf_op jit(solution)/shard_map/k2/pallas_call | solution.py:193
  187.8 1.9 reshape.96
  189.7 15.2 %k3.1 = (f32[4,197,384]{2,1,0:T(8,128)}, f32[384,1152]{1,0:T(8,128)}, f32[8,4608]{1,0:T(8,128)}) custom-call(bf16[4,197,384]{2,1,0:T(8,128)(2,1)} %bitcast.7, bf16[4,208,1152]{2,1,0:T(8,128)(2,1)} %get-tuple-element.23.qkv_ref, f32[4,8,256]{2,1,0:T(8,128)} %get-tuple-element.24.lse_ref, f32[4,208,384]{2,1,0:T(8,128)} %get-tuple-element.25.dr_ref, ...), custom_call_target="tpu_custom_call" | custom-call | tf_op jit(solution)/shard_map/k3/pallas_call | solution.py:283
  205.0 2.5 reshape.95
  207.5 3.3 reshape.97
  210.8 0.0 copy-done
  210.8 1.6 reshape.98
  212.4 0.0 all-reduce.13.cloned.1.call-update
  212.5 1.2 slice_reduce_fusion
  213.7 0.1 copy-done.1
  213.9 1.6 copy.27
  215.5 1.6 copy.28
  217.2 38.7 %all-reduce.8 = (f32[768]{0:T(1024)S(1)}, f32[3840]{0:T(1024)S(1)}) all-reduce(f32[768]{0:T(1024)S(1)} %slice.16, f32[3840]{0:T(1024)S(1)} %slice.17), channel_id=6, replica_groups=mesh['fsdp'=32] {'fsdp'}, use_global_device_ids=true, to_apply=%region_4.5.clone | all-reduce | flops 4608 | bytes 36864
  255.9 0.6 dynamic-slice.4
  256.5 0.6 dynamic-slice.5
  257.0 118.4 %all-reduce.13.cloned.1.call-done = (f32[442368]{0:T(1024)}, f32[147456]{0:T(1024)}, f32[589824]{0:T(1024)}, f32[589824]{0:T(1024)}) async-done(((f32[442368]{0:T(1024)}, f32[147456]{0:T(1024)}, f32[589824]{0:T(1024)}, f32[589824]{0:T(1024)}), (f32[442368]{0:T(1024)}, f32[147456]{0:T(1024)}, f32[589824]{0:T(1024)}, f32[589824]{0:T(1024)})) %all-reduce.13.cloned.1.call-update) | async-done | bytes 7077904
  375.4 1.5 dynamic-slice.2
  376.9 1.5 dynamic-slice.3
  378.5 1.5 dynamic-slice
  380.0 1.4 dynamic-slice.1
  (13 shorter events, 0.0 us)
Async XLA Ops:
  7.2 93.1 %copy-start.3 = (bf16[2,2,197,384]{3,1,2,0:T(2,128)(2,1)S(1)}, bf16[2,2,197,384]{3,1,2,0:T(2,128)(2,1)}, u32[]{:S(2)}) copy-start(bf16[2,2,197,384]{3,1,2,0:T(2,128)(2,1)} %param.9) | copy-start | bytes 1815556
  7.2 156.8 %all-gather.5.cloned.1.call-start = ((), (), s32[]{:S(2)}) async-start(), calls=%async_computation | async-start | bytes 1216512 | tf_op jit(solution)/shard_map/all_gather | solution.py:301
  7.9 93.2 %copy-start.4 = (bf16[2,2,197,384]{3,1,2,0:T(2,128)(2,1)S(1)}, bf16[2,2,197,384]{3,1,2,0:T(2,128)(2,1)}, u32[]{:S(2)}) copy-start(bf16[2,2,197,384]{3,1,2,0:T(2,128)(2,1)} %param.11) | copy-start | bytes 1815556
  7.9 159.5 %all-gather.7.cloned.1.call-start = ((), (), s32[]{:S(2)}) async-start(), calls=%async_computation.1 | async-start | bytes 1216512 | tf_op jit(solution)/shard_map/all_gather | solution.py:301
  8.7 366.8 %all-reduce.13.cloned.1.call-start = ((), (), s32[]{:S(2)}) async-start(), calls=%async_computation.2 | async-start | bytes 14155776
  207.5 3.3 copy-start
  212.4 1.4 copy-start.1
  212.5 3.1 copy-start.2
Sparse Core Ops, SparseCore 0:
  10.9 56.8 all-gather.4
  70.6 54.0 all-gather.6
  212.6 162.7 all-reduce.12

commit v2 on v1

v2 whole, which is shorter than its diff:
```python
import functools
import math

import jax
import jax.numpy as jnp
from jax import lax
from jax.experimental import pallas as pl
from jax.experimental.pallas import tpu as pltpu
from jax.sharding import PartitionSpec as P


D = 384
H = 6
FF = 1536
HD = 64
S = 197
SP = 208
SQ = 256
EPS = 1e-06
f32 = jnp.float32
bf16 = jnp.bfloat16
G1, G2, B1, B2, BO, BF2, BQ, BV, BF1 = 0, 384, 768, 1152, 1536, 1920, 2304, 2688, 3072
NV = 4608
VMEM_LIMIT = 60 * 1024 * 1024


def params(**kw):
    return pltpu.CompilerParams(vmem_limit_bytes=VMEM_LIMIT, **kw)


def full(shape):
    return pl.BlockSpec(shape, lambda *_: (0,) * len(shape))


def any_spec():
    return pl.BlockSpec(memory_space=pl.ANY)


def nn(a, b):
    return jnp.dot(a, b, preferred_element_type=f32)


def nt(a, b):
    return lax.dot_general(a, b, (((1,), (1,)), ((), ())), preferred_element_type=f32)


def tr(a):
    return a.astype(f32).T.astype(a.dtype)


def norm_stats(rows):
    mean = jnp.mean(rows, axis=-1, keepdims=True)
    cen = rows - mean
    var = jnp.mean(cen * cen, axis=-1, keepdims=True)
    inv = lax.rsqrt(var + EPS)
    return cen * inv, inv


def pad_rows(ref_val):
    return jnp.concatenate([ref_val, jnp.zeros((SP - S, ref_val.shape[1]), ref_val.dtype)], axis=0)


def head_masks():
    lane = lax.broadcasted_iota(jnp.int32, (SP, 128), 1)
    return lane < HD


def pick(block, first, head):
    zero = jnp.zeros_like(block)
    return jnp.where(first, block, zero) if head == 0 else jnp.where(first, zero, block)


TAIL = S // 8 * 8


def mask_tail(z):
    ok = lax.broadcasted_iota(jnp.int32, (SP - TAIL, z.shape[1]), 0) < S - TAIL
    return jnp.concatenate([z[:TAIL], jnp.where(ok, z[TAIL:], -1e30)], axis=0)


def attn_fwd_body(x_ref, w, vec, a1_ref, qkv_ref, o_ref, lse_ref, n1_ref):
    rows = pad_rows(x_ref[0].astype(f32))
    n1, _ = norm_stats(rows)
    a1 = (n1 * vec[:, G1 : G1 + D] + vec[:, B1 : B1 + D]).astype(bf16)
    a1_ref[0] = a1
    n1_ref[0] = n1.astype(bf16)
    mixed = nn(a1, w)
    q = (mixed[:, :D] + vec[:, BQ : BQ + D]).astype(bf16)
    k = mixed[:, D : 2 * D].astype(bf16)
    v = (mixed[:, 2 * D :] + vec[:, BV : BV + D]).astype(bf16)
    qkv_ref[0, :, :D] = q
    qkv_ref[0, :, D : 2 * D] = k
    qkv_ref[0, :, 2 * D :] = v
    first = head_masks()
    for j in range(H // 2):
        cols = slice(128 * j, 128 * j + 128)
        q2t = jnp.concatenate([tr(q[:, cols] * 0.125), jnp.zeros((128, SQ - SP), bf16)], axis=1)
        v2t = tr(v[:, cols])
        outs = []
        for h in range(2):
            z = mask_tail(nn(pick(k[:, cols], first, h), q2t))
            peak = jnp.max(z, axis=0, keepdims=True)
            e = jnp.exp(z - peak)
            total = jnp.sum(e, axis=0, keepdims=True)
            pb = (e * (1.0 / total)).astype(bf16)
            lse_ref[0, pl.ds(2 * j + h, 1), :] = peak + jnp.log(total)
            outs.append(nn(v2t[HD * h : HD * h + HD, :], pb))
        o_ref[0, :, cols] = jnp.concatenate(outs, axis=0).T[:SP].astype(bf16)


def cost(flops, nbytes, trans=0):
    return pl.CostEstimate(flops=int(flops), bytes_accessed=int(nbytes), transcendentals=int(trans))


def smem():
    return pl.BlockSpec(memory_space=pltpu.SMEM)


C1, C2 = 640, 1792
CF, CO = 768, 1024


def prep_kernel(core_ref, q_ref, o_ref, f1_ref, f2_ref, g_ref, b_ref, own_ref, send_ref, qs, os_, f1s, f2s):
    rows = own_ref.shape[0]
    core = core_ref[0]
    qs[...] = q_ref[...].astype(f32)
    os_[...] = o_ref[...].astype(f32)
    f1s[...] = f1_ref[...].astype(f32)
    f2s[...] = f2_ref[...].astype(f32)
    sets = []
    for s in range(2):
        parts = []
        for b in range(5):
            col = 5 * s + b
            if col < 9:
                parts.append(qs[pl.ds(col, rows, stride=9), :])
            else:
                small = jnp.zeros((rows, 128), f32)
                row = lax.broadcasted_iota(jnp.int32, (rows, 128), 0)
                gains = jnp.concatenate([g_ref[...].astype(f32), jnp.zeros((1, 128 - g_ref.shape[1]), f32)], axis=1)
                shifts = jnp.concatenate([b_ref[...].astype(f32), jnp.zeros((1, 128 - b_ref.shape[1]), f32)], axis=1)
                small = jnp.where(row == 0, gains, jnp.where(row == 1, shifts, small))
                parts.append(small)
        for b in range(6):
            parts.append(f1s[pl.ds(6 * s + b, rows, stride=12), :])
        for b in range(2):
            parts.append(os_[pl.ds(s + b, rows, stride=3), :])
        for half in range(2):
            for b in range(3):
                parts.append(f2s[pl.ds(3 * (2 * rows * s + rows * half) + b, rows, stride=3), :])
        sets.append(jnp.concatenate(parts, axis=1))
    own_ref[...] = jnp.where(core == 0, sets[0], sets[1]).astype(bf16)
    send_ref[...] = jnp.where(core == 0, sets[1], sets[0]).astype(bf16)


def prep(core, q, o, f1, f2, g, b):
    rows = q.shape[0] // 9
    shape = jax.ShapeDtypeStruct((rows, C1 + C2), bf16)
    vm = pl.BlockSpec(memory_space=pltpu.VMEM)
    return pl.pallas_call(
        prep_kernel, name="prep", in_specs=[smem()] + [vm] * 6, out_specs=[vm] * 2, out_shape=[shape] * 2,
        scratch_shapes=[pltpu.VMEM(v.shape, f32) for v in (q, o, f1, f2)],
        compiler_params=params(),
    )(core, q, o, f1, f2, g, b)


def merge_kernel(core_ref, own_ref, recv_ref, p1_ref, p2_ref):
    core = core_ref[0]
    own = own_ref[...].astype(f32)
    recv = recv_ref[...].astype(f32)
    top = jnp.where(core == 0, own, recv)
    low = jnp.where(core == 0, recv, own)
    cat = lambda a, b: jnp.concatenate([a, b], axis=0).astype(bf16)
    p1 = cat(top[:, :C1], low[:, :C1])
    for k in range(p1_ref.shape[0]):
        p1_ref[k] = p1
    p2_ref[:, :CO] = cat(top[:, C1 : C1 + CO], low[:, C1 : C1 + CO])
    for c, v in ((0, top), (1, low)):
        base = C1 + CO
        p2_ref[:, CO + D * c : CO + D * c + D] = cat(v[:, base : base + D], v[:, base + D : base + 2 * D])


def merge(core, own, recv, chips):
    rows = own.shape[0]
    vm = pl.BlockSpec(memory_space=pltpu.VMEM)
    return pl.pallas_call(
        merge_kernel, name="merge", in_specs=[smem(), vm, vm], out_specs=[vm] * 2,
        out_shape=[jax.ShapeDtypeStruct((chips, 2 * rows, C1), bf16), jax.ShapeDtypeStruct((2 * rows, C2), bf16)],
        compiler_params=params(),
    )(core, own, recv)


def k0_kernel(core_ref, own_ref, recv_ref, w_ref, vec_ref, m_s, *, n):
    core = core_ref[0]
    own = own_ref[...]
    recv = recv_ref[...]
    first = jnp.where(core == 0, own, recv)
    second = jnp.where(core == 0, recv, own)
    w_ref[:, :C1] = first
    w_ref[:, C1:] = second[:, : 3 * D - C1]
    m_s[...] = second[:, 3 * D - C1 :].astype(f32)
    per = D // n
    ng, nb = 2 * D // n, (NV - 2 * D) // n
    for d in range(n):
        vec_ref[0:1, ng * d : ng * d + ng] = m_s[per * d : per * d + 1, :ng]
        vec_ref[0:1, 2 * D + nb * d : 2 * D + nb * d + nb] = m_s[per * d + 1 : per * d + 2, :nb]


def k0(core, own, recv, n):
    vm = pl.BlockSpec(memory_space=pltpu.VMEM)
    return pl.pallas_call(
        functools.partial(k0_kernel, n=n), name="k0", in_specs=[smem(), vm, vm], out_specs=[vm, vm],
        out_shape=[jax.ShapeDtypeStruct((D, 3 * D), bf16), jax.ShapeDtypeStruct((1, NV), f32)],
        scratch_shapes=[pltpu.VMEM((D, 128), f32)],
        compiler_params=params(),
    )(core, own, recv)


def k1_kernel(x_ref, w_ref, vec_ref, *rest):
    attn_fwd_body(x_ref, w_ref[...], vec_ref[...], *rest[-5:])


def k1(x, w, vec, start, count, prev=()):
    n = x.shape[0]
    blk = lambda r, c: pl.BlockSpec((1, r, c), lambda i: (i + start, 0, 0))
    return pl.pallas_call(
        k1_kernel,
        name="k1",
        grid=(count,),
        in_specs=[blk(S, D), full((D, 3 * D)), full((1, NV))] + [any_spec()] * len(prev),
        out_specs=[blk(SP, D), blk(SP, 3 * D), blk(SP, D), blk(8, SQ), blk(SP, D)],
        out_shape=[
            jax.ShapeDtypeStruct((n, SP, D), bf16),
            jax.ShapeDtypeStruct((n, SP, 3 * D), bf16),
            jax.ShapeDtypeStruct((n, SP, D), bf16),
            jax.ShapeDtypeStruct((n, 8, SQ), f32),
            jax.ShapeDtypeStruct((n, SP, D), bf16),
        ],
        input_output_aliases={3 + k: k for k in range(len(prev))},
        cost_estimate=cost(count * 1e9, count * 1e6, count * 3e5),
        compiler_params=params(),
    )(x, w, vec, *prev)


CH = 768


def gelu_parts(u):
    cum = 0.5 * (1.0 + lax.erf(u * (1.0 / math.sqrt(2.0))))
    den = jnp.exp(-0.5 * u * u) * (1.0 / math.sqrt(2.0 * math.pi))
    return u * cum, cum + u * den


def k2_kernel(core_ref, live_ref, x_ref, g_ref, o_ref, oall_ref, owna_ref, ownb_ref, recva_ref, recvb_ref, vec_ref,
              out_ref, dr_ref, keep_ref, send_ref, wo_ref, sums_ref,
              a2_s, du_s, gl_s, eb_s, drb_s, w1_ref, w2_ref, *, pieces, cap):
    i = pl.program_id(0)
    n = pl.num_programs(0)
    core = core_ref[0]
    unit = D // pieces
    vec = vec_ref[...]
    live = (lax.rem(i, cap) < live_ref[lax.div(i, cap), 0]).astype(f32)
    rows = pl.ds(i * SP, SP)

    @pl.when(i == 0)
    def _():
        sums_ref[...] = jnp.zeros_like(sums_ref)
        own = jnp.concatenate([owna_ref[...], ownb_ref[...]], axis=1)
        recv = jnp.concatenate([recva_ref[...], recvb_ref[...]], axis=1)
        sets = (jnp.where(core == 0, own, recv), jnp.where(core == 0, recv, own))
        blocks = []
        for s in range(2):
            w1_ref[:, CF * s : CF * s + CF] = sets[s][:, :CF]
            blocks.append(sets[s][:, CO:].astype(f32))
        wo_ref[:, :256] = sets[0][:, CF:CO]
        wo_ref[:, 256:] = sets[1][:, CF + 128 : CO]
        for p in range(pieces):
            group = []
            for c in range(2):
                for s in range(2):
                    group.append(blocks[s][unit * p : unit * p + unit, D * c : D * c + D])
            w2_ref[4 * unit * p : 4 * unit * p + 4 * unit, :] = jnp.concatenate(group, axis=0).astype(bf16)

    res = pad_rows(x_ref[0].astype(f32)) + nn(o_ref[0], wo_ref[...]) + vec[:, BO : BO + D]
    n2, r2 = norm_stats(res)
    a2 = (n2 * vec[:, G2 : G2 + D] + vec[:, B2 : B2 + D]).astype(bf16)
    a2_s[rows, :] = a2
    e = pad_rows(g_ref[0].astype(f32)) * live
    eb = e.astype(bf16)
    eb_s[rows, :] = eb
    acc = res + vec[:, BF2 : BF2 + D]
    dn = jnp.zeros((SP, D), f32)
    for c in range(FF // CH):
        cs = slice(CH * c, CH * c + CH)
        u = nn(a2, w1_ref[:, cs]) + vec[:, BF1 + CH * c : BF1 + CH * c + CH]
        dg = nt(eb, w2_ref[cs, :])
        gel, slope = gelu_parts(u)
        gb = gel.astype(bf16)
        du = (dg * slope).astype(bf16)
        gl_s[rows, cs] = gb
        du_s[rows, cs] = du
        acc = acc + nn(gb, w2_ref[cs, :])
        dn = dn + nt(du, w1_ref[:, cs])
    out_ref[0] = (acc * live)[:S]
    t = dn * vec[:, G2 : G2 + D]
    dr = e + r2 * (
        t - jnp.mean(t, axis=-1, keepdims=True) - n2 * jnp.mean(t * n2, axis=-1, keepdims=True)
    )
    dr_ref[0] = dr
    drb_s[rows, :] = dr.astype(bf16)
    sums_ref[0:1, G2 : G2 + D] += jnp.sum(dn * n2, axis=0, keepdims=True)
    sums_ref[0:1, B2 : B2 + D] += jnp.sum(dn, axis=0, keepdims=True)

    @pl.when(i == n - 1)
    def _():
        ones = jnp.ones((8, a2_s.shape[0]), bf16)
        eball = eb_s[...]
        drball = drb_s[...]
        a2t = tr(a2_s[...])
        ebt = tr(eball)
        g2 = nn(ebt, gl_s[...]).T.reshape(pieces, 4, unit, D)
        go = nn(tr(oall_ref[...].reshape(-1, D)), drball).astype(bf16)

        def put(ref, s):
            ref[:, :CF] = nn(a2t, du_s[:, CF * s : CF * s + CF]).astype(bf16)
            ref[:, CF:CO] = go[:, 128 * s : 128 * s + 256]
            for c in range(2):
                ref[:, CO + D * c : CO + D * c + D] = g2[:, 2 * c + s].reshape(D, D).astype(bf16)

        @pl.when(core == 0)
        def _():
            put(keep_ref, 0)
            put(send_ref, 1)

        @pl.when(core != 0)
        def _():
            put(keep_ref, 1)
            put(send_ref, 0)

        sums_ref[:, BF1 : BF1 + FF] = nn(ones, du_s[...])
        sums_ref[:, BF2 : BF2 + D] = nn(ones, eball)
        sums_ref[:, BO : BO + D] = nn(ones, drball)


def k2(core, counts, x, g, o, own, recv, vec, pieces, cap):
    n = x.shape[0]
    blk = lambda r, c: pl.BlockSpec((1, r, c), lambda i: (i, 0, 0))
    return pl.pallas_call(
        functools.partial(k2_kernel, pieces=pieces, cap=cap),
        name="k2",
        grid=(n,),
        in_specs=[smem(), smem(), blk(S, D), blk(S, D), blk(SP, D), full((n, SP, D)),
                  full((D, C2 // 2)), full((D, C2 // 2)), full((D, C2 // 2)), full((D, C2 // 2)), full((1, NV))],
        out_specs=[blk(S, D), blk(SP, D), full((D, C2)), full((D, C2)), full((D, D)), full((8, NV))],
        out_shape=[
            jax.ShapeDtypeStruct((n, S, D), f32),
            jax.ShapeDtypeStruct((n, SP, D), f32),
            jax.ShapeDtypeStruct((D, C2), bf16),
            jax.ShapeDtypeStruct((D, C2), bf16),
            jax.ShapeDtypeStruct((D, D), bf16),
            jax.ShapeDtypeStruct((8, NV), f32),
        ],
        scratch_shapes=[
            pltpu.VMEM((n * SP, D), bf16),
            pltpu.VMEM((n * SP, FF), bf16),
            pltpu.VMEM((n * SP, FF), bf16),
            pltpu.VMEM((n * SP, D), bf16),
            pltpu.VMEM((n * SP, D), bf16),
            pltpu.VMEM((D, FF), bf16),
            pltpu.VMEM((FF, D), bf16),
        ],
        cost_estimate=cost(n * 2e9, n * 4e6, n * 6e5),
        compiler_params=params(),
    )(core, counts, x, g, o, o, *own, *recv, vec)


def k3_kernel(qkv_ref, lse_ref, dr_ref, wo_ref, *rest):
    dp_ref = rest[-1]
    do = nt(dr_ref[0].astype(bf16), wo_ref[...]).astype(bf16)
    first = head_masks()
    lanes0 = jnp.zeros((128, SQ - SP), bf16)
    rows0 = jnp.zeros((SQ - SP, 128), bf16)
    for j in range(H // 2):
        q2 = qkv_ref[0, :, 128 * j : 128 * j + 128]
        k2_ = qkv_ref[0, :, D + 128 * j : D + 128 * j + 128]
        v2 = qkv_ref[0, :, 2 * D + 128 * j : 2 * D + 128 * j + 128]
        do2 = do[:, 128 * j : 128 * j + 128]
        q2t = jnp.concatenate([tr(q2 * 0.125), lanes0], axis=1)
        do2t = jnp.concatenate([tr(do2), lanes0], axis=1)
        k2t = tr(k2_)
        dqs = []
        dk = jnp.zeros((SP, 128), f32)
        dv = jnp.zeros((SP, 128), f32)
        for h in range(2):
            z = mask_tail(nn(pick(k2_, first, h), q2t))
            p = jnp.exp(z - lse_ref[0, pl.ds(2 * j + h, 1), :])
            dpr = nn(pick(v2, first, h), do2t)
            dot_row = jnp.sum(p * dpr, axis=0, keepdims=True)
            dz = (p * (dpr - dot_row)).astype(bf16)
            pb = p.astype(bf16)
            dv = dv + nn(pb, jnp.concatenate([pick(do2, first, h), rows0], axis=0))
            dk = dk + nn(dz, jnp.concatenate([pick(q2, first, h), rows0], axis=0))
            dqs.append(nn(k2t[HD * h : HD * h + HD, :], dz))
        dp_ref[0, :, 128 * j : 128 * j + 128] = (jnp.concatenate(dqs, axis=0).T[:SP] * 0.125).astype(bf16)
        dp_ref[0, :, D + 128 * j : D + 128 * j + 128] = (dk * 0.125).astype(bf16)
        dp_ref[0, :, 2 * D + 128 * j : 2 * D + 128 * j + 128] = dv.astype(bf16)


def k3(qkv, lse, dr, wo, start, count, prev=()):
    n = qkv.shape[0]
    blk = lambda r, c: pl.BlockSpec((1, r, c), lambda i: (i + start, 0, 0))
    return pl.pallas_call(
        k3_kernel,
        name="k3",
        grid=(count,),
        in_specs=[blk(SP, 3 * D), blk(8, SQ), blk(SP, D), full((D, D))] + [any_spec()] * len(prev),
        out_specs=blk(SP, 3 * D),
        out_shape=jax.ShapeDtypeStruct((n, SP, 3 * D), bf16),
        input_output_aliases={4 + k: k for k in range(len(prev))},
        cost_estimate=cost(count * 1.2e9, count * 2e6, count * 3e5),
        compiler_params=params(),
    )(qkv, lse, dr, wo, *prev)


def k5_kernel(x_ref, dr_ref, dp_ref, w_ref, vec_ref, dx_ref):
    dn = nt(dp_ref[0], w_ref[...])
    n1, r1 = norm_stats(x_ref[0].astype(f32))
    t = dn[:S] * vec_ref[:, G1 : G1 + D]
    dx_ref[0] = dr_ref[0, :S, :] + r1 * (
        t - jnp.mean(t, axis=-1, keepdims=True) - n1 * jnp.mean(t * n1, axis=-1, keepdims=True)
    )


def k5(x, dr, dp, w, vec):
    n = x.shape[0]
    blk = lambda r, c: pl.BlockSpec((1, r, c), lambda i: (i, 0, 0))
    return pl.pallas_call(
        k5_kernel,
        name="k5",
        grid=(n,),
        in_specs=[blk(S, D), blk(SP, D), blk(SP, 3 * D), full((D, 3 * D)), full((1, NV))],
        out_specs=blk(S, D),
        out_shape=jax.ShapeDtypeStruct((n, S, D), f32),
        cost_estimate=cost(n * 2e8, n * 2e6),
        compiler_params=params(),
    )(x, dr, dp, w, vec)


def k4_kernel(core_ref, a1_ref, n1_ref, dp_ref, w_ref, sums2_ref, keep_ref, send_ref, v_s, m_s, *, n):
    core = core_ref[0]
    dpall = dp_ref[...].reshape(-1, 3 * D)
    gq = nn(tr(a1_ref[...].reshape(-1, D)), dpall).astype(bf16)
    bsum = nn(jnp.ones((8, dpall.shape[0]), bf16), dpall)
    weight = w_ref[...].astype(f32)
    gain = jnp.sum(weight * nn(tr(n1_ref[...].reshape(-1, D)), dpall), axis=1, keepdims=True)
    shift = jnp.sum(weight * bsum[0:1, :], axis=1, keepdims=True)
    lane = lax.broadcasted_iota(jnp.int32, (D, 128), 1)
    both = jnp.where(lane == 0, gain, shift).T
    v_s[...] = sums2_ref[0:1, :]
    v_s[:, G1 : G1 + D] = both[0:1, :]
    v_s[:, B1 : B1 + D] = both[1:2, :]
    v_s[:, BQ : BQ + D] = bsum[0:1, :D]
    v_s[:, BV : BV + D] = bsum[0:1, 2 * D :]
    m_s[...] = jnp.zeros_like(m_s)
    per = D // n
    ng, nb = 2 * D // n, (NV - 2 * D) // n
    for d in range(n):
        m_s[per * d : per * d + 1, :ng] = v_s[:, ng * d : ng * d + ng]
        m_s[per * d + 1 : per * d + 2, :nb] = v_s[:, 2 * D + nb * d : 2 * D + nb * d + nb]
    small = m_s[...].astype(bf16)

    def put(ref, s):
        if s == 0:
            ref[...] = gq[:, :C1]
        else:
            ref[:, : 3 * D - C1] = gq[:, C1:]
            ref[:, 3 * D - C1 :] = small

    @pl.when(core == 0)
    def _():
        put(keep_ref, 0)
        put(send_ref, 1)

    @pl.when(core != 0)
    def _():
        put(keep_ref, 1)
        put(send_ref, 0)


def k4(core, a1, n1, dp, w, sums2, n):
    vm = pl.BlockSpec(memory_space=pltpu.VMEM)
    shape = jax.ShapeDtypeStruct((D, C1), bf16)
    return pl.pallas_call(
        functools.partial(k4_kernel, n=n), name="k4",
        in_specs=[smem()] + [vm] * 5, out_specs=[vm] * 2, out_shape=[shape] * 2,
        scratch_shapes=[pltpu.VMEM((1, NV), f32), pltpu.VMEM((D, 128), f32)],
        cost_estimate=cost(1e9, 4e6),
        compiler_params=params(),
    )(core, a1, n1, dp, w, sums2)


def last_kernel(core_ref, own1_ref, recv1_ref, own2_ref, recv2_ref, q_ref, o_ref, f1_ref, f2_ref, g_ref, b_ref):
    core = core_ref[0]
    rows = own1_ref.shape[0] // 2
    ng, nb = g_ref.shape[1], b_ref.shape[1]

    def mine(v):
        return jnp.where(core == 0, v[:rows], v[rows:])

    pairs = []
    for own_ref, recv_ref in ((own1_ref, recv1_ref), (own2_ref, recv2_ref)):
        own = own_ref[...].astype(f32)
        recv = recv_ref[...].astype(f32)
        pairs.append((jnp.where(core == 0, own, recv), jnp.where(core == 0, recv, own)))
    qkv = [mine(v) for v in pairs[0]]
    for col in range(9):
        v = qkv[0] if col < 5 else qkv[1]
        k = col if col < 5 else col - 5
        q_ref[pl.ds(col, rows, stride=9), :] = v[:, 128 * k : 128 * k + 128]
    small = qkv[1][:, 3 * D - C1 :]
    g_ref[...] = small[0:1, :ng]
    b_ref[...] = small[1:2, :nb]
    top = [mine(v[:, :CO]) for v in pairs[1]]
    for col in range(12):
        f1_ref[pl.ds(col, rows, stride=12), :] = top[col // 6][:, 128 * (col % 6) : 128 * (col % 6) + 128]
    for col in range(3):
        s, k = (0, col) if col < 2 else (1, 1)
        o_ref[pl.ds(col, rows, stride=3), :] = top[s][:, CF + 128 * k : CF + 128 * k + 128]
    for s in range(2):
        v = pairs[1][s]
        blk = jnp.where(core == 0, v[:, CO : CO + D], v[:, CO + D :])
        for col in range(3):
            f2_ref[pl.ds(3 * 2 * rows * s + col, 2 * rows, stride=3), :] = blk[:, 128 * col : 128 * col + 128]


def last(core, own1, recv1, own2, recv2):
    rows = own1.shape[0] // 2
    n = D // rows
    vm = pl.BlockSpec(memory_space=pltpu.VMEM)
    outs = [(9 * rows, 128), (3 * rows, 128), (12 * rows, 128), (12 * rows, 128), (1, 2 * D // n), (1, (NV - 2 * D) // n)]
    return pl.pallas_call(
        last_kernel, name="last", in_specs=[smem()] + [vm] * 4, out_specs=[vm] * 6,
        out_shape=[jax.ShapeDtypeStruct(s, f32) for s in outs],
        compiler_params=params(),
    )(core, own1, recv1, own2, recv2)


def swap(v, bit, n):
    return lax.ppermute(v, "fsdp", [(i, i ^ (1 << bit)) for i in range(n)])


def exchange(v, n):
    return lax.all_to_all(v, "fsdp", 0, 0, axis_index_groups=chip_groups(n))


def side(me, bit):
    return (me >> bit) & 1


def join(own, recv, axis, flag):
    low = jnp.stack([own, recv], axis)
    high = jnp.stack([recv, own], axis)
    return jnp.where(flag == 0, low, high)


def split(arr, axis, flag):
    a = lax.index_in_dim(arr, 0, axis, keepdims=False)
    b = lax.index_in_dim(arr, 1, axis, keepdims=False)
    return jnp.where(flag == 0, a, b), jnp.where(flag == 0, b, a)


def add(keep, recv):
    return (keep.astype(f32) + recv.astype(f32)).astype(bf16)


ORDERS = ((1, 2), (2, 1))


def halves_of(arr):
    cut = (arr.shape[-1] // 2) // 128 * 128
    return [arr[..., :cut], arr[..., cut:]]


def gather_chips(piece, me, n):
    top = n.bit_length() - 2
    arr = piece
    for k, bit in enumerate(range(top, 2, -1)):
        arr = join(arr, swap(arr, bit, n), k, side(me, bit))
    ax = top - 2
    chunks = halves_of(arr)
    for stage in range(2):
        got = [swap(c, o[stage], n) for c, o in zip(chunks, ORDERS)]
        chunks = [
            join(c, r, ax + 1 if (stage == 1 and o[stage] == 1) else ax, side(me, o[stage]))
            for c, r, o in zip(chunks, got, ORDERS)
        ]
    return [c.reshape(D, -1) for c in chunks]


def scatter_chips(arr, me, n):
    top = n.bit_length() - 2
    arr = arr.reshape((2,) * top + (2 * D // n, arr.shape[1]))
    chunks = halves_of(arr)
    for stage in range(2):
        pairs = [
            split(c, top - 1 if (stage == 0 and o[stage] == 1) else top - 2, side(me, o[stage]))
            for c, o in zip(chunks, ORDERS)
        ]
        got = [swap(p[1], o[stage], n) for p, o in zip(pairs, ORDERS)]
        chunks = [add(p[0], r) for p, r in zip(pairs, got)]
    arr = jnp.concatenate(chunks, axis=-1)
    for bit in range(top, 2, -1):
        keep, send = split(arr, 0, side(me, bit))
        arr = add(keep, swap(send, bit, n))
    return arr


def local_chips(n, images, counts, out_grad, qkv_weight, out_weight, fc1_weight, fc2_weight, norm_gains, biases):
    me = lax.axis_index("fsdp")
    core = (me & 1).astype(jnp.int32).reshape(1)
    chips = n // 2
    mb, cap = images.shape[:2]
    ni = mb * cap
    x = by_image(images)
    g = by_image(out_grad)
    lanes = lambda v: v.reshape(-1, 128)
    own, send = prep(core, lanes(qkv_weight), lanes(out_weight), lanes(fc1_weight), lanes(fc2_weight),
                     norm_gains.reshape(1, -1), biases.reshape(1, -1))
    p1, p2 = merge(core, own, swap(send, 0, n), chips)
    w_own = exchange(p1, n).reshape(D, C1)
    w, vec = k0(core, w_own, swap(w_own, 0, n), n)
    f_own = gather_chips(p2, me, n)
    f_recv = [swap(f, 0, n) for f in f_own]
    half = ni // 2
    saved = ()
    for part in range(2):
        saved = k1(x, w, vec, half * part, half, saved)
    a1, qkv, o, lse, n1 = saved
    out, dr, keep2, send2, wo, sums2 = k2(core, counts, x, g, o, f_own, f_recv, vec, chips, cap)
    sum2 = scatter_chips(add(keep2, swap(send2, 0, n)), me, n)
    dp = ()
    for part in range(ni):
        dp = (k3(qkv, lse, dr, wo, part, 1, dp),)
    keep1, send1 = k4(core, a1, n1, dp[0], w, sums2, n)
    sum1 = add(keep1, swap(send1, 0, n))
    sum1 = total(exchange(sum1.reshape(chips, 2 * D // n, C1), n))
    dx = k5(x, dr, dp[0], w, vec)
    grads = last(core, sum1, swap(sum1, 0, n), sum2, swap(sum2, 0, n))
    out = by_slot(out, images.shape)
    dx = by_slot(dx, images.shape)
    return (out, dx) + tuple(v.reshape(-1) for v in grads)


def by_image(v):
    mb, cap = v.shape[:2]
    tokens = lax.optimization_barrier(v.transpose(0, 2, 1, 3))
    return tokens.transpose(0, 2, 1, 3).reshape(mb * cap, S, D)


def by_slot(v, shape):
    tokens = lax.optimization_barrier(v.reshape(shape).transpose(0, 2, 1, 3))
    return tokens.transpose(0, 2, 1, 3)


def local_named(n, *args):
    return local_chips(n, *args)


def total_kernel(x_ref, o_ref):
    acc = x_ref[0].astype(f32)
    for k in range(1, x_ref.shape[0]):
        acc = acc + x_ref[k].astype(f32)
    o_ref[...] = acc.astype(bf16)


def total(x):
    vm = pl.BlockSpec(memory_space=pltpu.VMEM)
    return pl.pallas_call(
        total_kernel, name="total", in_specs=[vm], out_specs=vm,
        out_shape=jax.ShapeDtypeStruct(x.shape[1:], bf16),
        compiler_params=params(),
    )(x)


def chip_groups(n):
    return [[i for i in range(n) if i % 2 == c] for c in range(2)]


def local_any(images, counts, out_grad, qkv_weight, out_weight, fc1_weight, fc2_weight, norm_gains, biases):
    ag = lambda v: lax.all_gather(v, "fsdp", axis=0, tiled=True)
    pieces = 16
    unit = D // pieces
    zero = jnp.zeros((1,), jnp.int32)
    w = ag(qkv_weight).reshape(D, 3 * D)
    wo_in = ag(out_weight).reshape(D, D)
    w1 = ag(fc1_weight).reshape(D, FF)
    w2 = ag(fc2_weight).reshape(pieces, 2, 2, unit, D)
    vec = jnp.concatenate([ag(norm_gains), ag(biases)]).astype(f32)[None, :]
    sets = [
        jnp.concatenate([w1[:, CF * s : CF * s + CF], wo_in[:, 128 * s : 128 * s + 256],
                         w2[:, 0, s].reshape(D, D), w2[:, 1, s].reshape(D, D)], axis=1)
        for s in range(2)
    ]
    mb, cap = images.shape[:2]
    ni = mb * cap
    x = images.reshape(ni, S, D)
    g = out_grad.reshape(ni, S, D)
    a1, qkv, o, lse, n1 = k1(x, w, vec, 0, ni)
    out, dr, set0, set1, wo, sums2 = k2(zero, counts, x, g, o, halves_of(sets[0]), halves_of(sets[1]), vec, pieces, cap)
    dp = k3(qkv, lse, dr, wo, 0, ni)
    dx = k5(x, dr, dp, w, vec)
    q0, q1 = k4(zero, a1, n1, dp, w, sums2, D // 12)
    g_qkv = jnp.concatenate([q0, q1[:, : 3 * D - C1]], axis=1)
    g_out = jnp.concatenate([set0[:, CF:CO], set1[:, CF + 128 : CO]], axis=1)
    g_fc1 = jnp.concatenate([set0[:, :CF], set1[:, :CF]], axis=1)
    f2 = [jnp.stack([s[:, CO : CO + D].reshape(pieces, unit, D), s[:, CO + D :].reshape(pieces, unit, D)], 1) for s in (set0, set1)]
    g_fc2 = jnp.stack(f2, 2).reshape(FF, D)
    small = q1[:, 3 * D - C1 :].reshape(D // 12, 12, 128)
    g_gain = small[:, 0, : 2 * D * 12 // D].reshape(-1)
    g_bias = small[:, 1, : (NV - 2 * D) * 12 // D].reshape(-1)
    rs = lambda v: lax.psum_scatter(v.reshape(-1).astype(f32), "fsdp", scatter_dimension=0, tiled=True)
    return (out.reshape(images.shape), dx.reshape(images.shape)) + tuple(
        rs(v) for v in (g_qkv, g_out, g_fc1, g_fc2, g_gain, g_bias)
    )


def solution(mesh):
    n = mesh.shape["fsdp"]
    placed = (
        P(None, "fsdp", None, None),
        P(None, "fsdp"),
        P(None, "fsdp", None, None),
    ) + (P("fsdp"),) * 6
    chips = n >= 8 and n & (n - 1) == 0 and D % n == 0 and (2 * D // n) % 8 == 0
    return jax.shard_map(
        functools.partial(local_named, n) if chips else local_any,
        mesh=mesh,
        in_specs=placed,
        out_specs=(placed[0], placed[2]) + (P("fsdp"),) * 6,
        check_vma=False,
    )
```

time: 389 us -> 157 us (0.40)
  blocking collectives: 165 us -> 0 us
  waiting for transfers between devices: 120 us -> 47.1 us
  local copies, waits for them, and re-layouts: 36.7 us -> 8.78 us
  starting transfers between devices: 0.11 us -> 27.3 us
  Pallas kernels: 44.2 us -> 68.1 us
  between operations: 13.9 us -> 0.95 us
  other arithmetic: 8.41 us -> 3.43 us
    unnamed x4 -> x0, waiting for transfers between devices: 120 us -> none
    all_gather x2 -> x0, blocking collectives: 84 us -> none  [local(): ag = lambda v: lax.all_gather(v, 'fsdp', axis=0, tiled=True)]
    unnamed x2 -> x0, blocking collectives: 80.9 us -> none
    ppermute x0 -> x20, waiting for transfers between devices: none -> 46.1 us  [swap(): return lax.ppermute(v, 'fsdp', [(i, i ^ 1 << bit) for i in range(n)])]
    pallas_call x3 -> x14, Pallas kernels: 44.2 us -> 68.1 us  [the longest x1 17.3 us: k2(): pl.pallas_call(functools.partial(k2_kernel, pieces=pieces, cap=cap), name...]
    ppermute x0 -> x20, starting transfers between devices: none -> 18.8 us  [swap(): return lax.ppermute(v, 'fsdp', [(i, i ^ 1 << bit) for i in range(n)])]
    reshape x8 -> x2, local copies, waits for them, and re-layouts: 19.3 us -> 3.29 us  [by_slot(): tokens = lax.optimization_barrier(v.reshape(shape).transpose(0, 2, 1, 3))]
    unnamed x26 -> x33, local copies, waits for them, and re-layouts: 15.6 us -> 3.33 us
  transfers between devices with their start and end apart: 3 -> 22, of which waited for: 1 -> 14; matrix products, arithmetic and copies ran while one was open for 7% -> 6% of each run, Pallas kernels for 3% -> 29%
where the time goes in v2:
time: 157 us; the launch traced here: 156 us
  Pallas kernels  68.1 us (43%)
  waiting for transfers between devices  47.1 us (30%)
  starting transfers between devices  27.3 us (17%)
  local copies, waits for them, and re-layouts  8.78 us (6%)
  other arithmetic  3.43 us (2%)
    ppermute x20, waiting for transfers between devices, swap(): return lax.ppermute(v, 'fsdp', [(i, i ^ 1 << bit) for i in range(n)])  46.1 us
    ppermute x20, starting transfers between devices, swap(): return lax.ppermute(v, 'fsdp', [(i, i ^ 1 << bit) for i in range(n)])  18.8 us
    pallas_call x1, Pallas kernels, k2(): pl.pallas_call(functools.partial(k2_kernel, pieces=pieces, cap=cap), name...  17.3 us
    pallas_call x4, Pallas kernels, k3(): pl.pallas_call(k3_kernel, name='k3', grid=(count,), in_specs=[blk(SP, 3 *...  16.5 us
    pallas_call x2, Pallas kernels, k1(): pl.pallas_call(k1_kernel, name='k1', grid=(count,), in_specs=[blk(S, D),...  13.7 us
    all_to_all x2, starting transfers between devices, exchange(): return lax.all_to_all(v, 'fsdp', 0, 0, axis_index_groups=chip_groups(n))  8.52 us
    pallas_call x1, Pallas kernels, k4(): pl.pallas_call(functools.partial(k4_kernel, n=n), name='k4', in_specs=[sm...  6.15 us
    pallas_call x1, Pallas kernels, k5(): pl.pallas_call(k5_kernel, name='k5', grid=(n,), in_specs=[blk(S, D), blk(...  5.53 us
  transfers between devices with their start and end apart: 22, of which 14 were waited for; matrix products, arithmetic and copies ran while one was open for 6% of the time, Pallas kernels for 29%

profile of v2, /device:TPU:0, one launch (start us, length us, event | category | flops | bytes accessed | tf_op | source)
XLA Modules:
  0.0 155.7 jit_solution(183150950262472607)
XLA Ops:
  0.6 1.5 prep.1
  2.7 1.1 collective-permute-done.recv_ref
  3.8 0.6 copy-done.13
  4.4 1.8 %merge.1 = (bf16[16,24,640]{2,1,0:T(8,128)(2,1)}, bf16[24,1792]{1,0:T(8,128)(2,1)}) custom-call(s32[1]{0:T(128)} %bitcast.core_ref, bf16[12,2432]{1,0:T(8,128)(2,1)} %get-tuple-element.38.own_ref, bf16[12,2432]{1,0:T(8,128)(2,1)} %copy-done.13), custom_call_target="tpu_custom_call" | custom-call | tf_op jit(solution)/shard_map/merge/pallas_call | solution.py:186
  6.2 3.9 %collective-permute-start.2 = (bf16[24,1792]{1,0:T(8,128)(2,1)}, bf16[24,1792]{1,0:T(8,128)(2,1)S(1)}, u32[]{:S(2)}, u32[]{:S(2)}) collective-permute-start(bf16[24,1792]{1,0:T(8,128)(2,1)} %get-tuple-element.49), channel_id=1, source_target_pairs={{0,16},{1,17},{2,18},{3,19},{4,20},{5,21},{6,22},{7,23},{8,24},{9,... | collective-permute-start | bytes 258056 | tf_op jit(solution)/shard_map/ppermute | solution.py:549
  10.1 4.8 %all-to-all-start = ((bf16[16,24,640]{2,1,0:T(8,128)(2,1)}), bf16[16,24,640]{2,1,0:T(8,128)(2,1)S(1)}, u32[]{:S(2)}, u32[]{:S(2)}) async-start(bf16[16,24,640]{2,1,0:T(8,128)(2,1)} %get-tuple-element.40), calls=%async_computation | async-start | bytes 983040 | tf_op jit(solution)/shard_map/all_to_all | solution.py:553
  15.1 1.0 maximum_select_fusion.8
  16.1 1.9 %collective-permute-start.3 = (bf16[2,24,1792]{2,1,0:T(8,128)(2,1)S(1)}, bf16[2,24,1792]{2,1,0:T(8,128)(2,1)S(1)}, u32[]{:S(2)}, u32[]{:S(2)}) collective-permute-start(bf16[2,24,1792]{2,1,0:T(8,128)(2,1)S(1)} %maximum_select_fusion.8), channel_id=1, source_target_pairs={{0,8},{1,9},{2,10},{3,11},{4,12},{5,13},{6,14},{7,15},{8,0},{9,1},... | collective-permute-start | bytes 516104 | tf_op jit(solution)/shard_map/ppermute | solution.py:549
  18.0 10.9 %collective-permute-done.3 = bf16[2,24,1792]{2,1,0:T(8,128)(2,1)S(1)} collective-permute-done((bf16[2,24,1792]{2,1,0:T(8,128)(2,1)S(1)}, bf16[2,24,1792]{2,1,0:T(8,128)(2,1)S(1)}, u32[]{:S(2)}, u32[]{:S(2)}) %collective-permute-start.3) | collective-permute-done | bytes 172064 | tf_op jit(solution)/shard_map/ppermute | solution.py:549
  29.0 1.5 collective-permute-start.4
  30.5 1.5 collective-permute-start.6
  32.0 2.5 %collective-permute-done.4 = bf16[2,2,24,896]{3,2,0,1:T(8,128)(2,1)S(1)} collective-permute-done((bf16[2,2,24,896]{3,2,0,1:T(8,128)(2,1)S(1)}, bf16[2,2,24,896]{3,2,0,1:T(8,128)(2,1)S(1)}, u32[]{:S(2)}, u32[]{:S(2)}) %collective-permute-start.4) | collective-permute-done | bytes 172064 | tf_op jit(solution)/shard_map/ppermute | solution.py:549
  34.5 1.5 collective-permute-start.5
  36.0 1.2 collective-permute-done.6
  37.9 5.4 %collective-permute-done.5 = bf16[2,2,2,24,896]{4,3,0,1,2:T(8,128)(2,1)S(1)} collective-permute-done((bf16[2,2,2,24,896]{4,3,0,1,2:T(8,128)(2,1)S(1)}, bf16[2,2,2,24,896]{4,3,0,1,2:T(8,128)(2,1)S(1)}, u32[]{:S(2)}, u32[]{:S(2)}) %collective-permute-start.5) | collective-permute-done | bytes 344096 | tf_op jit(solution)/shard_map/ppermute | solution.py:549
  43.5 1.1 collective-permute-done.7
  45.4 0.6 copy.40.live_ref
  46.1 0.9 copy.36
  47.0 0.9 copy.37
  47.9 2.3 %k0.1 = (bf16[384,1152]{1,0:T(8,128)(2,1)}, f32[1,4608]{1,0:T(1,128)}) custom-call(s32[1]{0:T(128)} %bitcast.core_ref, bf16[384,640]{1,0:T(8,128)(2,1)} %bitcast.91, bf16[384,640]{1,0:T(8,128)(2,1)} %collective-permute-done.1.recv_ref), custom_call_target="tpu_custom_call" | custom-call | tf_op jit(solution)/shard_map/k0/pallas_call | solution.py:211
  50.2 6.8 %k1.2 = (bf16[4,208,384]{2,1,0:T(8,128)(2,1)}, bf16[4,208,1152]{2,1,0:T(8,128)(2,1)}, bf16[4,208,384]{2,1,0:T(8,128)(2,1)}, f32[4,8,256]{2,1,0:T(8,128)}, bf16[4,208,384]{2,1,0:T(8,128)(2,1)}) custom-call(bf16[4,197,384]{2,1,0:T(8,128)(2,1)} %bitcast.86, bf16[384,1152]{1,0:T(8,128)(2,1)} %get-tuple-element.41.w_ref, f32[1,4608]{1,0:T(1,128)} %get-tuple-element.42.vec_ref), custom_call_target="tpu_custom_call" | custom-call | flops 2000000000 | bytes 2000000 | tf_op jit(solution)/shard_map/k1/pallas_call | solution.py:226
  57.1 6.8 %k1.3 = (bf16[4,208,384]{2,1,0:T(8,128)(2,1)}, bf16[4,208,1152]{2,1,0:T(8,128)(2,1)}, bf16[4,208,384]{2,1,0:T(8,128)(2,1)}, f32[4,8,256]{2,1,0:T(8,128)}, bf16[4,208,384]{2,1,0:T(8,128)(2,1)}) custom-call(bf16[4,197,384]{2,1,0:T(8,128)(2,1)} %bitcast.87, ...), custom_call_target="tpu_custom_call", output_to_operand_aliasing={{0}: (3, {}), {1}: (4, {}), {2}: (5, {}), {3}: (6, {}), {4}... | custom-call | flops 2000000000 | bytes 2000000 | tf_op jit(solution)/shard_map/k1/pallas_call | solution.py:226
  63.9 17.3 %k2.1 = (f32[4,197,384]{2,1,0:T(8,128)}, f32[4,208,384]{2,1,0:T(8,128)}, bf16[384,1792]{1,0:T(8,128)(2,1)}, bf16[384,1792]{1,0:T(8,128)(2,1)}, bf16[384,384]{1,0:T(8,128)(2,1)}, /*index=5*/f32[8,4608]{1,0:T(8,128)}) custom-call(s32[1]{0:T(128)} %bitcast.core_ref, s32[2,1]{1,0:T(2,128)} %copy.40.live_ref, bf16[4,197,384]{2,1,0:T(8,128)(2,1)} %bitcast.88, ...), custom_call_target="tpu_custom_call" | custom-call | flops 8000000000 | bytes 16000000 | tf_op jit(solution)/shard_map/k2/pallas_call | solution.py:348
  81.4 4.1 %k3.4.rest_0_ = bf16[4,208,1152]{2,1,0:T(8,128)(2,1)} custom-call(bf16[4,208,1152]{2,1,0:T(8,128)(2,1)} %get-tuple-element.52.qkv_ref, f32[4,8,256]{2,1,0:T(8,128)} %get-tuple-element.53.lse_ref, f32[4,208,384]{2,1,0:T(8,128)} %get-tuple-element.51.dr_ref, bf16[384,384]{1,0:T(8,128)(2,1)} %get-tuple-element.54.wo_ref), custom_call_target="tpu_custom_call" | custom-call | flops 1200000000 | bytes 2000000 | tf_op jit(solution)/shard_map/k3/pallas_call | solution.py:412
  85.5 4.1 %k3.5.rest_0_ = bf16[4,208,1152]{2,1,0:T(8,128)(2,1)} custom-call(bf16[4,208,1152]{2,1,0:T(8,128)(2,1)} %get-tuple-element.52.qkv_ref, f32[4,8,256]{2,1,0:T(8,128)} %get-tuple-element.53.lse_ref, f32[4,208,384]{2,1,0:T(8,128)} %get-tuple-element.51.dr_ref, bf16[384,384]{1,0:T(8,128)(2,1)} %get-tuple-element.54.wo_ref, ...), custom_call_target="tpu_custom_call", output_to_operand_aliasing={{}: (4, {})} | custom-call | flops 1200000000 | bytes 2000000 | tf_op jit(solution)/shard_map/k3/pallas_call | solution.py:412
  89.6 4.2 %k3.6.rest_0_ = bf16[4,208,1152]{2,1,0:T(8,128)(2,1)} custom-call(bf16[4,208,1152]{2,1,0:T(8,128)(2,1)} %get-tuple-element.52.qkv_ref, f32[4,8,256]{2,1,0:T(8,128)} %get-tuple-element.53.lse_ref, f32[4,208,384]{2,1,0:T(8,128)} %get-tuple-element.51.dr_ref, bf16[384,384]{1,0:T(8,128)(2,1)} %get-tuple-element.54.wo_ref, ...), custom_call_target="tpu_custom_call", output_to_operand_aliasing={{}: (4, {})} | custom-call | flops 1200000000 | bytes 2000000 | tf_op jit(solution)/shard_map/k3/pallas_call | solution.py:412
  93.8 4.1 %k3.7.dp_ref = bf16[4,208,1152]{2,1,0:T(8,128)(2,1)} custom-call(bf16[4,208,1152]{2,1,0:T(8,128)(2,1)} %get-tuple-element.52.qkv_ref, f32[4,8,256]{2,1,0:T(8,128)} %get-tuple-element.53.lse_ref, f32[4,208,384]{2,1,0:T(8,128)} %get-tuple-element.51.dr_ref, bf16[384,384]{1,0:T(8,128)(2,1)} %get-tuple-element.54.wo_ref, ...), custom_call_target="tpu_custom_call", output_to_operand_aliasing={{}: (4, {})} | custom-call | flops 1200000000 | bytes 2000000 | tf_op jit(solution)/shard_map/k3/pallas_call | solution.py:412
  97.9 6.2 %k4.1 = (bf16[384,640]{1,0:T(8,128)(2,1)}, bf16[384,640]{1,0:T(8,128)(2,1)}) custom-call(s32[1]{0:T(128)} %bitcast.core_ref, bf16[4,208,384]{2,1,0:T(8,128)(2,1)} %get-tuple-element.55.a1_ref, bf16[4,208,384]{2,1,0:T(8,128)(2,1)} %get-tuple-element.56.n1_ref, bf16[4,208,1152]{2,1,0:T(8,128)(2,1)} %k3.7.dp_ref, bf16[384,1152]{1,0:T(8,128)(2,1)} %get-tuple-element.41.w_ref, ...), custom_call_target="tpu_custom_call" | custom-call | flops 1000000000 | bytes 4000000 | tf_op jit(solution)/shard_map/k4/pallas_call | solution.py:493
  104.9 1.9 %collective-permute-start.15 = (bf16[2,2,2,24,896]{4,3,1,0,2:T(8,128)(2,1)S(1)}, bf16[2,2,2,24,896]{4,3,1,0,2:T(8,128)(2,1)S(1)}, u32[]{:S(2)}, u32[]{:S(2)}) collective-permute-start(bf16[2,2,2,24,896]{4,3,1,0,2:T(8,128)(2,1)S(1)} %select_bitcast_fusion), channel_id=1, source_target_pairs={{0,4},{1,5},{2,6},{3,7},{4,0},{5,1},{6,2},{7,3},{8,12},{9,13},{10,... | collective-permute-start | bytes 1032200 | tf_op jit(solution)/shard_map/ppermute | solution.py:549
  107.0 8.1 %collective-permute-done.15 = bf16[2,2,2,24,896]{4,3,1,0,2:T(8,128)(2,1)S(1)} collective-permute-done((bf16[2,2,2,24,896]{4,3,1,0,2:T(8,128)(2,1)S(1)}, bf16[2,2,2,24,896]{4,3,1,0,2:T(8,128)(2,1)S(1)}, u32[]{:S(2)}, u32[]{:S(2)}) %collective-permute-start.15) | collective-permute-done | bytes 344096 | tf_op jit(solution)/shard_map/ppermute | solution.py:549
  115.5 1.2 collective-permute-done.13
  117.3 3.5 %collective-permute-done.16 = bf16[2,2,24,896]{3,2,1,0:T(8,128)(2,1)S(1)} collective-permute-done((bf16[2,2,24,896]{3,2,1,0:T(8,128)(2,1)S(1)}, bf16[2,2,24,896]{3,2,1,0:T(8,128)(2,1)S(1)}, u32[]{:S(2)}, u32[]{:S(2)}) %collective-permute-start.16) | collective-permute-done | bytes 172064 | tf_op jit(solution)/shard_map/ppermute | solution.py:549
  121.0 1.4 collective-permute-done.14
  122.5 1.9 %collective-permute-start.17 = (bf16[2,24,1792]{2,1,0:T(8,128)(2,1)S(1)}, bf16[2,24,1792]{2,1,0:T(8,128)(2,1)S(1)}, u32[]{:S(2)}, u32[]{:S(2)}) collective-permute-start(bf16[2,24,1792]{2,1,0:T(8,128)(2,1)S(1)} %select_bitcast_fusion.2), channel_id=1, source_target_pairs={{0,16},{1,17},{2,18},{3,19},{4,20},{5,21},{6,22},{7,23},{8,24},{9,... | collective-permute-start | bytes 516104 | tf_op jit(solution)/shard_map/ppermute | solution.py:549
  124.4 0.9 add_convert_fusion.1
  125.3 3.7 %all-to-all-start.1 = ((bf16[16,24,640]{2,1,0:T(8,128)(2,1)}), bf16[16,24,640]{2,1,0:T(8,128)(2,1)S(1)}, u32[]{:S(2)}, u32[]{:S(2)}) async-start(bf16[16,24,640]{2,1,0:T(8,128)(2,1)} %bitcast.37), calls=%async_computation.1 | async-start | bytes 983040 | tf_op jit(solution)/shard_map/all_to_all | solution.py:553
  129.0 4.1 %collective-permute-done.17 = bf16[2,24,1792]{2,1,0:T(8,128)(2,1)S(1)} collective-permute-done((bf16[2,24,1792]{2,1,0:T(8,128)(2,1)S(1)}, bf16[2,24,1792]{2,1,0:T(8,128)(2,1)S(1)}, u32[]{:S(2)}, u32[]{:S(2)}) %collective-permute-start.17) | collective-permute-done | bytes 172064 | tf_op jit(solution)/shard_map/ppermute | solution.py:549
  133.2 1.8 %collective-permute-start.18 = (bf16[24,1792]{1,0:T(8,128)(2,1)S(1)}, bf16[24,1792]{1,0:T(8,128)(2,1)S(1)}, u32[]{:S(2)}, u32[]{:S(2)}) collective-permute-start(bf16[24,1792]{1,0:T(8,128)(2,1)S(1)} %select_bitcast_fusion.5), channel_id=1, source_target_pairs={{0,8},{1,9},{2,10},{3,11},{4,12},{5,13},{6,14},{7,15},{8,0},{9,1},... | collective-permute-start | bytes 258056 | tf_op jit(solution)/shard_map/ppermute | solution.py:549
  135.0 5.3 %collective-permute-done.18 = bf16[24,1792]{1,0:T(8,128)(2,1)S(1)} collective-permute-done((bf16[24,1792]{1,0:T(8,128)(2,1)S(1)}, bf16[24,1792]{1,0:T(8,128)(2,1)S(1)}, u32[]{:S(2)}, u32[]{:S(2)}) %collective-permute-start.18) | collective-permute-done | bytes 86048 | tf_op jit(solution)/shard_map/ppermute | solution.py:549
  140.4 1.1 all-to-all-done.1.x_ref
  141.5 0.8 copy-done.2
  142.3 1.7 %total.1.own1_ref = bf16[24,640]{1,0:T(8,128)(2,1)} custom-call(bf16[16,24,640]{2,1,0:T(8,128)(2,1)} %copy-done.2), custom_call_target="tpu_custom_call" | custom-call | tf_op jit(solution)/shard_map/total/pallas_call | solution.py:678
  144.0 5.5 %k5.1 = f32[4,197,384]{2,1,0:T(8,128)} custom-call(bf16[4,197,384]{2,1,0:T(8,128)(2,1)} %bitcast.89, f32[4,208,384]{2,1,0:T(8,128)} %get-tuple-element.51.dr_ref, bf16[4,208,1152]{2,1,0:T(8,128)(2,1)} %k3.7.dp_ref, bf16[384,1152]{1,0:T(8,128)(2,1)} %get-tuple-element.41.w_ref, f32[1,4608]{1,0:T(1,128)} %get-tuple-element.42.vec_ref), custom_call_target="tpu_custom_call" | custom-call | flops 800000000 | bytes 8000000 | tf_op jit(solution)/shard_map/k5/pallas_call | solution.py:437
  149.5 1.6 %copy.62 = f32[2,2,197,384]{3,1,2,0:T(2,128)} copy(f32[2,2,197,384]{3,2,1,0:T(8,128)S(1)} %bitcast.92) | data formatting | bytes 2420736 | tf_op jit(solution)/shard_map/reshape | solution.py:661
  151.2 1.6 %copy.61 = f32[2,2,197,384]{3,1,2,0:T(2,128)} copy(f32[2,2,197,384]{3,2,1,0:T(8,128)S(1)} %bitcast.85) | data formatting | bytes 2420736 | tf_op jit(solution)/shard_map/reshape | solution.py:661
  152.8 0.6 copy-done.14
  153.4 0.6 copy-done.12
  154.1 1.7 %last.1 = (f32[108,128]{1,0:T(8,128)}, f32[36,128]{1,0:T(8,128)}, f32[144,128]{1,0:T(8,128)}, f32[144,128]{1,0:T(8,128)}, f32[1,24]{1,0:T(1,128)}, /*index=5*/f32[1,120]{1,0:T(1,128)}) custom-call(s32[1]{0:T(128)} %bitcast.core_ref, bf16[24,640]{1,0:T(8,128)(2,1)} %total.1.own1_ref, bf16[24,640]{1,0:T(8,128)(2,1)} %copy-done.14, ...), custom_call_target="tpu_custom_call" | custom-call | tf_op jit(solution)/shard_map/last/pallas_call | solution.py:541
  (75 shorter events, 5.0 us)
Async XLA Ops:
  2.2 1.6 %collective-permute-start = (bf16[12,2432]{1,0:T(8,128)(2,1)}, bf16[12,2432]{1,0:T(8,128)(2,1)S(1)}, u32[]{:S(2)}, u32[]{:S(2)}) collective-permute-start(bf16[12,2432]{1,0:T(8,128)(2,1)} %get-tuple-element.39), channel_id=1, source_target_pairs={{0,1},{1,0},{2,3},{3,2},{4,5},{5,4},{6,7},{7,6},{8,9},{9,8},{10,11... | collective-permute-start | bytes 175112 | tf_op jit(solution)/shard_map/ppermute | solution.py:549
  3.8 0.6 copy-start.13
  6.2 11.8 %copy-start.11 = (bf16[24,1792]{1,0:T(8,128)(2,1)S(1)}, bf16[24,1792]{1,0:T(8,128)(2,1)}, u32[]{:S(2)}) copy-start(bf16[24,1792]{1,0:T(8,128)(2,1)} %get-tuple-element.49) | copy-start | bytes 258052
  6.2 8.9 %collective-permute-start.2 = (bf16[24,1792]{1,0:T(8,128)(2,1)}, bf16[24,1792]{1,0:T(8,128)(2,1)S(1)}, u32[]{:S(2)}, u32[]{:S(2)}) collective-permute-start(bf16[24,1792]{1,0:T(8,128)(2,1)} %get-tuple-element.49), channel_id=1, source_target_pairs={{0,16},{1,17},{2,18},{3,19},{4,20},{5,21},{6,22},{7,23},{8,24},{9,... | collective-permute-start | bytes 258056 | tf_op jit(solution)/shard_map/ppermute | solution.py:549
  10.1 27.7 %all-to-all-start = ((bf16[16,24,640]{2,1,0:T(8,128)(2,1)}), bf16[16,24,640]{2,1,0:T(8,128)(2,1)S(1)}, u32[]{:S(2)}, u32[]{:S(2)}) async-start(bf16[16,24,640]{2,1,0:T(8,128)(2,1)} %get-tuple-element.40), calls=%async_computation | async-start | bytes 983040 | tf_op jit(solution)/shard_map/all_to_all | solution.py:553
  16.1 12.8 %collective-permute-start.3 = (bf16[2,24,1792]{2,1,0:T(8,128)(2,1)S(1)}, bf16[2,24,1792]{2,1,0:T(8,128)(2,1)S(1)}, u32[]{:S(2)}, u32[]{:S(2)}) collective-permute-start(bf16[2,24,1792]{2,1,0:T(8,128)(2,1)S(1)} %maximum_select_fusion.8), channel_id=1, source_target_pairs={{0,8},{1,9},{2,10},{3,11},{4,12},{5,13},{6,14},{7,15},{8,0},{9,1},... | collective-permute-start | bytes 516104 | tf_op jit(solution)/shard_map/ppermute | solution.py:549
  29.0 5.5 %collective-permute-start.4 = (bf16[2,2,24,896]{3,2,0,1:T(8,128)(2,1)S(1)}, bf16[2,2,24,896]{3,2,0,1:T(8,128)(2,1)S(1)}, u32[]{:S(2)}, u32[]{:S(2)}) collective-permute-start(bf16[2,2,24,896]{3,2,0,1:T(8,128)(2,1)S(1)} %get-tuple-element.77), channel_id=1, source_target_pairs={{0,2},{1,3},{2,0},{3,1},{4,6},{5,7},{6,4},{7,5},{8,10},{9,11},{10,... | collective-permute-start | bytes 516104 | tf_op jit(solution)/shard_map/ppermute | solution.py:549
  30.5 6.7 %collective-permute-start.6 = (bf16[2,2,24,896]{3,2,0,1:T(8,128)(2,1)S(1)}, bf16[2,2,24,896]{3,2,0,1:T(8,128)(2,1)S(1)}, u32[]{:S(2)}, u32[]{:S(2)}) collective-permute-start(bf16[2,2,24,896]{3,2,0,1:T(8,128)(2,1)S(1)} %get-tuple-element.76), channel_id=1, source_target_pairs={{0,4},{1,5},{2,6},{3,7},{4,0},{5,1},{6,2},{7,3},{8,12},{9,13},{10,... | collective-permute-start | bytes 516104 | tf_op jit(solution)/shard_map/ppermute | solution.py:549
  34.5 8.8 %collective-permute-start.5 = (bf16[2,2,2,24,896]{4,3,0,1,2:T(8,128)(2,1)S(1)}, bf16[2,2,2,24,896]{4,3,0,1,2:T(8,128)(2,1)S(1)}, u32[]{:S(2)}, u32[]{:S(2)}) collective-permute-start(bf16[2,2,2,24,896]{4,3,0,1,2:T(8,128)(2,1)S(1)} %maximum_select_fusion.4), channel_id=1, source_target_pairs={{0,4},{1,5},{2,6},{3,7},{4,0},{5,1},{6,2},{7,3},{8,12},{9,13},{10,... | collective-permute-start | bytes 1032200 | tf_op jit(solution)/shard_map/ppermute | solution.py:549
  37.3 7.3 %collective-permute-start.7 = (bf16[2,2,2,24,896]{4,3,0,1,2:T(8,128)(2,1)S(1)}, bf16[2,2,2,24,896]{4,3,0,1,2:T(8,128)(2,1)S(1)}, u32[]{:S(2)}, u32[]{:S(2)}) collective-permute-start(bf16[2,2,2,24,896]{4,3,0,1,2:T(8,128)(2,1)S(1)} %maximum_select_fusion.6), channel_id=1, source_target_pairs={{0,2},{1,3},{2,0},{3,1},{4,6},{5,7},{6,4},{7,5},{8,10},{9,11},{10,... | collective-permute-start | bytes 1032200 | tf_op jit(solution)/shard_map/ppermute | solution.py:549
  37.8 5.7 %copy-start.1 = (bf16[16,24,640]{2,1,0:T(8,128)(2,1)}, bf16[16,24,640]{2,1,0:T(8,128)(2,1)S(1)}, u32[]{:S(2)}) copy-start(bf16[16,24,640]{2,1,0:T(8,128)(2,1)S(1)} %all-to-all-done) | copy-start | bytes 1474564
  37.8 10.1 %collective-permute-start.1 = (bf16[384,640]{1,0:T(8,128)(2,1)S(1)}, bf16[384,640]{1,0:T(8,128)(2,1)}, u32[]{:S(2)}, u32[]{:S(2)}) collective-permute-start(bf16[384,640]{1,0:T(8,128)(2,1)S(1)} %bitcast.90), channel_id=1, source_target_pairs={{0,1},{1,0},{2,3},{3,2},{4,5},{5,4},{6,7},{7,6},{8,9},{9,8},{10,11... | collective-permute-start | bytes 1474568 | tf_op jit(solution)/shard_map/ppermute | solution.py:549
  43.5 1.4 copy-start.5
  44.6 0.8 copy-start.15
  44.6 1.4 copy-start.7
  44.8 2.2 %copy-start.8 = (bf16[2,2,197,384]{3,1,2,0:T(2,128)(2,1)S(1)}, bf16[2,2,197,384]{3,1,2,0:T(2,128)(2,1)}, u32[]{:S(2)}) copy-start(bf16[2,2,197,384]{3,1,2,0:T(2,128)(2,1)} %param.11) | copy-start | bytes 1815556
  44.8 5.4 %copy-start.6 = (bf16[2,2,2,2,24,896]{5,4,3,2,1,0:T(8,128)(2,1)}, bf16[2,2,2,2,24,896]{5,4,3,2,1,0:T(8,128)(2,1)S(1)}, u32[]{:S(2)}) copy-start(bf16[2,2,2,2,24,896]{5,4,3,2,1,0:T(8,128)(2,1)S(1)} %copy.39) | copy-start | bytes 2064388
  44.8 19.1 %collective-permute-start.9 = (bf16[384,896]{1,0:T(8,128)(2,1)S(1)}, bf16[384,896]{1,0:T(8,128)(2,1)}, u32[]{:S(2)}, u32[]{:S(2)}) collective-permute-start(bf16[384,896]{1,0:T(8,128)(2,1)S(1)} %bitcast.95), channel_id=1, source_target_pairs={{0,1},{1,0},{2,3},{3,2},{4,5},{5,4},{6,7},{7,6},{8,9},{9,8},{10,11... | collective-permute-start | bytes 2064392 | tf_op jit(solution)/shard_map/ppermute | solution.py:549
  44.9 19.0 %collective-permute-start.8 = (bf16[384,896]{1,0:T(8,128)(2,1)S(1)}, bf16[384,896]{1,0:T(8,128)(2,1)}, u32[]{:S(2)}, u32[]{:S(2)}) collective-permute-start(bf16[384,896]{1,0:T(8,128)(2,1)S(1)} %bitcast.93), channel_id=1, source_target_pairs={{0,1},{1,0},{2,3},{3,2},{4,5},{5,4},{6,7},{7,6},{8,9},{9,8},{10,11... | collective-permute-start | bytes 2064392 | tf_op jit(solution)/shard_map/ppermute | solution.py:549
  81.2 23.3 %collective-permute-start.12 = (bf16[384,1792]{1,0:T(8,128)(2,1)}, bf16[384,1792]{1,0:T(8,128)(2,1)S(1)}, u32[]{:S(2)}, u32[]{:S(2)}) collective-permute-start(bf16[384,1792]{1,0:T(8,128)(2,1)} %get-tuple-element.61), channel_id=1, source_target_pairs={{0,1},{1,0},{2,3},{3,2},{4,5},{5,4},{6,7},{7,6},{8,9},{9,8},{10,11... | collective-permute-start | bytes 4128776 | tf_op jit(solution)/shard_map/ppermute | solution.py:549
  97.9 6.6 %copy-start.3 = (bf16[384,1792]{1,0:T(8,128)(2,1)S(1)}, bf16[384,1792]{1,0:T(8,128)(2,1)}, u32[]{:S(2)}) copy-start(bf16[384,1792]{1,0:T(8,128)(2,1)} %get-tuple-element.60) | copy-start | bytes 4128772
  104.1 20.4 %collective-permute-start.10 = (bf16[384,640]{1,0:T(8,128)(2,1)}, bf16[384,640]{1,0:T(8,128)(2,1)S(1)}, u32[]{:S(2)}, u32[]{:S(2)}) collective-permute-start(bf16[384,640]{1,0:T(8,128)(2,1)} %get-tuple-element.59), channel_id=1, source_target_pairs={{0,1},{1,0},{2,3},{3,2},{4,5},{5,4},{6,7},{7,6},{8,9},{9,8},{10,11... | collective-permute-start | bytes 1474568 | tf_op jit(solution)/shard_map/ppermute | solution.py:549
  104.9 10.2 %collective-permute-start.15 = (bf16[2,2,2,24,896]{4,3,1,0,2:T(8,128)(2,1)S(1)}, bf16[2,2,2,24,896]{4,3,1,0,2:T(8,128)(2,1)S(1)}, u32[]{:S(2)}, u32[]{:S(2)}) collective-permute-start(bf16[2,2,2,24,896]{4,3,1,0,2:T(8,128)(2,1)S(1)} %select_bitcast_fusion), channel_id=1, source_target_pairs={{0,4},{1,5},{2,6},{3,7},{4,0},{5,1},{6,2},{7,3},{8,12},{9,13},{10,... | collective-permute-start | bytes 1032200 | tf_op jit(solution)/shard_map/ppermute | solution.py:549
  106.9 9.8 %collective-permute-start.13 = (bf16[2,2,2,24,896]{4,3,1,0,2:T(8,128)(2,1)S(1)}, bf16[2,2,2,24,896]{4,3,1,0,2:T(8,128)(2,1)S(1)}, u32[]{:S(2)}, u32[]{:S(2)}) collective-permute-start(bf16[2,2,2,24,896]{4,3,1,0,2:T(8,128)(2,1)S(1)} %select_bitcast_fusion.1), channel_id=1, source_target_pairs={{0,2},{1,3},{2,0},{3,1},{4,6},{5,7},{6,4},{7,5},{8,10},{9,11},{10,... | collective-permute-start | bytes 1032200 | tf_op jit(solution)/shard_map/ppermute | solution.py:549
  115.3 5.6 %collective-permute-start.16 = (bf16[2,2,24,896]{3,2,1,0:T(8,128)(2,1)S(1)}, bf16[2,2,24,896]{3,2,1,0:T(8,128)(2,1)S(1)}, u32[]{:S(2)}, u32[]{:S(2)}) collective-permute-start(bf16[2,2,24,896]{3,2,1,0:T(8,128)(2,1)S(1)} %select_bitcast_fusion.3), channel_id=1, source_target_pairs={{0,2},{1,3},{2,0},{3,1},{4,6},{5,7},{6,4},{7,5},{8,10},{9,11},{10,... | collective-permute-start | bytes 516104 | tf_op jit(solution)/shard_map/ppermute | solution.py:549
  116.9 7.6 %copy-start.9 = (bf16[384,640]{1,0:T(8,128)(2,1)S(1)}, bf16[384,640]{1,0:T(8,128)(2,1)}, u32[]{:S(2)}) copy-start(bf16[384,640]{1,0:T(8,128)(2,1)} %get-tuple-element.58) | copy-start | bytes 1474564
  116.9 5.5 %collective-permute-start.14 = (bf16[2,2,24,896]{3,2,1,0:T(8,128)(2,1)S(1)}, bf16[2,2,24,896]{3,2,1,0:T(8,128)(2,1)S(1)}, u32[]{:S(2)}, u32[]{:S(2)}) collective-permute-start(bf16[2,2,24,896]{3,2,1,0:T(8,128)(2,1)S(1)} %select_bitcast_fusion.4), channel_id=1, source_target_pairs={{0,4},{1,5},{2,6},{3,7},{4,0},{5,1},{6,2},{7,3},{8,12},{9,13},{10,... | collective-permute-start | bytes 516104 | tf_op jit(solution)/shard_map/ppermute | solution.py:549
  122.5 10.6 %collective-permute-start.17 = (bf16[2,24,1792]{2,1,0:T(8,128)(2,1)S(1)}, bf16[2,24,1792]{2,1,0:T(8,128)(2,1)S(1)}, u32[]{:S(2)}, u32[]{:S(2)}) collective-permute-start(bf16[2,24,1792]{2,1,0:T(8,128)(2,1)S(1)} %select_bitcast_fusion.2), channel_id=1, source_target_pairs={{0,16},{1,17},{2,18},{3,19},{4,20},{5,21},{6,22},{7,23},{8,24},{9,... | collective-permute-start | bytes 516104 | tf_op jit(solution)/shard_map/ppermute | solution.py:549
  125.3 16.2 %all-to-all-start.1 = ((bf16[16,24,640]{2,1,0:T(8,128)(2,1)}), bf16[16,24,640]{2,1,0:T(8,128)(2,1)S(1)}, u32[]{:S(2)}, u32[]{:S(2)}) async-start(bf16[16,24,640]{2,1,0:T(8,128)(2,1)} %bitcast.37), calls=%async_computation.1 | async-start | bytes 983040 | tf_op jit(solution)/shard_map/all_to_all | solution.py:553
  133.2 7.1 %collective-permute-start.18 = (bf16[24,1792]{1,0:T(8,128)(2,1)S(1)}, bf16[24,1792]{1,0:T(8,128)(2,1)S(1)}, u32[]{:S(2)}, u32[]{:S(2)}) collective-permute-start(bf16[24,1792]{1,0:T(8,128)(2,1)S(1)} %select_bitcast_fusion.5), channel_id=1, source_target_pairs={{0,8},{1,9},{2,10},{3,11},{4,12},{5,13},{6,14},{7,15},{8,0},{9,1},... | collective-permute-start | bytes 258056 | tf_op jit(solution)/shard_map/ppermute | solution.py:549
  140.4 10.8 %copy-start.10 = (bf16[24,1792]{1,0:T(8,128)(2,1)}, bf16[24,1792]{1,0:T(8,128)(2,1)S(1)}, u32[]{:S(2)}) copy-start(bf16[24,1792]{1,0:T(8,128)(2,1)S(1)} %fusion.6.own2_ref) | copy-start | bytes 258052
  140.4 12.5 %collective-permute-start.19 = (bf16[24,1792]{1,0:T(8,128)(2,1)S(1)}, bf16[24,1792]{1,0:T(8,128)(2,1)S(1)}, u32[]{:S(2)}, u32[]{:S(2)}) collective-permute-start(bf16[24,1792]{1,0:T(8,128)(2,1)S(1)} %fusion.6.own2_ref), channel_id=1, source_target_pairs={{0,1},{1,0},{2,3},{3,2},{4,5},{5,4},{6,7},{7,6},{8,9},{9,8},{10,11... | collective-permute-start | bytes 258056 | tf_op jit(solution)/shard_map/ppermute | solution.py:549
  141.5 0.8 copy-start.2
  144.0 5.5 %copy-start.4 = (f32[4,197,384]{2,1,0:T(8,128)S(1)}, f32[4,197,384]{2,1,0:T(8,128)}, u32[]{:S(2)}) copy-start(f32[4,197,384]{2,1,0:T(8,128)} %get-tuple-element.50) | copy-start | bytes 3631108
  144.0 8.8 %collective-permute-start.11 = (bf16[24,640]{1,0:T(8,128)(2,1)}, bf16[24,640]{1,0:T(8,128)(2,1)S(1)}, u32[]{:S(2)}, u32[]{:S(2)}) collective-permute-start(bf16[24,640]{1,0:T(8,128)(2,1)} %total.1.own1_ref), channel_id=1, source_target_pairs={{0,1},{1,0},{2,3},{3,2},{4,5},{5,4},{6,7},{7,6},{8,9},{9,8},{10,11... | collective-permute-start | bytes 92168 | tf_op jit(solution)/shard_map/ppermute | solution.py:549
  149.5 1.7 %copy-start = (f32[4,197,384]{2,1,0:T(8,128)S(1)}, f32[4,197,384]{2,1,0:T(8,128)}, u32[]{:S(2)}) copy-start(f32[4,197,384]{2,1,0:T(8,128)} %k5.1) | copy-start | bytes 3631108
  152.8 0.6 copy-start.14
  153.4 0.6 copy-start.12

commit v3 on v2

v3 whole, which is shorter than its diff:
```python
import functools
import math

import jax
import jax.numpy as jnp
from jax import lax
from jax.experimental import pallas as pl
from jax.experimental.pallas import tpu as pltpu
from jax.sharding import PartitionSpec as P


D = 384
H = 6
FF = 1536
HD = 64
S = 197
SP = 208
SQ = 256
EPS = 1e-06
f32 = jnp.float32
bf16 = jnp.bfloat16
G1, G2, B1, B2, BO, BF2, BQ, BV, BF1 = 0, 384, 768, 1152, 1536, 1920, 2304, 2688, 3072
NV = 4608
VMEM_LIMIT = 60 * 1024 * 1024


def params(**kw):
    return pltpu.CompilerParams(vmem_limit_bytes=VMEM_LIMIT, **kw)


def full(shape):
    return pl.BlockSpec(shape, lambda *_: (0,) * len(shape))


def any_spec():
    return pl.BlockSpec(memory_space=pl.ANY)


def nn(a, b):
    return jnp.dot(a, b, preferred_element_type=f32)


def nt(a, b):
    return lax.dot_general(a, b, (((1,), (1,)), ((), ())), preferred_element_type=f32)


def tr(a):
    return a.astype(f32).T.astype(a.dtype)


def norm_stats(rows):
    mean = jnp.mean(rows, axis=-1, keepdims=True)
    cen = rows - mean
    var = jnp.mean(cen * cen, axis=-1, keepdims=True)
    inv = lax.rsqrt(var + EPS)
    return cen * inv, inv


def pad_rows(ref_val):
    return jnp.concatenate([ref_val, jnp.zeros((SP - S, ref_val.shape[1]), ref_val.dtype)], axis=0)


def stack_rows(ref):
    return jnp.concatenate([pad_rows(ref[k].astype(f32)) for k in range(ref.shape[0])], axis=0)


def head_masks():
    lane = lax.broadcasted_iota(jnp.int32, (SP, 128), 1)
    return lane < HD


def pick(block, first, head):
    zero = jnp.zeros_like(block)
    return jnp.where(first, block, zero) if head == 0 else jnp.where(first, zero, block)


TAIL = S // 8 * 8
HEAD_GROUPS = (tuple(range(H)),)


def mask_tail(z):
    ok = lax.broadcasted_iota(jnp.int32, (SP - TAIL, z.shape[1]), 0) < S - TAIL
    return jnp.concatenate([z[:TAIL], jnp.where(ok, z[TAIL:], -1e30)], axis=0)


def project(x_ref, w, vec, a1_ref, qkv_ref, n1_ref):
    rows = stack_rows(x_ref)
    shape = (x_ref.shape[0], SP)
    n1, _ = norm_stats(rows)
    a1 = (n1 * vec[:, G1 : G1 + D] + vec[:, B1 : B1 + D]).astype(bf16)
    a1_ref[...] = a1.reshape(shape + (D,))
    n1_ref[...] = n1.astype(bf16).reshape(shape + (D,))
    for part, at in ((0, BQ), (1, None), (2, BV)):
        p = nn(a1, w[:, D * part : D * part + D])
        if at is not None:
            p = p + vec[:, at : at + D]
        qkv_ref[:, :, D * part : D * part + D] = p.astype(bf16).reshape(shape + (D,))


def attn_fwd_body(qkv_ref, o_ref, lse_ref):
    q = qkv_ref[0, :, :D]
    k = qkv_ref[0, :, D : 2 * D]
    v = qkv_ref[0, :, 2 * D :]
    first = head_masks()
    for group in HEAD_GROUPS:
        cols = [slice(128 * (h // 2), 128 * (h // 2) + 128) for h in group]
        q2t = [jnp.concatenate([tr(q[:, c] * 0.125), jnp.zeros((128, SQ - SP), bf16)], axis=1) for c in cols[::2]]
        v2t = [tr(v[:, c]) for c in cols[::2]]
        z = [mask_tail(nn(pick(k[:, c], first, h % 2), q2t[at // 2])) for at, (c, h) in enumerate(zip(cols, group))]
        peak = [jnp.max(s, axis=0, keepdims=True) for s in z]
        e = [jnp.exp(s - p) for s, p in zip(z, peak)]
        total = [jnp.sum(s, axis=0, keepdims=True) for s in e]
        pb = [(s * (1.0 / t)).astype(bf16) for s, t in zip(e, total)]
        outs = [nn(v2t[at // 2][HD * (at % 2) : HD * (at % 2) + HD, :], p) for at, p in enumerate(pb)]
        for at, h in enumerate(group):
            lse_ref[0, pl.ds(h, 1), :] = peak[at] + jnp.log(total[at])
        for at in range(0, len(group), 2):
            o_ref[0, :, cols[at]] = jnp.concatenate(outs[at : at + 2], axis=0).T[:SP].astype(bf16)


def cost(flops, nbytes, trans=0):
    return pl.CostEstimate(flops=int(flops), bytes_accessed=int(nbytes), transcendentals=int(trans))


def smem():
    return pl.BlockSpec(memory_space=pltpu.SMEM)


C2 = 1792
CF, CO = 768, 1024


def prep_kernel(core_ref, o_ref, f1_ref, f2_ref, own_ref, send_ref, os_, f1s, f2s):
    rows = own_ref.shape[0]
    core = core_ref[0]
    os_[...] = o_ref[...].astype(f32)
    f1s[...] = f1_ref[...].astype(f32)
    f2s[...] = f2_ref[...].astype(f32)
    sets = []
    for s in range(2):
        parts = []
        for b in range(6):
            parts.append(f1s[pl.ds(6 * s + b, rows, stride=12), :])
        for b in range(2):
            parts.append(os_[pl.ds(s + b, rows, stride=3), :])
        for half in range(2):
            for b in range(3):
                parts.append(f2s[pl.ds(3 * (2 * rows * s + rows * half) + b, rows, stride=3), :])
        sets.append(jnp.concatenate(parts, axis=1))
    own_ref[...] = jnp.where(core == 0, sets[0], sets[1]).astype(bf16)
    send_ref[...] = jnp.where(core == 0, sets[1], sets[0]).astype(bf16)


def prep(core, o, f1, f2):
    rows = o.shape[0] // 3
    shape = jax.ShapeDtypeStruct((rows, C2), bf16)
    vm = pl.BlockSpec(memory_space=pltpu.VMEM)
    return pl.pallas_call(
        prep_kernel, name="prep", in_specs=[smem()] + [vm] * 3, out_specs=[vm] * 2, out_shape=[shape] * 2,
        scratch_shapes=[pltpu.VMEM(v.shape, f32) for v in (o, f1, f2)],
        cost_estimate=cost(1e6, 2e5),
        compiler_params=params(),
    )(core, o, f1, f2)


def piece_rows(per):
    return (9 * per + 2 + 15) // 16 * 16


def piece_kernel(q_ref, g_ref, b_ref, out_ref):
    rows = q_ref.shape[0]
    wide = lambda v: jnp.concatenate([v.astype(f32), jnp.zeros((1, 128 - v.shape[1]), f32)], axis=1)
    rest = jnp.zeros((out_ref.shape[1] - rows - 2, 128), f32)
    piece = jnp.concatenate([q_ref[...].astype(f32), wide(g_ref[...]), wide(b_ref[...]), rest], axis=0).astype(bf16)
    for k in range(out_ref.shape[0]):
        out_ref[k] = piece


def piece(q, g, b, chips):
    vm = pl.BlockSpec(memory_space=pltpu.VMEM)
    return pl.pallas_call(
        piece_kernel, name="piece", in_specs=[vm] * 3, out_specs=vm,
        out_shape=jax.ShapeDtypeStruct((chips, piece_rows(q.shape[0] // 9), 128), bf16),
        compiler_params=params(),
    )(q, g, b)


def merge_kernel(core_ref, own_ref, recv_ref, p2_ref):
    core = core_ref[0]
    own = own_ref[...].astype(f32)
    recv = recv_ref[...].astype(f32)
    top = jnp.where(core == 0, own, recv)
    low = jnp.where(core == 0, recv, own)
    cat = lambda a, b: jnp.concatenate([a, b], axis=0).astype(bf16)
    p2_ref[:, :CO] = cat(top[:, :CO], low[:, :CO])
    for c, v in ((0, top), (1, low)):
        base = CO
        p2_ref[:, CO + D * c : CO + D * c + D] = cat(v[:, base : base + D], v[:, base + D : base + 2 * D])


def merge(core, own, recv):
    vm = pl.BlockSpec(memory_space=pltpu.VMEM)
    return pl.pallas_call(
        merge_kernel, name="merge", in_specs=[smem(), vm, vm], out_specs=vm,
        out_shape=jax.ShapeDtypeStruct((2 * own.shape[0], C2), bf16),
        cost_estimate=cost(1e6, 2e5),
        compiler_params=params(),
    )(core, own, recv)


def k1_kernel(qkv_ref, *rest):
    attn_fwd_body(qkv_ref, *rest[-2:])


def k1(qkv, start, count, prev=()):
    n = qkv.shape[0]
    blk = lambda r, c: pl.BlockSpec((1, r, c), lambda i: (i + start, 0, 0))
    return pl.pallas_call(
        k1_kernel,
        name="k1",
        grid=(count,),
        in_specs=[blk(SP, 3 * D)] + [any_spec()] * len(prev),
        out_specs=[blk(SP, D), blk(8, SQ)],
        out_shape=[jax.ShapeDtypeStruct((n, SP, D), bf16), jax.ShapeDtypeStruct((n, 8, SQ), f32)],
        input_output_aliases={1 + k: k for k in range(len(prev))},
        cost_estimate=cost(count * 1e9, count * 1e6, count * 3e5),
        compiler_params=params(),
    )(qkv, *prev)


def kp_kernel(core_ref, own_ref, recv_ref, x_ref, w_ref, vec_ref, a1_ref, qkv_ref, n1_ref, s_s, w_s):
    core = core_ref[0]
    s_s[core] = own_ref[...].astype(f32)
    s_s[1 - core] = recv_ref[...].astype(f32)
    chips = own_ref.shape[0]
    per = D // (2 * chips)
    ng, nb = D // chips, (NV - 2 * D) // (2 * chips)
    for d in range(2 * chips):
        for b in range(9):
            w_s[per * d : per * d + per, 128 * b : 128 * b + 128] = s_s[d % 2, d // 2, pl.ds(b, per, stride=9), :]
        vec_ref[0:1, ng * d : ng * d + ng] = s_s[d % 2, d // 2, 9 * per : 9 * per + 1, :ng]
        vec_ref[0:1, 2 * D + nb * d : 2 * D + nb * d + nb] = s_s[d % 2, d // 2, 9 * per + 1 : 9 * per + 2, :nb]
    w = w_s[...].astype(bf16)
    w_ref[...] = w
    project(x_ref, w, vec_ref[...], a1_ref, qkv_ref, n1_ref)


def kp(core, own, recv, x):
    n = x.shape[0]
    vm = pl.BlockSpec(memory_space=pltpu.VMEM)
    return pl.pallas_call(
        kp_kernel, name="kp", in_specs=[smem()] + [vm] * 3, out_specs=[vm] * 5,
        out_shape=[jax.ShapeDtypeStruct((D, 3 * D), bf16), jax.ShapeDtypeStruct((1, NV), f32)]
        + [jax.ShapeDtypeStruct((n, SP, c), bf16) for c in (D, 3 * D, D)],
        scratch_shapes=[pltpu.VMEM((2,) + own.shape, f32), pltpu.VMEM((D, 3 * D), f32)],
        cost_estimate=cost(n * 4e8, n * 2e6),
        compiler_params=params(),
    )(core, own, recv, x)


CH = 768


def gelu_parts(u):
    cum = 0.5 * (1.0 + lax.erf(u * (1.0 / math.sqrt(2.0))))
    den = jnp.exp(-0.5 * u * u) * (1.0 / math.sqrt(2.0 * math.pi))
    return u * cum, cum + u * den


def k2_kernel(core_ref, live_ref, x_ref, g_ref, o_ref, owna_ref, ownb_ref, recva_ref, recvb_ref, vec_ref,
              out_ref, dr_ref, do_ref, keep_ref, send_ref, sums_ref,
              a2_s, du_s, gl_s, eb_s, drb_s, w1_ref, w2_ref, wo_ref, *, pieces, cap):
    core = core_ref[0]
    unit = D // pieces
    vec = vec_ref[...]
    group = x_ref.shape[0]
    height = group * SP
    flags = []
    for k in range(group):
        flag = (k % cap < live_ref[k // cap]).astype(f32)
        flags.append(jnp.full((SP, 1), 1.0, f32) * flag)
    live = jnp.concatenate(flags, axis=0)

    sums_ref[...] = jnp.zeros_like(sums_ref)
    own = jnp.concatenate([owna_ref[...], ownb_ref[...]], axis=1)
    recv = jnp.concatenate([recva_ref[...], recvb_ref[...]], axis=1)
    sets = (jnp.where(core == 0, own, recv), jnp.where(core == 0, recv, own))
    blocks = []
    for s in range(2):
        w1_ref[:, CF * s : CF * s + CF] = sets[s][:, :CF]
        blocks.append(sets[s][:, CO:].astype(f32))
    wo_ref[:, :256] = sets[0][:, CF:CO]
    wo_ref[:, 256:] = sets[1][:, CF + 128 : CO]
    for p in range(pieces):
        quad = []
        for c in range(2):
            for s in range(2):
                quad.append(blocks[s][unit * p : unit * p + unit, D * c : D * c + D])
        w2_ref[4 * unit * p : 4 * unit * p + 4 * unit, :] = jnp.concatenate(quad, axis=0).astype(bf16)

    res = stack_rows(x_ref) + nn(o_ref[...].reshape(height, D), wo_ref[...]) + vec[:, BO : BO + D]
    n2, r2 = norm_stats(res)
    a2 = (n2 * vec[:, G2 : G2 + D] + vec[:, B2 : B2 + D]).astype(bf16)
    a2_s[...] = a2
    e = stack_rows(g_ref) * live
    eb = e.astype(bf16)
    eb_s[...] = eb
    acc = res + vec[:, BF2 : BF2 + D]
    dn = jnp.zeros((height, D), f32)
    for c in range(FF // CH):
        cs = slice(CH * c, CH * c + CH)
        u = nn(a2, w1_ref[:, cs]) + vec[:, BF1 + CH * c : BF1 + CH * c + CH]
        dg = nt(eb, w2_ref[cs, :])
        gel, slope = gelu_parts(u)
        gb = gel.astype(bf16)
        du = (dg * slope).astype(bf16)
        gl_s[:, cs] = gb
        du_s[:, cs] = du
        acc = acc + nn(gb, w2_ref[cs, :])
        dn = dn + nt(du, w1_ref[:, cs])
    acc = acc * live
    for k in range(group):
        out_ref[k] = acc[SP * k : SP * k + S]
    t = dn * vec[:, G2 : G2 + D]
    dr = e + r2 * (
        t - jnp.mean(t, axis=-1, keepdims=True) - n2 * jnp.mean(t * n2, axis=-1, keepdims=True)
    )
    dr_ref[...] = dr.reshape(group, SP, D)
    drb = dr.astype(bf16)
    drb_s[...] = drb
    do_ref[...] = nt(drb, wo_ref[...]).astype(bf16).reshape(group, SP, D)
    sums_ref[0:1, G2 : G2 + D] += jnp.sum(dn * n2, axis=0, keepdims=True)
    sums_ref[0:1, B2 : B2 + D] += jnp.sum(dn, axis=0, keepdims=True)

    ones = jnp.ones((8, a2_s.shape[0]), bf16)
    eball = eb_s[...]
    drball = drb_s[...]
    a2t = tr(a2_s[...])
    ebt = tr(eball)
    g2 = nn(ebt, gl_s[...]).T.reshape(pieces, 4, unit, D)
    go = nn(tr(o_ref[...].reshape(-1, D)), drball).astype(bf16)

    def put(ref, s):
        ref[:, :CF] = nn(a2t, du_s[:, CF * s : CF * s + CF]).astype(bf16)
        ref[:, CF:CO] = go[:, 128 * s : 128 * s + 256]
        for c in range(2):
            ref[:, CO + D * c : CO + D * c + D] = g2[:, 2 * c + s].reshape(D, D).astype(bf16)

    @pl.when(core == 0)
    def _():
        put(keep_ref, 0)
        put(send_ref, 1)

    @pl.when(core != 0)
    def _():
        put(keep_ref, 1)
        put(send_ref, 0)

    sums_ref[:, BF1 : BF1 + FF] = nn(ones, du_s[...])
    sums_ref[:, BF2 : BF2 + D] = nn(ones, eball)
    sums_ref[:, BO : BO + D] = nn(ones, drball)


def k2(core, counts, x, g, o, own, recv, vec, pieces, cap):
    n = x.shape[0]
    vm = pl.BlockSpec(memory_space=pltpu.VMEM)
    return pl.pallas_call(
        functools.partial(k2_kernel, pieces=pieces, cap=cap),
        name="k2",
        in_specs=[smem(), smem()] + [vm] * 8,
        out_specs=[vm] * 6,
        out_shape=[
            jax.ShapeDtypeStruct((n, S, D), f32),
            jax.ShapeDtypeStruct((n, SP, D), f32),
            jax.ShapeDtypeStruct((n, SP, D), bf16),
            jax.ShapeDtypeStruct((D, C2), bf16),
            jax.ShapeDtypeStruct((D, C2), bf16),
            jax.ShapeDtypeStruct((8, NV), f32),
        ],
        scratch_shapes=[
            pltpu.VMEM((n * SP, D), bf16),
            pltpu.VMEM((n * SP, FF), bf16),
            pltpu.VMEM((n * SP, FF), bf16),
            pltpu.VMEM((n * SP, D), bf16),
            pltpu.VMEM((n * SP, D), bf16),
            pltpu.VMEM((D, FF), bf16),
            pltpu.VMEM((FF, D), bf16),
            pltpu.VMEM((D, D), bf16),
        ],
        cost_estimate=cost(n * 2e9, n * 4e6, n * 6e5),
        compiler_params=params(),
    )(core, counts, x, g, o, *own, *recv, vec)


def k3_kernel(qkv_ref, lse_ref, do_ref, *rest):
    dp_ref = rest[-1]
    do = do_ref[0]
    first = head_masks()
    lanes0 = jnp.zeros((128, SQ - SP), bf16)
    rows0 = jnp.zeros((SQ - SP, 128), bf16)
    for group in HEAD_GROUPS:
        cols = [128 * (h // 2) for h in group[::2]]
        q2 = [qkv_ref[0, :, c : c + 128] for c in cols]
        k2_ = [qkv_ref[0, :, D + c : D + c + 128] for c in cols]
        v2 = [qkv_ref[0, :, 2 * D + c : 2 * D + c + 128] for c in cols]
        do2 = [do[:, c : c + 128] for c in cols]
        q2t = [jnp.concatenate([tr(a * 0.125), lanes0], axis=1) for a in q2]
        do2t = [jnp.concatenate([tr(a), lanes0], axis=1) for a in do2]
        k2t = [tr(a) for a in k2_]
        own = [(at // 2, h % 2, h) for at, h in enumerate(group)]
        z = [mask_tail(nn(pick(k2_[a], first, b), q2t[a])) for a, b, _ in own]
        dpr = [nn(pick(v2[a], first, b), do2t[a]) for a, b, _ in own]
        p = [jnp.exp(s - lse_ref[0, pl.ds(h, 1), :]) for s, (_, _, h) in zip(z, own)]
        dot_row = [jnp.sum(s * t, axis=0, keepdims=True) for s, t in zip(p, dpr)]
        dz = [(s * (t - r)).astype(bf16) for s, t, r in zip(p, dpr, dot_row)]
        dv = [nn(s.astype(bf16), jnp.concatenate([pick(do2[a], first, b), rows0], axis=0)) for s, (a, b, _) in zip(p, own)]
        dk = [nn(s, jnp.concatenate([pick(q2[a], first, b), rows0], axis=0)) for s, (a, b, _) in zip(dz, own)]
        dq = [nn(k2t[a][HD * b : HD * b + HD, :], s) for s, (a, b, _) in zip(dz, own)]
        for a, c in enumerate(cols):
            two = slice(2 * a, 2 * a + 2)
            dp_ref[0, :, c : c + 128] = (jnp.concatenate(dq[two], axis=0).T[:SP] * 0.125).astype(bf16)
            dp_ref[0, :, D + c : D + c + 128] = ((dk[2 * a] + dk[2 * a + 1]) * 0.125).astype(bf16)
            dp_ref[0, :, 2 * D + c : 2 * D + c + 128] = (dv[2 * a] + dv[2 * a + 1]).astype(bf16)


def k3(qkv, lse, do, start, count, prev=()):
    n = qkv.shape[0]
    blk = lambda r, c: pl.BlockSpec((1, r, c), lambda i: (i + start, 0, 0))
    return pl.pallas_call(
        k3_kernel,
        name="k3",
        grid=(count,),
        in_specs=[blk(SP, 3 * D), blk(8, SQ), blk(SP, D)] + [any_spec()] * len(prev),
        out_specs=blk(SP, 3 * D),
        out_shape=jax.ShapeDtypeStruct((n, SP, 3 * D), bf16),
        input_output_aliases={3 + k: k for k in range(len(prev))},
        cost_estimate=cost(count * 1.2e9, count * 2e6, count * 3e5),
        compiler_params=params(),
    )(qkv, lse, do, *prev)


def k5_kernel(x_ref, dr_ref, dp_ref, w_ref, vec_ref, dx_ref):
    dn = nt(dp_ref[0], w_ref[...])
    n1, r1 = norm_stats(x_ref[0].astype(f32))
    t = dn[:S] * vec_ref[:, G1 : G1 + D]
    dx_ref[0] = dr_ref[0, :S, :] + r1 * (
        t - jnp.mean(t, axis=-1, keepdims=True) - n1 * jnp.mean(t * n1, axis=-1, keepdims=True)
    )


def k5(x, dr, dp, w, vec):
    n = x.shape[0]
    blk = lambda r, c: pl.BlockSpec((1, r, c), lambda i: (i, 0, 0))
    return pl.pallas_call(
        k5_kernel,
        name="k5",
        grid=(n,),
        in_specs=[blk(S, D), blk(SP, D), blk(SP, 3 * D), full((D, 3 * D)), full((1, NV))],
        out_specs=blk(S, D),
        out_shape=jax.ShapeDtypeStruct((n, S, D), f32),
        cost_estimate=cost(n * 2e8, n * 2e6),
        compiler_params=params(),
    )(x, dr, dp, w, vec)


def k4_kernel(core_ref, a1_ref, n1_ref, dp_ref, w_ref, sums2_ref, keep_ref, send_ref, v_s, q_s, t_s):
    core = core_ref[0]
    dpall = dp_ref[...].reshape(-1, 3 * D)
    q_s[...] = nn(tr(a1_ref[...].reshape(-1, D)), dpall)
    bsum = nn(jnp.ones((8, dpall.shape[0]), bf16), dpall)
    weight = w_ref[...].astype(f32)
    gain = jnp.sum(weight * nn(tr(n1_ref[...].reshape(-1, D)), dpall), axis=1, keepdims=True)
    shift = jnp.sum(weight * bsum[0:1, :], axis=1, keepdims=True)
    lane = lax.broadcasted_iota(jnp.int32, (D, 128), 1)
    both = jnp.where(lane == 0, gain, shift).T
    v_s[...] = sums2_ref[0:1, :]
    v_s[:, G1 : G1 + D] = both[0:1, :]
    v_s[:, B1 : B1 + D] = both[1:2, :]
    v_s[:, BQ : BQ + D] = bsum[0:1, :D]
    v_s[:, BV : BV + D] = bsum[0:1, 2 * D :]
    chips = keep_ref.shape[0]
    per = D // (2 * chips)
    ng, nb = D // chips, (NV - 2 * D) // (2 * chips)
    tail = 9 * per // 8 * 8
    t_s[:, :, tail:, :] = jnp.zeros((2, chips, t_s.shape[2] - tail, 128), f32)
    for d in range(2 * chips):
        for b in range(9):
            t_s[d % 2, d // 2, pl.ds(b, per, stride=9), :] = q_s[per * d : per * d + per, 128 * b : 128 * b + 128]
        t_s[d % 2, d // 2, 9 * per : 9 * per + 1, :ng] = v_s[:, ng * d : ng * d + ng]
        t_s[d % 2, d // 2, 9 * per + 1 : 9 * per + 2, :nb] = v_s[:, 2 * D + nb * d : 2 * D + nb * d + nb]
    keep_ref[...] = t_s[core].astype(bf16)
    send_ref[...] = t_s[1 - core].astype(bf16)


def k4(core, a1, n1, dp, w, sums2, chips):
    vm = pl.BlockSpec(memory_space=pltpu.VMEM)
    rows = piece_rows(D // (2 * chips))
    shape = jax.ShapeDtypeStruct((chips, rows, 128), bf16)
    return pl.pallas_call(
        k4_kernel, name="k4",
        in_specs=[smem()] + [vm] * 5, out_specs=[vm] * 2, out_shape=[shape] * 2,
        scratch_shapes=[pltpu.VMEM((1, NV), f32), pltpu.VMEM((D, 3 * D), f32), pltpu.VMEM((2, chips, rows, 128), f32)],
        cost_estimate=cost(1e9, 4e6),
        compiler_params=params(),
    )(core, a1, n1, dp, w, sums2)


def last_kernel(core_ref, own_ref, recv_ref, o_ref, f1_ref, f2_ref):
    core = core_ref[0]
    rows = own_ref.shape[0] // 2

    def mine(v):
        return jnp.where(core == 0, v[:rows], v[rows:])

    own = own_ref[...].astype(f32)
    recv = recv_ref[...].astype(f32)
    pair = (jnp.where(core == 0, own, recv), jnp.where(core == 0, recv, own))
    top = [mine(v[:, :CO]) for v in pair]
    for col in range(12):
        f1_ref[pl.ds(col, rows, stride=12), :] = top[col // 6][:, 128 * (col % 6) : 128 * (col % 6) + 128]
    for col in range(3):
        s, k = (0, col) if col < 2 else (1, 1)
        o_ref[pl.ds(col, rows, stride=3), :] = top[s][:, CF + 128 * k : CF + 128 * k + 128]
    for s in range(2):
        v = pair[s]
        blk = jnp.where(core == 0, v[:, CO : CO + D], v[:, CO + D :])
        for col in range(3):
            f2_ref[pl.ds(3 * 2 * rows * s + col, 2 * rows, stride=3), :] = blk[:, 128 * col : 128 * col + 128]


def last(core, own, recv):
    rows = own.shape[0] // 2
    vm = pl.BlockSpec(memory_space=pltpu.VMEM)
    return pl.pallas_call(
        last_kernel, name="last", in_specs=[smem()] + [vm] * 2, out_specs=[vm] * 3,
        out_shape=[jax.ShapeDtypeStruct((k * rows, 128), f32) for k in (3, 12, 12)],
        cost_estimate=cost(1e6, 4e5),
        compiler_params=params(),
    )(core, own, recv)


def swap(v, bit, n):
    return lax.ppermute(v, "fsdp", [(i, i ^ (1 << bit)) for i in range(n)])


def exchange(v, n):
    return lax.all_to_all(v, "fsdp", 0, 0, axis_index_groups=chip_groups(n))


def side(me, bit):
    return (me >> bit) & 1


def join(own, recv, axis, flag):
    low = jnp.stack([own, recv], axis)
    high = jnp.stack([recv, own], axis)
    return jnp.where(flag == 0, low, high)


def split(arr, axis, flag):
    a = lax.index_in_dim(arr, 0, axis, keepdims=False)
    b = lax.index_in_dim(arr, 1, axis, keepdims=False)
    return jnp.where(flag == 0, a, b), jnp.where(flag == 0, b, a)


def add(keep, recv):
    return (keep.astype(f32) + recv.astype(f32)).astype(bf16)


ORDERS = ((1, 2), (2, 1))


def halves_of(arr):
    cut = (arr.shape[-1] // 2) // 128 * 128
    return [arr[..., :cut], arr[..., cut:]]


def gather_chips(piece, me, n):
    top = n.bit_length() - 2
    arr = piece
    for k, bit in enumerate(range(top, 2, -1)):
        recv = swap(arr, bit, n)
        arr = join(arr, recv, k, side(me, bit))
    ax = top - 2
    chunks = halves_of(arr)
    for stage in range(2):
        got = [swap(c, o[stage], n) for c, o in zip(chunks, ORDERS)]
        chunks = [
            join(c, r, ax + 1 if (stage == 1 and o[stage] == 1) else ax, side(me, o[stage]))
            for c, r, o in zip(chunks, got, ORDERS)
        ]
    return [c.reshape(D, -1) for c in chunks]


def scatter_chips(arr, me, n):
    top = n.bit_length() - 2
    arr = arr.reshape((2,) * top + (2 * D // n, arr.shape[1]))
    chunks = halves_of(arr)
    for stage in range(2):
        pairs = [
            split(c, top - 1 if (stage == 0 and o[stage] == 1) else top - 2, side(me, o[stage]))
            for c, o in zip(chunks, ORDERS)
        ]
        got = [swap(p[1], o[stage], n) for p, o in zip(pairs, ORDERS)]
        chunks = [add(p[0], r) for p, r in zip(pairs, got)]
    arr = jnp.concatenate(chunks, axis=-1)
    for bit in range(top, 2, -1):
        keep, send = split(arr, 0, side(me, bit))
        arr = add(keep, swap(send, bit, n))
    return arr


def local_chips(n, images, counts, out_grad, qkv_weight, out_weight, fc1_weight, fc2_weight, norm_gains, biases):
    me = lax.axis_index("fsdp")
    core = (me & 1).astype(jnp.int32).reshape(1)
    chips = n // 2
    mb, cap = images.shape[:2]
    ni = mb * cap
    x = by_image(images)
    g = by_image(out_grad)
    lanes = lambda v: v.reshape(-1, 128)
    own, send = prep(core, lanes(out_weight), lanes(fc1_weight), lanes(fc2_weight))
    first = piece(lanes(qkv_weight), norm_gains.reshape(1, -1), biases.reshape(1, -1), chips)
    q_own = exchange(first, n)
    q_recv = swap(q_own, 0, n)
    p2 = merge(core, own, swap(send, 0, n))
    f_own = gather_chips(p2, me, n)
    f_recv = [swap(f, 0, n) for f in f_own]
    w, vec, a1, qkv, n1 = kp(core, q_own, q_recv, x)
    o, lse = k1(qkv, 0, ni)
    counts = lax.optimization_barrier(counts.reshape(-1) + 0)
    out, dr, do, keep2, send2, sums2 = k2(core, counts, x, g, o, f_own, f_recv, vec, chips, cap)
    sum2 = scatter_chips(add(keep2, swap(send2, 0, n)), me, n)
    half = ni // 2
    dp = ()
    for part in range(2):
        dp = (k3(qkv, lse, do, half * part, half, dp),)
    keep1, send1 = k4(core, a1, n1, dp[0], w, sums2, chips)
    sum1 = add(keep1, swap(send1, 0, n))
    g_qkv, g_gain, g_bias = total(exchange(sum1, n))
    dx = k5(x, dr, dp[0], w, vec)
    g_out, g_fc1, g_fc2 = last(core, sum2, swap(sum2, 0, n))
    grads = (g_qkv, g_out, g_fc1, g_fc2, g_gain, g_bias)
    out = by_slot(out, images.shape)
    dx = by_slot(dx, images.shape)
    return (out, dx) + tuple(v.reshape(-1) for v in grads)


def by_image(v):
    mb, cap = v.shape[:2]
    tokens = lax.optimization_barrier(v.transpose(0, 2, 1, 3))
    return tokens.transpose(0, 2, 1, 3).reshape(mb * cap, S, D)


def by_slot(v, shape):
    tokens = lax.optimization_barrier(v.reshape(shape).transpose(0, 2, 1, 3))
    return tokens.transpose(0, 2, 1, 3)


def local_named(n, *args):
    return local_chips(n, *args)


def total_kernel(x_ref, q_ref, g_ref, b_ref):
    acc = x_ref[0].astype(f32)
    for k in range(1, x_ref.shape[0]):
        acc = acc + x_ref[k].astype(f32)
    rows = q_ref.shape[0]
    q_ref[...] = acc[:rows]
    g_ref[...] = acc[rows : rows + 1, : g_ref.shape[1]]
    b_ref[...] = acc[rows + 1 : rows + 2, : b_ref.shape[1]]


def total(x):
    vm = pl.BlockSpec(memory_space=pltpu.VMEM)
    n = 2 * x.shape[0]
    shapes = [(9 * D // n, 128), (1, 2 * D // n), (1, (NV - 2 * D) // n)]
    return pl.pallas_call(
        total_kernel, name="total", in_specs=[vm], out_specs=[vm] * 3,
        out_shape=[jax.ShapeDtypeStruct(s, f32) for s in shapes],
        compiler_params=params(),
    )(x)


def chip_groups(n):
    return [[i for i in range(n) if i % 2 == c] for c in range(2)]


def local_any(images, counts, out_grad, qkv_weight, out_weight, fc1_weight, fc2_weight, norm_gains, biases):
    ag = lambda v: lax.all_gather(v, "fsdp", axis=0, tiled=True)
    pieces = 16
    unit = D // pieces
    zero = jnp.zeros((1,), jnp.int32)
    parts = 2 * pieces
    per = D // parts
    rows = piece_rows(per)
    wide = lambda v: jnp.pad(v.reshape(parts, 1, -1), ((0, 0), (0, 0), (0, 128 - v.shape[0] // parts)))
    flat = jnp.concatenate([ag(qkv_weight).reshape(parts, 9 * per, 128), wide(ag(norm_gains)), wide(ag(biases))], axis=1)
    flat = jnp.pad(flat, ((0, 0), (0, rows - 9 * per - 2), (0, 0)))
    wo_in = ag(out_weight).reshape(D, D)
    w1 = ag(fc1_weight).reshape(D, FF)
    w2 = ag(fc2_weight).reshape(pieces, 2, 2, unit, D)
    sets = [
        jnp.concatenate([w1[:, CF * s : CF * s + CF], wo_in[:, 128 * s : 128 * s + 256],
                         w2[:, 0, s].reshape(D, D), w2[:, 1, s].reshape(D, D)], axis=1)
        for s in range(2)
    ]
    mb, cap = images.shape[:2]
    ni = mb * cap
    x = images.reshape(ni, S, D)
    g = out_grad.reshape(ni, S, D)
    w, vec, a1, qkv, n1 = kp(zero, flat[0::2], flat[1::2], x)
    o, lse = k1(qkv, 0, ni)
    out, dr, do, set0, set1, sums2 = k2(zero, counts.reshape(-1), x, g, o, halves_of(sets[0]), halves_of(sets[1]), vec, pieces, cap)
    dp = k3(qkv, lse, do, 0, ni)
    dx = k5(x, dr, dp, w, vec)
    q0, q1 = k4(zero, a1, n1, dp, w, sums2, pieces)
    q01 = jnp.stack([q0, q1], 1).reshape(parts, rows, 128)
    g_qkv = q01[:, : 9 * per]
    g_gain = q01[:, 9 * per, : 2 * D // parts]
    g_bias = q01[:, 9 * per + 1, : (NV - 2 * D) // parts]
    g_out = jnp.concatenate([set0[:, CF:CO], set1[:, CF + 128 : CO]], axis=1)
    g_fc1 = jnp.concatenate([set0[:, :CF], set1[:, :CF]], axis=1)
    f2 = [jnp.stack([s[:, CO : CO + D].reshape(pieces, unit, D), s[:, CO + D :].reshape(pieces, unit, D)], 1) for s in (set0, set1)]
    g_fc2 = jnp.stack(f2, 2).reshape(FF, D)
    rs = lambda v: lax.psum_scatter(v.reshape(-1).astype(f32), "fsdp", scatter_dimension=0, tiled=True)
    return (out.reshape(images.shape), dx.reshape(images.shape)) + tuple(
        rs(v) for v in (g_qkv, g_out, g_fc1, g_fc2, g_gain, g_bias)
    )


def solution(mesh):
    n = mesh.shape["fsdp"]
    placed = (
        P(None, "fsdp", None, None),
        P(None, "fsdp"),
        P(None, "fsdp", None, None),
    ) + (P("fsdp"),) * 6
    chips = n >= 8 and n & (n - 1) == 0 and D % n == 0 and (2 * D // n) % 8 == 0
    return jax.shard_map(
        functools.partial(local_named, n) if chips else local_any,
        mesh=mesh,
        in_specs=placed,
        out_specs=(placed[0], placed[2]) + (P("fsdp"),) * 6,
        check_vma=False,
    )
```

time: 157 us -> 143 us (0.911)
  Pallas kernels: 68.1 us -> 54.1 us
  local copies, waits for them, and re-layouts: 8.78 us -> 10.9 us
    pallas_call x4 -> x2, Pallas kernels: 16.5 us -> 8.36 us  [k3(): pl.pallas_call(k3_kernel, name='k3', grid=(count,), in_specs=[blk(SP, 3 *...]
    pallas_call x7, Pallas kernels: 27 us -> 23.2 us  [the longest x1 6.19 us: k4(): pl.pallas_call(k4_kernel, name='k4', in_specs=[smem()] + [vm] * 5, out_sp...]
    pallas_call x1, Pallas kernels: 17.3 us -> 15.5 us  [k2(): pl.pallas_call(functools.partial(k2_kernel, pieces=pieces, cap=cap), name...]
    unnamed x33 -> x32, local copies, waits for them, and re-layouts: 3.33 us -> 4.18 us
    ppermute x20 -> x19, waiting for transfers between devices: 46.1 us -> 45.8 us  [swap(): return lax.ppermute(v, 'fsdp', [(i, i ^ 1 << bit) for i in range(n)])]
    ppermute x20 -> x19, starting transfers between devices: 18.8 us -> 18.8 us  [swap(): return lax.ppermute(v, 'fsdp', [(i, i ^ 1 << bit) for i in range(n)])]
  transfers between devices with their start and end apart: 22 -> 21, of which waited for: 14 -> 12; matrix products, arithmetic and copies ran while one was open for 6% -> 7% of each run, Pallas kernels for 29% -> 24%
where the time goes in v3:
time: 143 us; the launch traced here: 142 us
  Pallas kernels  54.1 us (38%)
  waiting for transfers between devices  45.8 us (32%)
  starting transfers between devices  27.3 us (19%)
  local copies, waits for them, and re-layouts  10.9 us (8%)
  other arithmetic  2.47 us (2%)
    ppermute x19, waiting for transfers between devices, swap(): return lax.ppermute(v, 'fsdp', [(i, i ^ 1 << bit) for i in range(n)])  45.8 us
    ppermute x19, starting transfers between devices, swap(): return lax.ppermute(v, 'fsdp', [(i, i ^ 1 << bit) for i in range(n)])  18.8 us
    pallas_call x1, Pallas kernels, k2(): pl.pallas_call(functools.partial(k2_kernel, pieces=pieces, cap=cap), name...  15.5 us
    all_to_all x2, starting transfers between devices, exchange(): return lax.all_to_all(v, 'fsdp', 0, 0, axis_index_groups=chip_groups(n))  8.56 us
    pallas_call x2, Pallas kernels, k3(): pl.pallas_call(k3_kernel, name='k3', grid=(count,), in_specs=[blk(SP, 3 *...  8.36 us
    pallas_call x1, Pallas kernels, k4(): pl.pallas_call(k4_kernel, name='k4', in_specs=[smem()] + [vm] * 5, out_sp...  6.19 us
    pallas_call x1, Pallas kernels, k1(): pl.pallas_call(k1_kernel, name='k1', grid=(count,), in_specs=[blk(SP, 3 *...  5.5 us
    pallas_call x1, Pallas kernels, k5(): pl.pallas_call(k5_kernel, name='k5', grid=(n,), in_specs=[blk(S, D), blk(...  5.44 us
  transfers between devices with their start and end apart: 21, of which 12 were waited for; matrix products, arithmetic and copies ran while one was open for 7% of the time, Pallas kernels for 24%

profile of v3, /device:TPU:0, one launch (start us, length us, event | category | flops | bytes accessed | tf_op | source)
XLA Modules:
  0.0 141.6 jit_solution(6434800157968116739)
XLA Ops:
  0.6 1.5 %prep.1 = (bf16[12,1792]{1,0:T(8,128)(2,1)}, bf16[12,1792]{1,0:T(8,128)(2,1)}) custom-call(s32[1]{0:T(128)} %bitcast.core_ref, bf16[36,128]{1,0:T(8,128)(2,1)} %bitcast.108, bf16[144,128]{1,0:T(8,128)(2,1)} %bitcast.105, bf16[144,128]{1,0:T(8,128)(2,1)} %bitcast.106), custom_call_target="tpu_custom_call" | custom-call | flops 1000000 | bytes 200000 | tf_op jit(solution)/shard_map/prep/pallas_call | solution.py:158
  2.1 0.5 collective-permute-start.1
  2.6 1.1 collective-permute-done.1.recv_ref
  3.7 0.6 copy-done.12
  4.3 1.5 %merge.1 = bf16[24,1792]{1,0:T(8,128)(2,1)} custom-call(s32[1]{0:T(128)} %bitcast.core_ref, bf16[12,1792]{1,0:T(8,128)(2,1)} %get-tuple-element.33.own_ref, bf16[12,1792]{1,0:T(8,128)(2,1)} %copy-done.12), custom_call_target="tpu_custom_call" | custom-call | flops 1000000 | bytes 200000 | tf_op jit(solution)/shard_map/merge/pallas_call | solution.py:203
  5.8 3.9 %collective-permute-start.2 = (bf16[24,1792]{1,0:T(8,128)(2,1)}, bf16[24,1792]{1,0:T(8,128)(2,1)S(1)}, u32[]{:S(2)}, u32[]{:S(2)}) collective-permute-start(bf16[24,1792]{1,0:T(8,128)(2,1)} %merge.1), channel_id=1, source_target_pairs={{0,16},{1,17},{2,18},{3,19},{4,20},{5,21},{6,22},{7,23},{8,24},{9,... | collective-permute-start | bytes 258056 | tf_op jit(solution)/shard_map/ppermute | solution.py:543
  9.8 1.6 %piece.1 = bf16[16,112,128]{2,1,0:T(8,128)(2,1)} custom-call(bf16[108,128]{1,0:T(8,128)(2,1)} %bitcast.107, bf16[1,24]{1,0:T(2,128)(2,1)} %bitcast.109, bf16[1,120]{1,0:T(2,128)(2,1)} %bitcast.110), custom_call_target="tpu_custom_call" | custom-call | tf_op jit(solution)/shard_map/piece/pallas_call | solution.py:181
  11.4 4.8 %all-to-all-start = ((bf16[16,112,128]{2,1,0:T(8,128)(2,1)}), bf16[16,112,128]{2,1,0:T(8,128)(2,1)S(1)}, u32[]{:S(2)}, u32[]{:S(2)}) async-start(bf16[16,112,128]{2,1,0:T(8,128)(2,1)} %piece.1), calls=%async_computation | async-start | bytes 917504 | tf_op jit(solution)/shard_map/all_to_all | solution.py:547
  16.3 2.0 %collective-permute-start.3 = (bf16[2,24,1792]{2,1,0:T(8,128)(2,1)S(1)}, bf16[2,24,1792]{2,1,0:T(8,128)(2,1)S(1)}, u32[]{:S(2)}, u32[]{:S(2)}) collective-permute-start(bf16[2,24,1792]{2,1,0:T(8,128)(2,1)S(1)} %maximum_select_fusion.8), channel_id=1, source_target_pairs={{0,8},{1,9},{2,10},{3,11},{4,12},{5,13},{6,14},{7,15},{8,0},{9,1},... | collective-permute-start | bytes 516104 | tf_op jit(solution)/shard_map/ppermute | solution.py:543
  18.3 11.3 %collective-permute-done.3 = bf16[2,24,1792]{2,1,0:T(8,128)(2,1)S(1)} collective-permute-done((bf16[2,24,1792]{2,1,0:T(8,128)(2,1)S(1)}, bf16[2,24,1792]{2,1,0:T(8,128)(2,1)S(1)}, u32[]{:S(2)}, u32[]{:S(2)}) %collective-permute-start.3) | collective-permute-done | bytes 172064 | tf_op jit(solution)/shard_map/ppermute | solution.py:543
  29.7 1.5 %collective-permute-start.4 = (bf16[2,2,24,896]{3,2,0,1:T(8,128)(2,1)S(1)}, bf16[2,2,24,896]{3,2,0,1:T(8,128)(2,1)S(1)}, u32[]{:S(2)}, u32[]{:S(2)}) collective-permute-start(bf16[2,2,24,896]{3,2,0,1:T(8,128)(2,1)S(1)} %get-tuple-element.63), channel_id=1, source_target_pairs={{0,2},{1,3},{2,0},{3,1},{4,6},{5,7},{6,4},{7,5},{8,10},{9,11},{10,... | collective-permute-start | bytes 516104 | tf_op jit(solution)/shard_map/ppermute | solution.py:543
  31.2 1.5 %collective-permute-start.6 = (bf16[2,2,24,896]{3,2,0,1:T(8,128)(2,1)S(1)}, bf16[2,2,24,896]{3,2,0,1:T(8,128)(2,1)S(1)}, u32[]{:S(2)}, u32[]{:S(2)}) collective-permute-start(bf16[2,2,24,896]{3,2,0,1:T(8,128)(2,1)S(1)} %get-tuple-element.62), channel_id=1, source_target_pairs={{0,4},{1,5},{2,6},{3,7},{4,0},{5,1},{6,2},{7,3},{8,12},{9,13},{10,... | collective-permute-start | bytes 516104 | tf_op jit(solution)/shard_map/ppermute | solution.py:543
  32.7 2.5 %collective-permute-done.4 = bf16[2,2,24,896]{3,2,0,1:T(8,128)(2,1)S(1)} collective-permute-done((bf16[2,2,24,896]{3,2,0,1:T(8,128)(2,1)S(1)}, bf16[2,2,24,896]{3,2,0,1:T(8,128)(2,1)S(1)}, u32[]{:S(2)}, u32[]{:S(2)}) %collective-permute-start.4) | collective-permute-done | bytes 172064 | tf_op jit(solution)/shard_map/ppermute | solution.py:543
  35.2 1.5 %collective-permute-start.5 = (bf16[2,2,2,24,896]{4,3,0,1,2:T(8,128)(2,1)S(1)}, bf16[2,2,2,24,896]{4,3,0,1,2:T(8,128)(2,1)S(1)}, u32[]{:S(2)}, u32[]{:S(2)}) collective-permute-start(bf16[2,2,2,24,896]{4,3,0,1,2:T(8,128)(2,1)S(1)} %maximum_select_fusion.4), channel_id=1, source_target_pairs={{0,4},{1,5},{2,6},{3,7},{4,0},{5,1},{6,2},{7,3},{8,12},{9,13},{10,... | collective-permute-start | bytes 1032200 | tf_op jit(solution)/shard_map/ppermute | solution.py:543
  36.8 1.1 collective-permute-done.6
  37.9 0.4 collective-permute-start.7
  38.6 5.4 %collective-permute-done.5 = bf16[2,2,2,24,896]{4,3,0,1,2:T(8,128)(2,1)S(1)} collective-permute-done((bf16[2,2,2,24,896]{4,3,0,1,2:T(8,128)(2,1)S(1)}, bf16[2,2,2,24,896]{4,3,0,1,2:T(8,128)(2,1)S(1)}, u32[]{:S(2)}, u32[]{:S(2)}) %collective-permute-start.5) | collective-permute-done | bytes 344096 | tf_op jit(solution)/shard_map/ppermute | solution.py:543
  44.2 1.0 collective-permute-done.7
  45.6 0.5 collective-permute-start.8
  46.3 0.9 copy.28
  47.3 0.9 copy.29
  48.2 0.8 copy-done.15
  49.0 5.2 %kp.1 = (bf16[384,1152]{1,0:T(8,128)(2,1)}, f32[1,4608]{1,0:T(1,128)}, bf16[4,208,384]{2,1,0:T(8,128)(2,1)}, bf16[4,208,1152]{2,1,0:T(8,128)(2,1)}, bf16[4,208,384]{2,1,0:T(8,128)(2,1)}) custom-call(s32[1]{0:T(128)} %bitcast.core_ref, bf16[16,112,128]{2,1,0:T(8,128)(2,1)} %copy-done.8, bf16[16,112,128]{2,1,0:T(8,128)(2,1)} %copy-done.15, ...), custom_call_target="tpu_custom_call" | custom-call | flops 1600000000 | bytes 8000000 | tf_op jit(solution)/shard_map/kp/pallas_call | solution.py:251
  54.1 5.5 %k1.1 = (bf16[4,208,384]{2,1,0:T(8,128)(2,1)}, f32[4,8,256]{2,1,0:T(8,128)}) custom-call(bf16[4,208,1152]{2,1,0:T(8,128)(2,1)} %get-tuple-element.31.qkv_ref), custom_call_target="tpu_custom_call" | custom-call | flops 4000000000 | bytes 4000000 | tf_op jit(solution)/shard_map/k1/pallas_call | solution.py:218
  59.7 0.8 copy-done.13
  60.7 15.5 %k2.1 = (f32[4,197,384]{2,1,0:T(8,128)}, f32[4,208,384]{2,1,0:T(8,128)}, bf16[4,208,384]{2,1,0:T(8,128)(2,1)}, bf16[384,1792]{1,0:T(8,128)(2,1)}, bf16[384,1792]{1,0:T(8,128)(2,1)}, /*index=5*/f32[8,4608]{1,0:T(8,128)}) custom-call(s32[1]{0:T(128)} %bitcast.core_ref, s32[2]{0:T(128)} %bitcast.115, bf16[4,197,384]{2,1,0:T(8,128)(2,1)} %bitcast.86, ...), custom_call_target="tpu_custom_call" | custom-call | flops 8000000000 | bytes 16000000 | tf_op jit(solution)/shard_map/k2/pallas_call | solution.py:367
  76.2 4.3 %k3.2.rest_0_ = bf16[4,208,1152]{2,1,0:T(8,128)(2,1)} custom-call(bf16[4,208,1152]{2,1,0:T(8,128)(2,1)} %get-tuple-element.31.qkv_ref, f32[4,8,256]{2,1,0:T(8,128)} %get-tuple-element.38.lse_ref, bf16[4,208,384]{2,1,0:T(8,128)(2,1)} %get-tuple-element.39.do_ref), custom_call_target="tpu_custom_call" | custom-call | flops 2400000000 | bytes 4000000 | tf_op jit(solution)/shard_map/k3/pallas_call | solution.py:429
  80.5 4.1 %k3.3.dp_ref = bf16[4,208,1152]{2,1,0:T(8,128)(2,1)} custom-call(bf16[4,208,1152]{2,1,0:T(8,128)(2,1)} %get-tuple-element.31.qkv_ref, f32[4,8,256]{2,1,0:T(8,128)} %get-tuple-element.38.lse_ref, bf16[4,208,384]{2,1,0:T(8,128)(2,1)} %get-tuple-element.39.do_ref, bf16[4,208,1152]{2,1,0:T(8,128)(2,1)} %k3.2.rest_0_), custom_call_target="tpu_custom_call", output_to_operand_aliasing={{}: (3, {})} | custom-call | flops 2400000000 | bytes 4000000 | tf_op jit(solution)/shard_map/k3/pallas_call | solution.py:429
  84.6 6.2 %k4.1 = (bf16[16,112,128]{2,1,0:T(8,128)(2,1)}, bf16[16,112,128]{2,1,0:T(8,128)(2,1)}) custom-call(s32[1]{0:T(128)} %bitcast.core_ref, bf16[4,208,384]{2,1,0:T(8,128)(2,1)} %get-tuple-element.41.a1_ref, bf16[4,208,384]{2,1,0:T(8,128)(2,1)} %get-tuple-element.42.n1_ref, bf16[4,208,1152]{2,1,0:T(8,128)(2,1)} %k3.3.dp_ref, ...), custom_call_target="tpu_custom_call" | custom-call | flops 1000000000 | bytes 4000000 | tf_op jit(solution)/shard_map/k4/pallas_call | solution.py:499
  91.5 1.8 %collective-permute-start.14 = (bf16[2,2,2,24,896]{4,3,1,0,2:T(8,128)(2,1)S(1)}, bf16[2,2,2,24,896]{4,3,1,0,2:T(8,128)(2,1)S(1)}, u32[]{:S(2)}, u32[]{:S(2)}) collective-permute-start(bf16[2,2,2,24,896]{4,3,1,0,2:T(8,128)(2,1)S(1)} %select_bitcast_fusion), channel_id=1, source_target_pairs={{0,4},{1,5},{2,6},{3,7},{4,0},{5,1},{6,2},{7,3},{8,12},{9,13},{10,... | collective-permute-start | bytes 1032200 | tf_op jit(solution)/shard_map/ppermute | solution.py:543
  93.5 8.3 %collective-permute-done.14 = bf16[2,2,2,24,896]{4,3,1,0,2:T(8,128)(2,1)S(1)} collective-permute-done((bf16[2,2,2,24,896]{4,3,1,0,2:T(8,128)(2,1)S(1)}, bf16[2,2,2,24,896]{4,3,1,0,2:T(8,128)(2,1)S(1)}, u32[]{:S(2)}, u32[]{:S(2)}) %collective-permute-start.14) | collective-permute-done | bytes 344096 | tf_op jit(solution)/shard_map/ppermute | solution.py:543
  102.4 1.1 collective-permute-done.12
  103.6 0.4 collective-permute-start.13
  104.0 3.7 %collective-permute-done.15 = bf16[2,2,24,896]{3,2,1,0:T(8,128)(2,1)S(1)} collective-permute-done((bf16[2,2,24,896]{3,2,1,0:T(8,128)(2,1)S(1)}, bf16[2,2,24,896]{3,2,1,0:T(8,128)(2,1)S(1)}, u32[]{:S(2)}, u32[]{:S(2)}) %collective-permute-start.15) | collective-permute-done | bytes 172064 | tf_op jit(solution)/shard_map/ppermute | solution.py:543
  107.8 1.3 collective-permute-done.13
  109.2 2.0 %collective-permute-start.16 = (bf16[2,24,1792]{2,1,0:T(8,128)(2,1)S(1)}, bf16[2,24,1792]{2,1,0:T(8,128)(2,1)S(1)}, u32[]{:S(2)}, u32[]{:S(2)}) collective-permute-start(bf16[2,24,1792]{2,1,0:T(8,128)(2,1)S(1)} %select_bitcast_fusion.2), channel_id=1, source_target_pairs={{0,16},{1,17},{2,18},{3,19},{4,20},{5,21},{6,22},{7,23},{8,24},{9,... | collective-permute-start | bytes 516104 | tf_op jit(solution)/shard_map/ppermute | solution.py:543
  111.2 0.9 add_convert_fusion.1
  112.1 3.7 %all-to-all-start.1 = ((bf16[16,112,128]{2,1,0:T(8,128)(2,1)}), bf16[16,112,128]{2,1,0:T(8,128)(2,1)S(1)}, u32[]{:S(2)}, u32[]{:S(2)}) async-start(bf16[16,112,128]{2,1,0:T(8,128)(2,1)} %add_convert_fusion.1), calls=%async_computation.1 | async-start | bytes 917504 | tf_op jit(solution)/shard_map/all_to_all | solution.py:547
  115.9 4.1 %collective-permute-done.16 = bf16[2,24,1792]{2,1,0:T(8,128)(2,1)S(1)} collective-permute-done((bf16[2,24,1792]{2,1,0:T(8,128)(2,1)S(1)}, bf16[2,24,1792]{2,1,0:T(8,128)(2,1)S(1)}, u32[]{:S(2)}, u32[]{:S(2)}) %collective-permute-start.16) | collective-permute-done | bytes 172064 | tf_op jit(solution)/shard_map/ppermute | solution.py:543
  120.0 1.7 %collective-permute-start.17 = (bf16[24,1792]{1,0:T(8,128)(2,1)S(1)}, bf16[24,1792]{1,0:T(8,128)(2,1)S(1)}, u32[]{:S(2)}, u32[]{:S(2)}) collective-permute-start(bf16[24,1792]{1,0:T(8,128)(2,1)S(1)} %select_bitcast_fusion.5), channel_id=1, source_target_pairs={{0,8},{1,9},{2,10},{3,11},{4,12},{5,13},{6,14},{7,15},{8,0},{9,1},... | collective-permute-start | bytes 258056 | tf_op jit(solution)/shard_map/ppermute | solution.py:543
  121.8 5.0 %collective-permute-done.17 = bf16[24,1792]{1,0:T(8,128)(2,1)S(1)} collective-permute-done((bf16[24,1792]{1,0:T(8,128)(2,1)S(1)}, bf16[24,1792]{1,0:T(8,128)(2,1)S(1)}, u32[]{:S(2)}, u32[]{:S(2)}) %collective-permute-start.17) | collective-permute-done | bytes 86048 | tf_op jit(solution)/shard_map/ppermute | solution.py:543
  126.9 1.6 %copy.53 = f32[2,2,197,384]{3,1,2,0:T(2,128)} copy(f32[2,2,197,384]{3,2,1,0:T(8,128)S(1)} %bitcast.88) | data formatting | bytes 2420736 | tf_op jit(solution)/shard_map/reshape | solution.py:656
  128.5 5.4 %k5.1 = f32[4,197,384]{2,1,0:T(8,128)} custom-call(bf16[4,197,384]{2,1,0:T(8,128)(2,1)} %bitcast.87, f32[4,208,384]{2,1,0:T(8,128)} %get-tuple-element.37.dr_ref, bf16[4,208,1152]{2,1,0:T(8,128)(2,1)} %k3.3.dp_ref, bf16[384,1152]{1,0:T(8,128)(2,1)} %get-tuple-element.40.w_ref, f32[1,4608]{1,0:T(1,128)} %get-tuple-element.35.vec_ref), custom_call_target="tpu_custom_call" | custom-call | flops 800000000 | bytes 8000000 | tf_op jit(solution)/shard_map/k5/pallas_call | solution.py:454
  134.0 2.9 %copy.52 = f32[2,2,197,384]{3,1,2,0:T(2,128)} copy(f32[2,2,197,384]{3,2,1,0:T(8,128)} %bitcast.84) | data formatting | bytes 2420736 | tf_op jit(solution)/shard_map/reshape | solution.py:656
  136.9 0.8 copy-done
  137.7 1.7 %total.1 = (f32[108,128]{1,0:T(8,128)}, f32[1,24]{1,0:T(1,128)}, f32[1,120]{1,0:T(1,128)}) custom-call(bf16[16,112,128]{2,1,0:T(8,128)(2,1)} %copy-done), custom_call_target="tpu_custom_call" | custom-call | tf_op jit(solution)/shard_map/total/pallas_call | solution.py:678
  139.4 0.6 copy-done.11
  140.0 1.6 %last.1 = (f32[36,128]{1,0:T(8,128)}, f32[144,128]{1,0:T(8,128)}, f32[144,128]{1,0:T(8,128)}) custom-call(s32[1]{0:T(128)} %bitcast.core_ref, bf16[24,1792]{1,0:T(8,128)(2,1)} %copy-done.10, bf16[24,1792]{1,0:T(8,128)(2,1)} %copy-done.11), custom_call_target="tpu_custom_call" | custom-call | flops 1000000 | bytes 400000 | tf_op jit(solution)/shard_map/last/pallas_call | solution.py:534
  (70 shorter events, 3.4 us)
Async XLA Ops:
  2.1 1.6 %collective-permute-start.1 = (bf16[12,1792]{1,0:T(8,128)(2,1)}, bf16[12,1792]{1,0:T(8,128)(2,1)S(1)}, u32[]{:S(2)}, u32[]{:S(2)}) collective-permute-start(bf16[12,1792]{1,0:T(8,128)(2,1)} %get-tuple-element.34), channel_id=1, source_target_pairs={{0,1},{1,0},{2,3},{3,2},{4,5},{5,4},{6,7},{7,6},{8,9},{9,8},{10,11... | collective-permute-start | bytes 129032 | tf_op jit(solution)/shard_map/ppermute | solution.py:543
  3.7 0.6 copy-start.12
  5.8 10.4 %copy-start.3 = (bf16[24,1792]{1,0:T(8,128)(2,1)S(1)}, bf16[24,1792]{1,0:T(8,128)(2,1)}, u32[]{:S(2)}) copy-start(bf16[24,1792]{1,0:T(8,128)(2,1)} %merge.1) | copy-start | bytes 258052
  5.8 10.4 %collective-permute-start.2 = (bf16[24,1792]{1,0:T(8,128)(2,1)}, bf16[24,1792]{1,0:T(8,128)(2,1)S(1)}, u32[]{:S(2)}, u32[]{:S(2)}) collective-permute-start(bf16[24,1792]{1,0:T(8,128)(2,1)} %merge.1), channel_id=1, source_target_pairs={{0,16},{1,17},{2,18},{3,19},{4,20},{5,21},{6,22},{7,23},{8,24},{9,... | collective-permute-start | bytes 258056 | tf_op jit(solution)/shard_map/ppermute | solution.py:543
  11.4 27.1 %all-to-all-start = ((bf16[16,112,128]{2,1,0:T(8,128)(2,1)}), bf16[16,112,128]{2,1,0:T(8,128)(2,1)S(1)}, u32[]{:S(2)}, u32[]{:S(2)}) async-start(bf16[16,112,128]{2,1,0:T(8,128)(2,1)} %piece.1), calls=%async_computation | async-start | bytes 917504 | tf_op jit(solution)/shard_map/all_to_all | solution.py:547
  16.3 13.3 %collective-permute-start.3 = (bf16[2,24,1792]{2,1,0:T(8,128)(2,1)S(1)}, bf16[2,24,1792]{2,1,0:T(8,128)(2,1)S(1)}, u32[]{:S(2)}, u32[]{:S(2)}) collective-permute-start(bf16[2,24,1792]{2,1,0:T(8,128)(2,1)S(1)} %maximum_select_fusion.8), channel_id=1, source_target_pairs={{0,8},{1,9},{2,10},{3,11},{4,12},{5,13},{6,14},{7,15},{8,0},{9,1},... | collective-permute-start | bytes 516104 | tf_op jit(solution)/shard_map/ppermute | solution.py:543
  29.7 5.5 %collective-permute-start.4 = (bf16[2,2,24,896]{3,2,0,1:T(8,128)(2,1)S(1)}, bf16[2,2,24,896]{3,2,0,1:T(8,128)(2,1)S(1)}, u32[]{:S(2)}, u32[]{:S(2)}) collective-permute-start(bf16[2,2,24,896]{3,2,0,1:T(8,128)(2,1)S(1)} %get-tuple-element.63), channel_id=1, source_target_pairs={{0,2},{1,3},{2,0},{3,1},{4,6},{5,7},{6,4},{7,5},{8,10},{9,11},{10,... | collective-permute-start | bytes 516104 | tf_op jit(solution)/shard_map/ppermute | solution.py:543
  31.2 6.6 %collective-permute-start.6 = (bf16[2,2,24,896]{3,2,0,1:T(8,128)(2,1)S(1)}, bf16[2,2,24,896]{3,2,0,1:T(8,128)(2,1)S(1)}, u32[]{:S(2)}, u32[]{:S(2)}) collective-permute-start(bf16[2,2,24,896]{3,2,0,1:T(8,128)(2,1)S(1)} %get-tuple-element.62), channel_id=1, source_target_pairs={{0,4},{1,5},{2,6},{3,7},{4,0},{5,1},{6,2},{7,3},{8,12},{9,13},{10,... | collective-permute-start | bytes 516104 | tf_op jit(solution)/shard_map/ppermute | solution.py:543
  35.2 8.8 %collective-permute-start.5 = (bf16[2,2,2,24,896]{4,3,0,1,2:T(8,128)(2,1)S(1)}, bf16[2,2,2,24,896]{4,3,0,1,2:T(8,128)(2,1)S(1)}, u32[]{:S(2)}, u32[]{:S(2)}) collective-permute-start(bf16[2,2,2,24,896]{4,3,0,1,2:T(8,128)(2,1)S(1)} %maximum_select_fusion.4), channel_id=1, source_target_pairs={{0,4},{1,5},{2,6},{3,7},{4,0},{5,1},{6,2},{7,3},{8,12},{9,13},{10,... | collective-permute-start | bytes 1032200 | tf_op jit(solution)/shard_map/ppermute | solution.py:543
  37.9 7.3 %collective-permute-start.7 = (bf16[2,2,2,24,896]{4,3,0,1,2:T(8,128)(2,1)S(1)}, bf16[2,2,2,24,896]{4,3,0,1,2:T(8,128)(2,1)S(1)}, u32[]{:S(2)}, u32[]{:S(2)}) collective-permute-start(bf16[2,2,2,24,896]{4,3,0,1,2:T(8,128)(2,1)S(1)} %maximum_select_fusion.6), channel_id=1, source_target_pairs={{0,2},{1,3},{2,0},{3,1},{4,6},{5,7},{6,4},{7,5},{8,10},{9,11},{10,... | collective-permute-start | bytes 1032200 | tf_op jit(solution)/shard_map/ppermute | solution.py:543
  38.4 5.8 %copy-start.8 = (bf16[16,112,128]{2,1,0:T(8,128)(2,1)}, bf16[16,112,128]{2,1,0:T(8,128)(2,1)S(1)}, u32[]{:S(2)}) copy-start(bf16[16,112,128]{2,1,0:T(8,128)(2,1)S(1)} %all-to-all-done.own_ref) | copy-start | bytes 1376260
  38.4 9.8 %collective-permute-start = (bf16[16,112,128]{2,1,0:T(8,128)(2,1)S(1)}, bf16[16,112,128]{2,1,0:T(8,128)(2,1)S(1)}, u32[]{:S(2)}, u32[]{:S(2)}) collective-permute-start(bf16[16,112,128]{2,1,0:T(8,128)(2,1)S(1)} %all-to-all-done.own_ref), channel_id=1, source_target_pairs={{0,1},{1,0},{2,3},{3,2},{4,5},{5,4},{6,7},{7,6},{8,9},{9,8},{10,11... | collective-permute-start | bytes 1376264 | tf_op jit(solution)/shard_map/ppermute | solution.py:543
  44.2 1.3 copy-start.4
  45.2 1.1 copy-start.6
  45.4 1.9 %copy-start.7 = (bf16[2,2,197,384]{3,1,2,0:T(2,128)(2,1)S(1)}, bf16[2,2,197,384]{3,1,2,0:T(2,128)(2,1)}, u32[]{:S(2)}) copy-start(bf16[2,2,197,384]{3,1,2,0:T(2,128)(2,1)} %param.11) | copy-start | bytes 1815556
  45.5 8.7 %copy-start.5 = (bf16[2,2,2,2,24,896]{5,4,3,2,1,0:T(8,128)(2,1)}, bf16[2,2,2,2,24,896]{5,4,3,2,1,0:T(8,128)(2,1)S(1)}, u32[]{:S(2)}) copy-start(bf16[2,2,2,2,24,896]{5,4,3,2,1,0:T(8,128)(2,1)S(1)} %copy.31) | copy-start | bytes 2064388
  45.5 14.2 %collective-permute-start.9 = (bf16[384,896]{1,0:T(8,128)(2,1)S(1)}, bf16[384,896]{1,0:T(8,128)(2,1)S(1)}, u32[]{:S(2)}, u32[]{:S(2)}) collective-permute-start(bf16[384,896]{1,0:T(8,128)(2,1)S(1)} %bitcast.93), channel_id=1, source_target_pairs={{0,1},{1,0},{2,3},{3,2},{4,5},{5,4},{6,7},{7,6},{8,9},{9,8},{10,11... | collective-permute-start | bytes 2064392 | tf_op jit(solution)/shard_map/ppermute | solution.py:543
  45.6 14.1 %collective-permute-start.8 = (bf16[384,896]{1,0:T(8,128)(2,1)S(1)}, bf16[384,896]{1,0:T(8,128)(2,1)S(1)}, u32[]{:S(2)}, u32[]{:S(2)}) collective-permute-start(bf16[384,896]{1,0:T(8,128)(2,1)S(1)} %bitcast.91), channel_id=1, source_target_pairs={{0,1},{1,0},{2,3},{3,2},{4,5},{5,4},{6,7},{7,6},{8,9},{9,8},{10,11... | collective-permute-start | bytes 2064392 | tf_op jit(solution)/shard_map/ppermute | solution.py:543
  48.2 0.8 copy-start.15
  59.6 0.8 copy-start.13
  59.7 1.1 copy-start.14
  76.2 14.8 %collective-permute-start.11 = (bf16[384,1792]{1,0:T(8,128)(2,1)}, bf16[384,1792]{1,0:T(8,128)(2,1)S(1)}, u32[]{:S(2)}, u32[]{:S(2)}) collective-permute-start(bf16[384,1792]{1,0:T(8,128)(2,1)} %get-tuple-element.48), channel_id=1, source_target_pairs={{0,1},{1,0},{2,3},{3,2},{4,5},{5,4},{6,7},{7,6},{8,9},{9,8},{10,11... | collective-permute-start | bytes 4128776 | tf_op jit(solution)/shard_map/ppermute | solution.py:543
  84.6 6.5 %copy-start.1 = (bf16[384,1792]{1,0:T(8,128)(2,1)S(1)}, bf16[384,1792]{1,0:T(8,128)(2,1)}, u32[]{:S(2)}) copy-start(bf16[384,1792]{1,0:T(8,128)(2,1)} %get-tuple-element.47) | copy-start | bytes 4128772
  90.8 20.4 %collective-permute-start.10 = (bf16[16,112,128]{2,1,0:T(8,128)(2,1)}, bf16[16,112,128]{2,1,0:T(8,128)(2,1)S(1)}, u32[]{:S(2)}, u32[]{:S(2)}) collective-permute-start(bf16[16,112,128]{2,1,0:T(8,128)(2,1)} %get-tuple-element.45), channel_id=1, source_target_pairs={{0,1},{1,0},{2,3},{3,2},{4,5},{5,4},{6,7},{7,6},{8,9},{9,8},{10,11... | collective-permute-start | bytes 1376264 | tf_op jit(solution)/shard_map/ppermute | solution.py:543
  91.5 10.3 %collective-permute-start.14 = (bf16[2,2,2,24,896]{4,3,1,0,2:T(8,128)(2,1)S(1)}, bf16[2,2,2,24,896]{4,3,1,0,2:T(8,128)(2,1)S(1)}, u32[]{:S(2)}, u32[]{:S(2)}) collective-permute-start(bf16[2,2,2,24,896]{4,3,1,0,2:T(8,128)(2,1)S(1)} %select_bitcast_fusion), channel_id=1, source_target_pairs={{0,4},{1,5},{2,6},{3,7},{4,0},{5,1},{6,2},{7,3},{8,12},{9,13},{10,... | collective-permute-start | bytes 1032200 | tf_op jit(solution)/shard_map/ppermute | solution.py:543
  93.4 10.0 %collective-permute-start.12 = (bf16[2,2,2,24,896]{4,3,1,0,2:T(8,128)(2,1)S(1)}, bf16[2,2,2,24,896]{4,3,1,0,2:T(8,128)(2,1)S(1)}, u32[]{:S(2)}, u32[]{:S(2)}) collective-permute-start(bf16[2,2,2,24,896]{4,3,1,0,2:T(8,128)(2,1)S(1)} %select_bitcast_fusion.1), channel_id=1, source_target_pairs={{0,2},{1,3},{2,0},{3,1},{4,6},{5,7},{6,4},{7,5},{8,10},{9,11},{10,... | collective-permute-start | bytes 1032200 | tf_op jit(solution)/shard_map/ppermute | solution.py:543
  102.0 5.8 %collective-permute-start.15 = (bf16[2,2,24,896]{3,2,1,0:T(8,128)(2,1)S(1)}, bf16[2,2,24,896]{3,2,1,0:T(8,128)(2,1)S(1)}, u32[]{:S(2)}, u32[]{:S(2)}) collective-permute-start(bf16[2,2,24,896]{3,2,1,0:T(8,128)(2,1)S(1)} %select_bitcast_fusion.3), channel_id=1, source_target_pairs={{0,2},{1,3},{2,0},{3,1},{4,6},{5,7},{6,4},{7,5},{8,10},{9,11},{10,... | collective-permute-start | bytes 516104 | tf_op jit(solution)/shard_map/ppermute | solution.py:543
  103.6 7.7 %copy-start.9 = (bf16[16,112,128]{2,1,0:T(8,128)(2,1)S(1)}, bf16[16,112,128]{2,1,0:T(8,128)(2,1)}, u32[]{:S(2)}) copy-start(bf16[16,112,128]{2,1,0:T(8,128)(2,1)} %get-tuple-element.44) | copy-start | bytes 1376260
  103.6 5.5 %collective-permute-start.13 = (bf16[2,2,24,896]{3,2,1,0:T(8,128)(2,1)S(1)}, bf16[2,2,24,896]{3,2,1,0:T(8,128)(2,1)S(1)}, u32[]{:S(2)}, u32[]{:S(2)}) collective-permute-start(bf16[2,2,24,896]{3,2,1,0:T(8,128)(2,1)S(1)} %select_bitcast_fusion.4), channel_id=1, source_target_pairs={{0,4},{1,5},{2,6},{3,7},{4,0},{5,1},{6,2},{7,3},{8,12},{9,13},{10,... | collective-permute-start | bytes 516104 | tf_op jit(solution)/shard_map/ppermute | solution.py:543
  109.2 10.7 %collective-permute-start.16 = (bf16[2,24,1792]{2,1,0:T(8,128)(2,1)S(1)}, bf16[2,24,1792]{2,1,0:T(8,128)(2,1)S(1)}, u32[]{:S(2)}, u32[]{:S(2)}) collective-permute-start(bf16[2,24,1792]{2,1,0:T(8,128)(2,1)S(1)} %select_bitcast_fusion.2), channel_id=1, source_target_pairs={{0,16},{1,17},{2,18},{3,19},{4,20},{5,21},{6,22},{7,23},{8,24},{9,... | collective-permute-start | bytes 516104 | tf_op jit(solution)/shard_map/ppermute | solution.py:543
  112.1 14.7 %copy-start.2 = (f32[4,197,384]{2,1,0:T(8,128)S(1)}, f32[4,197,384]{2,1,0:T(8,128)}, u32[]{:S(2)}) copy-start(f32[4,197,384]{2,1,0:T(8,128)} %get-tuple-element.36) | copy-start | bytes 3631108
  112.1 24.8 %all-to-all-start.1 = ((bf16[16,112,128]{2,1,0:T(8,128)(2,1)}), bf16[16,112,128]{2,1,0:T(8,128)(2,1)S(1)}, u32[]{:S(2)}, u32[]{:S(2)}) async-start(bf16[16,112,128]{2,1,0:T(8,128)(2,1)} %add_convert_fusion.1), calls=%async_computation.1 | async-start | bytes 917504 | tf_op jit(solution)/shard_map/all_to_all | solution.py:547
  120.0 6.7 %collective-permute-start.17 = (bf16[24,1792]{1,0:T(8,128)(2,1)S(1)}, bf16[24,1792]{1,0:T(8,128)(2,1)S(1)}, u32[]{:S(2)}, u32[]{:S(2)}) collective-permute-start(bf16[24,1792]{1,0:T(8,128)(2,1)S(1)} %select_bitcast_fusion.5), channel_id=1, source_target_pairs={{0,8},{1,9},{2,10},{3,11},{4,12},{5,13},{6,14},{7,15},{8,0},{9,1},... | collective-permute-start | bytes 258056 | tf_op jit(solution)/shard_map/ppermute | solution.py:543
  126.8 7.2 %copy-start.10 = (bf16[24,1792]{1,0:T(8,128)(2,1)}, bf16[24,1792]{1,0:T(8,128)(2,1)S(1)}, u32[]{:S(2)}) copy-start(bf16[24,1792]{1,0:T(8,128)(2,1)S(1)} %fusion.6.own_ref) | copy-start | bytes 258052
  126.8 12.6 %collective-permute-start.18 = (bf16[24,1792]{1,0:T(8,128)(2,1)S(1)}, bf16[24,1792]{1,0:T(8,128)(2,1)S(1)}, u32[]{:S(2)}, u32[]{:S(2)}) collective-permute-start(bf16[24,1792]{1,0:T(8,128)(2,1)S(1)} %fusion.6.own_ref), channel_id=1, source_target_pairs={{0,1},{1,0},{2,3},{3,2},{4,5},{5,4},{6,7},{7,6},{8,9},{9,8},{10,11... | collective-permute-start | bytes 258056 | tf_op jit(solution)/shard_map/ppermute | solution.py:543
  136.9 0.8 copy-start
  139.4 0.6 copy-start.11

commit v4 on v3

--- a/solution.py
+++ b/solution.py
@@ -21,11 +21,10 @@
 bf16 = jnp.bfloat16
 G1, G2, B1, B2, BO, BF2, BQ, BV, BF1 = 0, 384, 768, 1152, 1536, 1920, 2304, 2688, 3072
 NV = 4608
-VMEM_LIMIT = 60 * 1024 * 1024
-
-
-def params(**kw):
-    return pltpu.CompilerParams(vmem_limit_bytes=VMEM_LIMIT, **kw)
+
+
+def params(mib):
+    return pltpu.CompilerParams(vmem_limit_bytes=mib * 1024 * 1024)
 
 
 def full(shape):
@@ -83,13 +82,13 @@
     return jnp.concatenate([z[:TAIL], jnp.where(ok, z[TAIL:], -1e30)], axis=0)
 
 
-def project(x_ref, w, vec, a1_ref, qkv_ref, n1_ref):
+def project(x_ref, w, vec, qkv_ref, t_ref):
     rows = stack_rows(x_ref)
     shape = (x_ref.shape[0], SP)
     n1, _ = norm_stats(rows)
     a1 = (n1 * vec[:, G1 : G1 + D] + vec[:, B1 : B1 + D]).astype(bf16)
-    a1_ref[...] = a1.reshape(shape + (D,))
-    n1_ref[...] = n1.astype(bf16).reshape(shape + (D,))
+    t_ref[:D, :] = tr(a1)
+    t_ref[D:, :] = n1.T.astype(bf16)
     for part, at in ((0, BQ), (1, None), (2, BV)):
         p = nn(a1, w[:, D * part : D * part + D])
         if at is not None:
@@ -159,7 +158,7 @@
         prep_kernel, name="prep", in_specs=[smem()] + [vm] * 3, out_specs=[vm] * 2, out_shape=[shape] * 2,
         scratch_shapes=[pltpu.VMEM(v.shape, f32) for v in (o, f1, f2)],
         cost_estimate=cost(1e6, 2e5),
-        compiler_params=params(),
+        compiler_params=params(60),
     )(core, o, f1, f2)
 
 
@@ -181,7 +180,7 @@
     return pl.pallas_call(
         piece_kernel, name="piece", in_specs=[vm] * 3, out_specs=vm,
         out_shape=jax.ShapeDtypeStruct((chips, piece_rows(q.shape[0] // 9), 128), bf16),
-        compiler_params=params(),
+        compiler_params=params(60),
     )(q, g, b)
 
 
@@ -204,7 +203,7 @@
         merge_kernel, name="merge", in_specs=[smem(), vm, vm], out_specs=vm,
         out_shape=jax.ShapeDtypeStruct((2 * own.shape[0], C2), bf16),
         cost_estimate=cost(1e6, 2e5),
-        compiler_params=params(),
+        compiler_params=params(4),
     )(core, own, recv)
 
 
@@ -224,11 +223,11 @@
         out_shape=[jax.ShapeDtypeStruct((n, SP, D), bf16), jax.ShapeDtypeStruct((n, 8, SQ), f32)],
         input_output_aliases={1 + k: k for k in range(len(prev))},
         cost_estimate=cost(count * 1e9, count * 1e6, count * 3e5),
-        compiler_params=params(),
+        compiler_params=params(16),
     )(qkv, *prev)
 
 
-def kp_kernel(core_ref, own_ref, recv_ref, x_ref, w_ref, vec_ref, a1_ref, qkv_ref, n1_ref, s_s, w_s):
+def kp_kernel(core_ref, own_ref, recv_ref, x_ref, w_ref, vec_ref, qkv_ref, t_ref, s_s, w_s):
     core = core_ref[0]
     s_s[core] = own_ref[...].astype(f32)
     s_s[1 - core] = recv_ref[...].astype(f32)
@@ -242,19 +241,23 @@
         vec_ref[0:1, 2 * D + nb * d : 2 * D + nb * d + nb] = s_s[d % 2, d // 2, 9 * per + 1 : 9 * per + 2, :nb]
     w = w_s[...].astype(bf16)
     w_ref[...] = w
-    project(x_ref, w, vec_ref[...], a1_ref, qkv_ref, n1_ref)
+    project(x_ref, w, vec_ref[...], qkv_ref, t_ref)
 
 
 def kp(core, own, recv, x):
     n = x.shape[0]
     vm = pl.BlockSpec(memory_space=pltpu.VMEM)
     return pl.pallas_call(
-        kp_kernel, name="kp", in_specs=[smem()] + [vm] * 3, out_specs=[vm] * 5,
-        out_shape=[jax.ShapeDtypeStruct((D, 3 * D), bf16), jax.ShapeDtypeStruct((1, NV), f32)]
-        + [jax.ShapeDtypeStruct((n, SP, c), bf16) for c in (D, 3 * D, D)],
+        kp_kernel, name="kp", in_specs=[smem()] + [vm] * 3, out_specs=[vm] * 4,
+        out_shape=[
+            jax.ShapeDtypeStruct((D, 3 * D), bf16),
+            jax.ShapeDtypeStruct((1, NV), f32),
+            jax.ShapeDtypeStruct((n, SP, 3 * D), bf16),
+            jax.ShapeDtypeStruct((2 * D, n * SP), bf16),
+        ],
         scratch_shapes=[pltpu.VMEM((2,) + own.shape, f32), pltpu.VMEM((D, 3 * D), f32)],
         cost_estimate=cost(n * 4e8, n * 2e6),
-        compiler_params=params(),
+        compiler_params=params(20),
     )(core, own, recv, x)
 
 
@@ -388,7 +391,7 @@
             pltpu.VMEM((D, D), bf16),
         ],
         cost_estimate=cost(n * 2e9, n * 4e6, n * 6e5),
-        compiler_params=params(),
+        compiler_params=params(44),
     )(core, counts, x, g, o, *own, *recv, vec)
 
 
@@ -435,7 +438,7 @@
         out_shape=jax.ShapeDtypeStruct((n, SP, 3 * D), bf16),
         input_output_aliases={3 + k: k for k in range(len(prev))},
         cost_estimate=cost(count * 1.2e9, count * 2e6, count * 3e5),
-        compiler_params=params(),
+        compiler_params=params(16),
     )(qkv, lse, do, *prev)
 
 
@@ -459,17 +462,17 @@
         out_specs=blk(S, D),
         out_shape=jax.ShapeDtypeStruct((n, S, D), f32),
         cost_estimate=cost(n * 2e8, n * 2e6),
-        compiler_params=params(),
+        compiler_params=params(16),
     )(x, dr, dp, w, vec)
 
 
-def k4_kernel(core_ref, a1_ref, n1_ref, dp_ref, w_ref, sums2_ref, keep_ref, send_ref, v_s, q_s, t_s):
+def k4_kernel(core_ref, rows_ref, dp_ref, w_ref, sums2_ref, keep_ref, send_ref, v_s, q_s, t_s):
     core = core_ref[0]
     dpall = dp_ref[...].reshape(-1, 3 * D)
-    q_s[...] = nn(tr(a1_ref[...].reshape(-1, D)), dpall)
+    q_s[...] = nn(rows_ref[:D, :], dpall)
     bsum = nn(jnp.ones((8, dpall.shape[0]), bf16), dpall)
     weight = w_ref[...].astype(f32)
-    gain = jnp.sum(weight * nn(tr(n1_ref[...].reshape(-1, D)), dpall), axis=1, keepdims=True)
+    gain = jnp.sum(weight * nn(rows_ref[D:, :], dpall), axis=1, keepdims=True)
     shift = jnp.sum(weight * bsum[0:1, :], axis=1, keepdims=True)
     lane = lax.broadcasted_iota(jnp.int32, (D, 128), 1)
     both = jnp.where(lane == 0, gain, shift).T
@@ -492,17 +495,17 @@
     send_ref[...] = t_s[1 - core].astype(bf16)
 
 
-def k4(core, a1, n1, dp, w, sums2, chips):
+def k4(core, rows_t, dp, w, sums2, chips):
     vm = pl.BlockSpec(memory_space=pltpu.VMEM)
     rows = piece_rows(D // (2 * chips))
     shape = jax.ShapeDtypeStruct((chips, rows, 128), bf16)
     return pl.pallas_call(
         k4_kernel, name="k4",
-        in_specs=[smem()] + [vm] * 5, out_specs=[vm] * 2, out_shape=[shape] * 2,
+        in_specs=[smem()] + [vm] * 4, out_specs=[vm] * 2, out_shape=[shape] * 2,
         scratch_shapes=[pltpu.VMEM((1, NV), f32), pltpu.VMEM((D, 3 * D), f32), pltpu.VMEM((2, chips, rows, 128), f32)],
         cost_estimate=cost(1e9, 4e6),
-        compiler_params=params(),
-    )(core, a1, n1, dp, w, sums2)
+        compiler_params=params(20),
+    )(core, rows_t, dp, w, sums2)
 
 
 def last_kernel(core_ref, own_ref, recv_ref, o_ref, f1_ref, f2_ref):
@@ -535,7 +538,7 @@
         last_kernel, name="last", in_specs=[smem()] + [vm] * 2, out_specs=[vm] * 3,
         out_shape=[jax.ShapeDtypeStruct((k * rows, 128), f32) for k in (3, 12, 12)],
         cost_estimate=cost(1e6, 4e5),
-        compiler_params=params(),
+        compiler_params=params(4),
     )(core, own, recv)
 
 
@@ -626,7 +629,7 @@
     p2 = merge(core, own, swap(send, 0, n))
     f_own = gather_chips(p2, me, n)
     f_recv = [swap(f, 0, n) for f in f_own]
-    w, vec, a1, qkv, n1 = kp(core, q_own, q_recv, x)
+    w, vec, qkv, rows_t = kp(core, q_own, q_recv, x)
     o, lse = k1(qkv, 0, ni)
     counts = lax.optimization_barrier(counts.reshape(-1) + 0)
     out, dr, do, keep2, send2, sums2 = k2(core, counts, x, g, o, f_own, f_recv, vec, chips, cap)
@@ -635,7 +638,7 @@
     dp = ()
     for part in range(2):
         dp = (k3(qkv, lse, do, half * part, half, dp),)
-    keep1, send1 = k4(core, a1, n1, dp[0], w, sums2, chips)
+    keep1, send1 = k4(core, rows_t, dp[0], w, sums2, chips)
     sum1 = add(keep1, swap(send1, 0, n))
     g_qkv, g_gain, g_bias = total(exchange(sum1, n))
     dx = k5(x, dr, dp[0], w, vec)
@@ -678,7 +681,7 @@
     return pl.pallas_call(
         total_kernel, name="total", in_specs=[vm], out_specs=[vm] * 3,
         out_shape=[jax.ShapeDtypeStruct(s, f32) for s in shapes],
-        compiler_params=params(),
+        compiler_params=params(4),
     )(x)
 
 
@@ -709,12 +712,12 @@
     ni = mb * cap
     x = images.reshape(ni, S, D)
     g = out_grad.reshape(ni, S, D)
-    w, vec, a1, qkv, n1 = kp(zero, flat[0::2], flat[1::2], x)
+    w, vec, qkv, rows_t = kp(zero, flat[0::2], flat[1::2], x)
     o, lse = k1(qkv, 0, ni)
     out, dr, do, set0, set1, sums2 = k2(zero, counts.reshape(-1), x, g, o, halves_of(sets[0]), halves_of(sets[1]), vec, pieces, cap)
     dp = k3(qkv, lse, do, 0, ni)
     dx = k5(x, dr, dp, w, vec)
-    q0, q1 = k4(zero, a1, n1, dp, w, sums2, pieces)
+    q0, q1 = k4(zero, rows_t, dp, w, sums2, pieces)
     q01 = jnp.stack([q0, q1], 1).reshape(parts, rows, 128)
     g_qkv = q01[:, : 9 * per]
     g_gain = q01[:, 9 * per, : 2 * D // parts]

time: 143 us -> 118 us (0.83)
  Pallas kernels: 54.1 us -> 34.9 us
  local copies, waits for them, and re-layouts: 10.9 us -> 5.03 us
  other arithmetic: 2.47 us -> 4.25 us
  waiting for transfers between devices: 45.8 us -> 44.3 us
    pallas_call x2, Pallas kernels: 8.36 us -> 4.77 us  [k3(): pl.pallas_call(k3_kernel, name='k3', grid=(count,), in_specs=[blk(SP, 3 *...]
    pallas_call x1, Pallas kernels: 6.19 us -> 2.98 us  [k4(): pl.pallas_call(k4_kernel, name='k4', in_specs=[smem()] + [vm] * 4, out_sp...]
    pallas_call x1, Pallas kernels: 5.44 us -> 2.38 us  [k5(): pl.pallas_call(k5_kernel, name='k5', grid=(n,), in_specs=[blk(S, D), blk(...]
    pallas_call x1, Pallas kernels: 15.5 us -> 12.4 us  [k2(): pl.pallas_call(functools.partial(k2_kernel, pieces=pieces, cap=cap), name...]
    pallas_call x1, Pallas kernels: 5.17 us -> 2.11 us  [kp(): pl.pallas_call(kp_kernel, name='kp', in_specs=[smem()] + [vm] * 3, out_sp...]
    unnamed x32 -> x20, local copies, waits for them, and re-layouts: 4.18 us -> 1.28 us
    pallas_call x1, Pallas kernels: 5.5 us -> 3.79 us  [k1(): pl.pallas_call(k1_kernel, name='k1', grid=(count,), in_specs=[blk(SP, 3 *...]
    transpose x2, local copies, waits for them, and re-layouts: 1.87 us -> 0.16 us  [by_image(): return tokens.transpose(0, 2, 1, 3).reshape(mb * cap, S, D)]
  transfers between devices with their start and end apart: 21 -> 21, of which waited for: 12 -> 12; matrix products, arithmetic and copies ran while one was open for 7% -> 7% of each run, Pallas kernels for 24% -> 16%
where the time goes in v4:
time: 118 us; the launch traced here: 117 us
  waiting for transfers between devices  44.3 us (38%)
  Pallas kernels  34.9 us (30%)
  starting transfers between devices  27.9 us (24%)
  local copies, waits for them, and re-layouts  5.03 us (4%)
  other arithmetic  4.25 us (4%)
    ppermute x19, waiting for transfers between devices, swap(): return lax.ppermute(v, 'fsdp', [(i, i ^ 1 << bit) for i in range(n)])  44.3 us
    ppermute x19, starting transfers between devices, swap(): return lax.ppermute(v, 'fsdp', [(i, i ^ 1 << bit) for i in range(n)])  18.9 us
    pallas_call x1, Pallas kernels, k2(): pl.pallas_call(functools.partial(k2_kernel, pieces=pieces, cap=cap), name...  12.4 us
    all_to_all x2, starting transfers between devices, exchange(): return lax.all_to_all(v, 'fsdp', 0, 0, axis_index_groups=chip_groups(n))  9.06 us
    pallas_call x2, Pallas kernels, k3(): pl.pallas_call(k3_kernel, name='k3', grid=(count,), in_specs=[blk(SP, 3 *...  4.77 us
    pallas_call x1, Pallas kernels, k1(): pl.pallas_call(k1_kernel, name='k1', grid=(count,), in_specs=[blk(SP, 3 *...  3.79 us
    reshape x2, local copies, waits for them, and re-layouts, by_slot(): tokens = lax.optimization_barrier(v.reshape(shape).transpose(0, 2, 1, 3))  3.29 us
    pallas_call x1, Pallas kernels, k4(): pl.pallas_call(k4_kernel, name='k4', in_specs=[smem()] + [vm] * 4, out_sp...  2.98 us
  transfers between devices with their start and end apart: 21, of which 12 were waited for; matrix products, arithmetic and copies ran while one was open for 7% of the time, Pallas kernels for 16%

profile of v4, /device:TPU:0, one launch (start us, length us, event | category | flops | bytes accessed | tf_op | source)
XLA Modules:
  0.0 117.4 jit_solution(5690803355088912686)
XLA Ops:
  0.6 1.5 %prep.1 = (bf16[12,1792]{1,0:T(8,128)(2,1)}, bf16[12,1792]{1,0:T(8,128)(2,1)}) custom-call(s32[1]{0:T(128)} %bitcast.core_ref, bf16[36,128]{1,0:T(8,128)(2,1)} %bitcast.109, bf16[144,128]{1,0:T(8,128)(2,1)} %bitcast.106, bf16[144,128]{1,0:T(8,128)(2,1)} %bitcast.107), custom_call_target="tpu_custom_call" | custom-call | flops 1000000 | bytes 200000 | tf_op jit(solution)/shard_map/prep/pallas_call | solution.py:157
  2.1 0.5 collective-permute-start.1
  2.6 1.1 collective-permute-done.1.recv_ref
  3.7 0.8 copy-done.4
  4.6 4.0 %collective-permute-start.2 = (bf16[24,1792]{1,0:T(8,128)(2,1)S(1)}, bf16[24,1792]{1,0:T(8,128)(2,1)S(1)}, u32[]{:S(2)}, u32[]{:S(2)}) collective-permute-start(bf16[24,1792]{1,0:T(8,128)(2,1)S(1)} %merge.1), channel_id=1, source_target_pairs={{0,16},{1,17},{2,18},{3,19},{4,20},{5,21},{6,22},{7,23},{8,24},{9,... | collective-permute-start | bytes 258056 | tf_op jit(solution)/shard_map/ppermute | solution.py:546
  8.6 1.6 %piece.1 = bf16[16,112,128]{2,1,0:T(8,128)(2,1)} custom-call(bf16[108,128]{1,0:T(8,128)(2,1)} %bitcast.108, bf16[1,24]{1,0:T(2,128)(2,1)} %bitcast.110, bf16[1,120]{1,0:T(2,128)(2,1)} %bitcast.111), custom_call_target="tpu_custom_call" | custom-call | tf_op jit(solution)/shard_map/piece/pallas_call | solution.py:180
  10.1 4.8 %all-to-all-start = ((bf16[16,112,128]{2,1,0:T(8,128)(2,1)}), bf16[16,112,128]{2,1,0:T(8,128)(2,1)S(1)}, u32[]{:S(2)}, u32[]{:S(2)}) async-start(bf16[16,112,128]{2,1,0:T(8,128)(2,1)} %piece.1), calls=%async_computation | async-start | bytes 917504 | tf_op jit(solution)/shard_map/all_to_all | solution.py:550
  15.0 2.0 %collective-permute-start.3 = (bf16[2,24,1792]{2,1,0:T(8,128)(2,1)S(1)}, bf16[2,24,1792]{2,1,0:T(8,128)(2,1)S(1)}, u32[]{:S(2)}, u32[]{:S(2)}) collective-permute-start(bf16[2,24,1792]{2,1,0:T(8,128)(2,1)S(1)} %maximum_select_fusion.8), channel_id=1, source_target_pairs={{0,8},{1,9},{2,10},{3,11},{4,12},{5,13},{6,14},{7,15},{8,0},{9,1},... | collective-permute-start | bytes 516104 | tf_op jit(solution)/shard_map/ppermute | solution.py:546
  17.0 11.3 %collective-permute-done.3 = bf16[2,24,1792]{2,1,0:T(8,128)(2,1)S(1)} collective-permute-done((bf16[2,24,1792]{2,1,0:T(8,128)(2,1)S(1)}, bf16[2,24,1792]{2,1,0:T(8,128)(2,1)S(1)}, u32[]{:S(2)}, u32[]{:S(2)}) %collective-permute-start.3) | collective-permute-done | bytes 172064 | tf_op jit(solution)/shard_map/ppermute | solution.py:546
  28.5 1.5 %collective-permute-start.4 = (bf16[2,2,24,896]{3,2,0,1:T(8,128)(2,1)S(1)}, bf16[2,2,24,896]{3,2,0,1:T(8,128)(2,1)S(1)}, u32[]{:S(2)}, u32[]{:S(2)}) collective-permute-start(bf16[2,2,24,896]{3,2,0,1:T(8,128)(2,1)S(1)} %get-tuple-element.61), channel_id=1, source_target_pairs={{0,2},{1,3},{2,0},{3,1},{4,6},{5,7},{6,4},{7,5},{8,10},{9,11},{10,... | collective-permute-start | bytes 516104 | tf_op jit(solution)/shard_map/ppermute | solution.py:546
  30.0 1.5 %collective-permute-start.6 = (bf16[2,2,24,896]{3,2,0,1:T(8,128)(2,1)S(1)}, bf16[2,2,24,896]{3,2,0,1:T(8,128)(2,1)S(1)}, u32[]{:S(2)}, u32[]{:S(2)}) collective-permute-start(bf16[2,2,24,896]{3,2,0,1:T(8,128)(2,1)S(1)} %get-tuple-element.60), channel_id=1, source_target_pairs={{0,4},{1,5},{2,6},{3,7},{4,0},{5,1},{6,2},{7,3},{8,12},{9,13},{10,... | collective-permute-start | bytes 516104 | tf_op jit(solution)/shard_map/ppermute | solution.py:546
  31.5 2.5 %collective-permute-done.4 = bf16[2,2,24,896]{3,2,0,1:T(8,128)(2,1)S(1)} collective-permute-done((bf16[2,2,24,896]{3,2,0,1:T(8,128)(2,1)S(1)}, bf16[2,2,24,896]{3,2,0,1:T(8,128)(2,1)S(1)}, u32[]{:S(2)}, u32[]{:S(2)}) %collective-permute-start.4) | collective-permute-done | bytes 172064 | tf_op jit(solution)/shard_map/ppermute | solution.py:546
  34.0 1.5 %collective-permute-start.5 = (bf16[2,2,2,24,896]{4,3,0,1,2:T(8,128)(2,1)S(1)}, bf16[2,2,2,24,896]{4,3,0,1,2:T(8,128)(2,1)S(1)}, u32[]{:S(2)}, u32[]{:S(2)}) collective-permute-start(bf16[2,2,2,24,896]{4,3,0,1,2:T(8,128)(2,1)S(1)} %maximum_select_fusion.4), channel_id=1, source_target_pairs={{0,4},{1,5},{2,6},{3,7},{4,0},{5,1},{6,2},{7,3},{8,12},{9,13},{10,... | collective-permute-start | bytes 1032200 | tf_op jit(solution)/shard_map/ppermute | solution.py:546
  35.5 1.1 collective-permute-done.6
  36.7 0.4 collective-permute-start.7
  37.3 5.4 %collective-permute-done.5 = bf16[2,2,2,24,896]{4,3,0,1,2:T(8,128)(2,1)S(1)} collective-permute-done((bf16[2,2,2,24,896]{4,3,0,1,2:T(8,128)(2,1)S(1)}, bf16[2,2,2,24,896]{4,3,0,1,2:T(8,128)(2,1)S(1)}, u32[]{:S(2)}, u32[]{:S(2)}) %collective-permute-start.5) | collective-permute-done | bytes 344096 | tf_op jit(solution)/shard_map/ppermute | solution.py:546
  42.8 0.1 maximum_select_fusion
  43.0 1.0 collective-permute-done.7
  44.3 0.5 collective-permute-start.8
  44.8 0.3 copy-done.8
  45.4 2.1 %kp.1 = (bf16[384,1152]{1,0:T(8,128)(2,1)S(1)}, f32[1,4608]{1,0:T(1,128)S(1)}, bf16[4,208,1152]{2,1,0:T(8,128)(2,1)S(1)}, bf16[768,832]{1,0:T(8,128)(2,1)S(1)}) custom-call(s32[1]{0:T(128)} %bitcast.core_ref, bf16[16,112,128]{2,1,0:T(8,128)(2,1)S(1)} %all-to-all-done.own_ref, bf16[16,112,128]{2,1,0:T(8,128)(2,1)S(1)} %collective-permute-done.recv_ref, ...), custom_call_target="tpu_custom_call" | custom-call | flops 1600000000 | bytes 8000000 | tf_op jit(solution)/shard_map/kp/pallas_call | solution.py:250
  47.5 3.8 %k1.1 = (bf16[4,208,384]{2,1,0:T(8,128)(2,1)S(1)}, f32[4,8,256]{2,1,0:T(8,128)S(1)}) custom-call(bf16[4,208,1152]{2,1,0:T(8,128)(2,1)S(1)} %get-tuple-element.30.qkv_ref), custom_call_target="tpu_custom_call" | custom-call | flops 4000000000 | bytes 4000000 | tf_op jit(solution)/shard_map/k1/pallas_call | solution.py:217
  51.4 12.4 %k2.1 = (f32[4,197,384]{2,1,0:T(8,128)S(1)}, f32[4,208,384]{2,1,0:T(8,128)S(1)}, bf16[4,208,384]{2,1,0:T(8,128)(2,1)S(1)}, bf16[384,1792]{1,0:T(8,128)(2,1)S(1)}...) custom-call(s32[1]{0:T(128)} %bitcast.core_ref, s32[2]{0:T(128)S(1)} %bitcast.94, bf16[4,197,384]{2,1,0:T(8,128)(2,1)S(1)} %bitcast.84, ...), custom_call_target="tpu_custom_call" | custom-call | flops 8000000000 | bytes 16000000 | tf_op jit(solution)/shard_map/k2/pallas_call | solution.py:370
  63.8 2.5 %k3.2.rest_0_ = bf16[4,208,1152]{2,1,0:T(8,128)(2,1)S(1)} custom-call(bf16[4,208,1152]{2,1,0:T(8,128)(2,1)S(1)} %get-tuple-element.30.qkv_ref, f32[4,8,256]{2,1,0:T(8,128)S(1)} %get-tuple-element.37.lse_ref, bf16[4,208,384]{2,1,0:T(8,128)(2,1)S(1)} %get-tuple-element.38.do_ref), custom_call_target="tpu_custom_call" | custom-call | flops 2400000000 | bytes 4000000 | tf_op jit(solution)/shard_map/k3/pallas_call | solution.py:432
  66.3 2.3 %k3.3.dp_ref = bf16[4,208,1152]{2,1,0:T(8,128)(2,1)S(1)} custom-call(bf16[4,208,1152]{2,1,0:T(8,128)(2,1)S(1)} %get-tuple-element.30.qkv_ref, f32[4,8,256]{2,1,0:T(8,128)S(1)} %get-tuple-element.37.lse_ref, bf16[4,208,384]{2,1,0:T(8,128)(2,1)S(1)} %get-tuple-element.38.do_ref, bf16[4,208,1152]{2,1,0:T(8,128)(2,1)S(1)} %k3.2.rest_0_), custom_call_target="tpu_custom_call", output_to_operand_aliasing={{}: (3, {})} | custom-call | flops 2400000000 | bytes 4000000 | tf_op jit(solution)/shard_map/k3/pallas_call | solution.py:432
  68.6 3.0 %k4.1 = (bf16[16,112,128]{2,1,0:T(8,128)(2,1)S(1)}, bf16[16,112,128]{2,1,0:T(8,128)(2,1)S(1)}) custom-call(s32[1]{0:T(128)} %bitcast.core_ref, bf16[768,832]{1,0:T(8,128)(2,1)S(1)} %get-tuple-element.40.rows_ref, bf16[4,208,1152]{2,1,0:T(8,128)(2,1)S(1)} %k3.3.dp_ref, bf16[384,1152]{1,0:T(8,128)(2,1)S(1)} %get-tuple-element.39.w_ref, ...), custom_call_target="tpu_custom_call" | custom-call | flops 1000000000 | bytes 4000000 | tf_op jit(solution)/shard_map/k4/pallas_call | solution.py:502
  71.6 0.3 collective-permute-start.10
  72.0 0.3 add_convert_fusion
  72.4 1.8 %collective-permute-start.14 = (bf16[2,2,2,24,896]{4,3,1,0,2:T(8,128)(2,1)S(1)}, bf16[2,2,2,24,896]{4,3,1,0,2:T(8,128)(2,1)S(1)}, u32[]{:S(2)}, u32[]{:S(2)}) collective-permute-start(bf16[2,2,2,24,896]{4,3,1,0,2:T(8,128)(2,1)S(1)} %select_bitcast_fusion), channel_id=1, source_target_pairs={{0,4},{1,5},{2,6},{3,7},{4,0},{5,1},{6,2},{7,3},{8,12},{9,13},{10,... | collective-permute-start | bytes 1032200 | tf_op jit(solution)/shard_map/ppermute | solution.py:546
  74.4 8.3 %collective-permute-done.14 = bf16[2,2,2,24,896]{4,3,1,0,2:T(8,128)(2,1)S(1)} collective-permute-done((bf16[2,2,2,24,896]{4,3,1,0,2:T(8,128)(2,1)S(1)}, bf16[2,2,2,24,896]{4,3,1,0,2:T(8,128)(2,1)S(1)}, u32[]{:S(2)}, u32[]{:S(2)}) %collective-permute-start.14) | collective-permute-done | bytes 344096 | tf_op jit(solution)/shard_map/ppermute | solution.py:546
  82.9 0.4 collective-permute-start.15
  83.3 1.1 collective-permute-done.12
  84.5 0.4 collective-permute-start.13
  84.9 3.7 %collective-permute-done.15 = bf16[2,2,24,896]{3,2,1,0:T(8,128)(2,1)S(1)} collective-permute-done((bf16[2,2,24,896]{3,2,1,0:T(8,128)(2,1)S(1)}, bf16[2,2,24,896]{3,2,1,0:T(8,128)(2,1)S(1)}, u32[]{:S(2)}, u32[]{:S(2)}) %collective-permute-start.15) | collective-permute-done | bytes 172064 | tf_op jit(solution)/shard_map/ppermute | solution.py:546
  88.7 1.3 %collective-permute-done.13 = bf16[2,2,24,896]{3,2,1,0:T(8,128)(2,1)S(1)} collective-permute-done((bf16[2,2,24,896]{3,2,1,0:T(8,128)(2,1)S(1)}, bf16[2,2,24,896]{3,2,1,0:T(8,128)(2,1)S(1)}, u32[]{:S(2)}, u32[]{:S(2)}) %collective-permute-start.13) | collective-permute-done | bytes 172064 | tf_op jit(solution)/shard_map/ppermute | solution.py:546
  90.1 0.7 select_bitcast_fusion.2
  90.8 2.0 %collective-permute-start.16 = (bf16[2,24,1792]{2,1,0:T(8,128)(2,1)}, bf16[2,24,1792]{2,1,0:T(8,128)(2,1)}, u32[]{:S(2)}, u32[]{:S(2)}) collective-permute-start(bf16[2,24,1792]{2,1,0:T(8,128)(2,1)} %select_bitcast_fusion.2), channel_id=1, source_target_pairs={{0,16},{1,17},{2,18},{3,19},{4,20},{5,21},{6,22},{7,23},{8,24},{9,... | collective-permute-start | bytes 516104 | tf_op jit(solution)/shard_map/ppermute | solution.py:546
  92.8 0.9 add_convert_fusion.1
  93.7 4.2 %all-to-all-start.1 = ((bf16[16,112,128]{2,1,0:T(8,128)(2,1)}), bf16[16,112,128]{2,1,0:T(8,128)(2,1)}, u32[]{:S(2)}, u32[]{:S(2)}) async-start(bf16[16,112,128]{2,1,0:T(8,128)(2,1)} %add_convert_fusion.1), calls=%async_computation.1 | async-start | bytes 917504 | tf_op jit(solution)/shard_map/all_to_all | solution.py:550
  97.9 2.4 %collective-permute-done.16 = bf16[2,24,1792]{2,1,0:T(8,128)(2,1)} collective-permute-done((bf16[2,24,1792]{2,1,0:T(8,128)(2,1)}, bf16[2,24,1792]{2,1,0:T(8,128)(2,1)}, u32[]{:S(2)}, u32[]{:S(2)}) %collective-permute-start.16) | collective-permute-done | bytes 172064 | tf_op jit(solution)/shard_map/ppermute | solution.py:546
  100.3 1.2 fusion.2
  101.5 1.7 %collective-permute-start.17 = (bf16[24,1792]{1,0:T(8,128)(2,1)S(1)}, bf16[24,1792]{1,0:T(8,128)(2,1)S(1)}, u32[]{:S(2)}, u32[]{:S(2)}) collective-permute-start(bf16[24,1792]{1,0:T(8,128)(2,1)S(1)} %select_bitcast_fusion.5), channel_id=1, source_target_pairs={{0,8},{1,9},{2,10},{3,11},{4,12},{5,13},{6,14},{7,15},{8,0},{9,1},... | collective-permute-start | bytes 258056 | tf_op jit(solution)/shard_map/ppermute | solution.py:546
  103.2 5.1 %collective-permute-done.17 = bf16[24,1792]{1,0:T(8,128)(2,1)S(1)} collective-permute-done((bf16[24,1792]{1,0:T(8,128)(2,1)S(1)}, bf16[24,1792]{1,0:T(8,128)(2,1)S(1)}, u32[]{:S(2)}, u32[]{:S(2)}) %collective-permute-start.17) | collective-permute-done | bytes 86048 | tf_op jit(solution)/shard_map/ppermute | solution.py:546
  108.4 1.6 %copy.53 = f32[2,2,197,384]{3,1,2,0:T(2,128)} copy(f32[2,2,197,384]{3,2,1,0:T(8,128)S(1)} %bitcast.86) | data formatting | bytes 2420736 | tf_op jit(solution)/shard_map/reshape | solution.py:659
  110.1 2.4 %k5.1 = f32[4,197,384]{2,1,0:T(8,128)S(1)} custom-call(bf16[4,197,384]{2,1,0:T(8,128)(2,1)S(1)} %bitcast.85, f32[4,208,384]{2,1,0:T(8,128)S(1)} %copy-done.1, bf16[4,208,1152]{2,1,0:T(8,128)(2,1)S(1)} %k3.3.dp_ref, bf16[384,1152]{1,0:T(8,128)(2,1)S(1)} %get-tuple-element.39.w_ref, f32[1,4608]{1,0:T(1,128)S(1)} %get-tuple-element.34.vec_ref), custom_call_target="tpu_custom_call" | custom-call | flops 800000000 | bytes 8000000 | tf_op jit(solution)/shard_map/k5/pallas_call | solution.py:457
  112.5 1.6 %copy.52 = f32[2,2,197,384]{3,1,2,0:T(2,128)} copy(f32[2,2,197,384]{3,2,1,0:T(8,128)S(1)} %bitcast.82) | data formatting | bytes 2420736 | tf_op jit(solution)/shard_map/reshape | solution.py:659
  114.1 1.7 %total.1 = (f32[108,128]{1,0:T(8,128)}, f32[1,24]{1,0:T(1,128)}, f32[1,120]{1,0:T(1,128)}) custom-call(bf16[16,112,128]{2,1,0:T(8,128)(2,1)} %all-to-all-done.1.x_ref), custom_call_target="tpu_custom_call" | custom-call | tf_op jit(solution)/shard_map/total/pallas_call | solution.py:681
  115.8 1.6 %last.1 = (f32[36,128]{1,0:T(8,128)}, f32[144,128]{1,0:T(8,128)}, f32[144,128]{1,0:T(8,128)}) custom-call(s32[1]{0:T(128)} %bitcast.core_ref, bf16[24,1792]{1,0:T(8,128)(2,1)S(1)} %fusion.6.own_ref, bf16[24,1792]{1,0:T(8,128)(2,1)} %collective-permute-done.18.recv_ref), custom_call_target="tpu_custom_call" | custom-call | flops 1000000 | bytes 400000 | tf_op jit(solution)/shard_map/last/pallas_call | solution.py:537
  (58 shorter events, 2.0 us)
Async XLA Ops:
  2.1 1.6 %collective-permute-start.1 = (bf16[12,1792]{1,0:T(8,128)(2,1)}, bf16[12,1792]{1,0:T(8,128)(2,1)S(1)}, u32[]{:S(2)}, u32[]{:S(2)}) collective-permute-start(bf16[12,1792]{1,0:T(8,128)(2,1)} %get-tuple-element.33), channel_id=1, source_target_pairs={{0,1},{1,0},{2,3},{3,2},{4,5},{5,4},{6,7},{7,6},{8,9},{9,8},{10,11... | collective-permute-start | bytes 129032 | tf_op jit(solution)/shard_map/ppermute | solution.py:546
  3.7 0.8 copy-start.4
  4.6 10.4 %collective-permute-start.2 = (bf16[24,1792]{1,0:T(8,128)(2,1)S(1)}, bf16[24,1792]{1,0:T(8,128)(2,1)S(1)}, u32[]{:S(2)}, u32[]{:S(2)}) collective-permute-start(bf16[24,1792]{1,0:T(8,128)(2,1)S(1)} %merge.1), channel_id=1, source_target_pairs={{0,16},{1,17},{2,18},{3,19},{4,20},{5,21},{6,22},{7,23},{8,24},{9,... | collective-permute-start | bytes 258056 | tf_op jit(solution)/shard_map/ppermute | solution.py:546
  10.1 27.1 %all-to-all-start = ((bf16[16,112,128]{2,1,0:T(8,128)(2,1)}), bf16[16,112,128]{2,1,0:T(8,128)(2,1)S(1)}, u32[]{:S(2)}, u32[]{:S(2)}) async-start(bf16[16,112,128]{2,1,0:T(8,128)(2,1)} %piece.1), calls=%async_computation | async-start | bytes 917504 | tf_op jit(solution)/shard_map/all_to_all | solution.py:550
  15.0 13.3 %collective-permute-start.3 = (bf16[2,24,1792]{2,1,0:T(8,128)(2,1)S(1)}, bf16[2,24,1792]{2,1,0:T(8,128)(2,1)S(1)}, u32[]{:S(2)}, u32[]{:S(2)}) collective-permute-start(bf16[2,24,1792]{2,1,0:T(8,128)(2,1)S(1)} %maximum_select_fusion.8), channel_id=1, source_target_pairs={{0,8},{1,9},{2,10},{3,11},{4,12},{5,13},{6,14},{7,15},{8,0},{9,1},... | collective-permute-start | bytes 516104 | tf_op jit(solution)/shard_map/ppermute | solution.py:546
  28.5 5.5 %collective-permute-start.4 = (bf16[2,2,24,896]{3,2,0,1:T(8,128)(2,1)S(1)}, bf16[2,2,24,896]{3,2,0,1:T(8,128)(2,1)S(1)}, u32[]{:S(2)}, u32[]{:S(2)}) collective-permute-start(bf16[2,2,24,896]{3,2,0,1:T(8,128)(2,1)S(1)} %get-tuple-element.61), channel_id=1, source_target_pairs={{0,2},{1,3},{2,0},{3,1},{4,6},{5,7},{6,4},{7,5},{8,10},{9,11},{10,... | collective-permute-start | bytes 516104 | tf_op jit(solution)/shard_map/ppermute | solution.py:546
  30.0 6.6 %collective-permute-start.6 = (bf16[2,2,24,896]{3,2,0,1:T(8,128)(2,1)S(1)}, bf16[2,2,24,896]{3,2,0,1:T(8,128)(2,1)S(1)}, u32[]{:S(2)}, u32[]{:S(2)}) collective-permute-start(bf16[2,2,24,896]{3,2,0,1:T(8,128)(2,1)S(1)} %get-tuple-element.60), channel_id=1, source_target_pairs={{0,4},{1,5},{2,6},{3,7},{4,0},{5,1},{6,2},{7,3},{8,12},{9,13},{10,... | collective-permute-start | bytes 516104 | tf_op jit(solution)/shard_map/ppermute | solution.py:546
  34.0 8.8 %collective-permute-start.5 = (bf16[2,2,2,24,896]{4,3,0,1,2:T(8,128)(2,1)S(1)}, bf16[2,2,2,24,896]{4,3,0,1,2:T(8,128)(2,1)S(1)}, u32[]{:S(2)}, u32[]{:S(2)}) collective-permute-start(bf16[2,2,2,24,896]{4,3,0,1,2:T(8,128)(2,1)S(1)} %maximum_select_fusion.4), channel_id=1, source_target_pairs={{0,4},{1,5},{2,6},{3,7},{4,0},{5,1},{6,2},{7,3},{8,12},{9,13},{10,... | collective-permute-start | bytes 1032200 | tf_op jit(solution)/shard_map/ppermute | solution.py:546
  36.7 7.3 %collective-permute-start.7 = (bf16[2,2,2,24,896]{4,3,0,1,2:T(8,128)(2,1)S(1)}, bf16[2,2,2,24,896]{4,3,0,1,2:T(8,128)(2,1)S(1)}, u32[]{:S(2)}, u32[]{:S(2)}) collective-permute-start(bf16[2,2,2,24,896]{4,3,0,1,2:T(8,128)(2,1)S(1)} %maximum_select_fusion.6), channel_id=1, source_target_pairs={{0,2},{1,3},{2,0},{3,1},{4,6},{5,7},{6,4},{7,5},{8,10},{9,11},{10,... | collective-permute-start | bytes 1032200 | tf_op jit(solution)/shard_map/ppermute | solution.py:546
  37.2 8.2 %collective-permute-start = (bf16[16,112,128]{2,1,0:T(8,128)(2,1)S(1)}, bf16[16,112,128]{2,1,0:T(8,128)(2,1)S(1)}, u32[]{:S(2)}, u32[]{:S(2)}) collective-permute-start(bf16[16,112,128]{2,1,0:T(8,128)(2,1)S(1)} %all-to-all-done.own_ref), channel_id=1, source_target_pairs={{0,1},{1,0},{2,3},{3,2},{4,5},{5,4},{6,7},{7,6},{8,9},{9,8},{10,11... | collective-permute-start | bytes 1376264 | tf_op jit(solution)/shard_map/ppermute | solution.py:546
  44.0 1.1 copy-start.8
  44.2 1.2 copy-start.9
  44.2 7.1 %collective-permute-start.9 = (bf16[384,896]{1,0:T(8,128)(2,1)S(1)}, bf16[384,896]{1,0:T(8,128)(2,1)S(1)}, u32[]{:S(2)}, u32[]{:S(2)}) collective-permute-start(bf16[384,896]{1,0:T(8,128)(2,1)S(1)} %bitcast.91), channel_id=1, source_target_pairs={{0,1},{1,0},{2,3},{3,2},{4,5},{5,4},{6,7},{7,6},{8,9},{9,8},{10,11... | collective-permute-start | bytes 2064392 | tf_op jit(solution)/shard_map/ppermute | solution.py:546
  44.3 7.0 %collective-permute-start.8 = (bf16[384,896]{1,0:T(8,128)(2,1)S(1)}, bf16[384,896]{1,0:T(8,128)(2,1)S(1)}, u32[]{:S(2)}, u32[]{:S(2)}) collective-permute-start(bf16[384,896]{1,0:T(8,128)(2,1)S(1)} %bitcast.89), channel_id=1, source_target_pairs={{0,1},{1,0},{2,3},{3,2},{4,5},{5,4},{6,7},{7,6},{8,9},{9,8},{10,11... | collective-permute-start | bytes 2064392 | tf_op jit(solution)/shard_map/ppermute | solution.py:546
  47.5 3.8 %copy-start.5 = (s32[2,1]{0,1:T(1,128)S(1)}, s32[2,1]{0,1:T(1,128)}, u32[]{:S(2)}) copy-start(s32[2,1]{0,1:T(1,128)} %param.10) | copy-start | bytes 28
  63.8 2.5 %copy-start = (f32[4,208,384]{2,1,0:T(8,128)}, f32[4,208,384]{2,1,0:T(8,128)S(1)}, u32[]{:S(2)}) copy-start(f32[4,208,384]{2,1,0:T(8,128)S(1)} %get-tuple-element.36.dr_ref) | copy-start | bytes 3833860
  63.8 2.5 %copy-start.2 = (f32[4,197,384]{2,1,0:T(8,128)}, f32[4,197,384]{2,1,0:T(8,128)S(1)}, u32[]{:S(2)}) copy-start(f32[4,197,384]{2,1,0:T(8,128)S(1)} %get-tuple-element.35) | copy-start | bytes 3631108
  63.8 8.1 %collective-permute-start.11 = (bf16[384,1792]{1,0:T(8,128)(2,1)}, bf16[384,1792]{1,0:T(8,128)(2,1)S(1)}, u32[]{:S(2)}, u32[]{:S(2)}) collective-permute-start(bf16[384,1792]{1,0:T(8,128)(2,1)} %get-tuple-element.46), channel_id=1, source_target_pairs={{0,1},{1,0},{2,3},{3,2},{4,5},{5,4},{6,7},{7,6},{8,9},{9,8},{10,11... | collective-permute-start | bytes 4128776 | tf_op jit(solution)/shard_map/ppermute | solution.py:546
  71.6 21.1 %collective-permute-start.10 = (bf16[16,112,128]{2,1,0:T(8,128)(2,1)S(1)}, bf16[16,112,128]{2,1,0:T(8,128)(2,1)S(1)}, u32[]{:S(2)}, u32[]{:S(2)}) collective-permute-start(bf16[16,112,128]{2,1,0:T(8,128)(2,1)S(1)} %get-tuple-element.43), channel_id=1, source_target_pairs={{0,1},{1,0},{2,3},{3,2},{4,5},{5,4},{6,7},{7,6},{8,9},{9,8},{10,11... | collective-permute-start | bytes 1376264 | tf_op jit(solution)/shard_map/ppermute | solution.py:546
  72.4 10.3 %collective-permute-start.14 = (bf16[2,2,2,24,896]{4,3,1,0,2:T(8,128)(2,1)S(1)}, bf16[2,2,2,24,896]{4,3,1,0,2:T(8,128)(2,1)S(1)}, u32[]{:S(2)}, u32[]{:S(2)}) collective-permute-start(bf16[2,2,2,24,896]{4,3,1,0,2:T(8,128)(2,1)S(1)} %select_bitcast_fusion), channel_id=1, source_target_pairs={{0,4},{1,5},{2,6},{3,7},{4,0},{5,1},{6,2},{7,3},{8,12},{9,13},{10,... | collective-permute-start | bytes 1032200 | tf_op jit(solution)/shard_map/ppermute | solution.py:546
  74.3 10.0 %collective-permute-start.12 = (bf16[2,2,2,24,896]{4,3,1,0,2:T(8,128)(2,1)S(1)}, bf16[2,2,2,24,896]{4,3,1,0,2:T(8,128)(2,1)S(1)}, u32[]{:S(2)}, u32[]{:S(2)}) collective-permute-start(bf16[2,2,2,24,896]{4,3,1,0,2:T(8,128)(2,1)S(1)} %select_bitcast_fusion.1), channel_id=1, source_target_pairs={{0,2},{1,3},{2,0},{3,1},{4,6},{5,7},{6,4},{7,5},{8,10},{9,11},{10,... | collective-permute-start | bytes 1032200 | tf_op jit(solution)/shard_map/ppermute | solution.py:546
  82.9 5.8 %collective-permute-start.15 = (bf16[2,2,24,896]{3,2,1,0:T(8,128)(2,1)S(1)}, bf16[2,2,24,896]{3,2,1,0:T(8,128)(2,1)S(1)}, u32[]{:S(2)}, u32[]{:S(2)}) collective-permute-start(bf16[2,2,24,896]{3,2,1,0:T(8,128)(2,1)S(1)} %select_bitcast_fusion.3), channel_id=1, source_target_pairs={{0,2},{1,3},{2,0},{3,1},{4,6},{5,7},{6,4},{7,5},{8,10},{9,11},{10,... | collective-permute-start | bytes 516104 | tf_op jit(solution)/shard_map/ppermute | solution.py:546
  84.5 5.5 %collective-permute-start.13 = (bf16[2,2,24,896]{3,2,1,0:T(8,128)(2,1)S(1)}, bf16[2,2,24,896]{3,2,1,0:T(8,128)(2,1)S(1)}, u32[]{:S(2)}, u32[]{:S(2)}) collective-permute-start(bf16[2,2,24,896]{3,2,1,0:T(8,128)(2,1)S(1)} %select_bitcast_fusion.4), channel_id=1, source_target_pairs={{0,4},{1,5},{2,6},{3,7},{4,0},{5,1},{6,2},{7,3},{8,12},{9,13},{10,... | collective-permute-start | bytes 516104 | tf_op jit(solution)/shard_map/ppermute | solution.py:546
  88.7 4.1 %copy-start.6 = (bf16[2,2,24,896]{3,2,1,0:T(8,128)(2,1)}, bf16[2,2,24,896]{3,2,1,0:T(8,128)(2,1)S(1)}, u32[]{:S(2)}) copy-start(bf16[2,2,24,896]{3,2,1,0:T(8,128)(2,1)S(1)} %fusion.3) | copy-start | bytes 516100
  90.0 2.7 %copy-start.7 = (bf16[2,2,24,896]{3,2,1,0:T(8,128)(2,1)}, bf16[2,2,24,896]{3,2,1,0:T(8,128)(2,1)S(1)}, u32[]{:S(2)}) copy-start(bf16[2,2,24,896]{3,2,1,0:T(8,128)(2,1)S(1)} %fusion.4) | copy-start | bytes 516100
  90.8 9.5 %collective-permute-start.16 = (bf16[2,24,1792]{2,1,0:T(8,128)(2,1)}, bf16[2,24,1792]{2,1,0:T(8,128)(2,1)}, u32[]{:S(2)}, u32[]{:S(2)}) collective-permute-start(bf16[2,24,1792]{2,1,0:T(8,128)(2,1)} %select_bitcast_fusion.2), channel_id=1, source_target_pairs={{0,16},{1,17},{2,18},{3,19},{4,20},{5,21},{6,22},{7,23},{8,24},{9,... | collective-permute-start | bytes 516104 | tf_op jit(solution)/shard_map/ppermute | solution.py:546
  93.7 20.5 %all-to-all-start.1 = ((bf16[16,112,128]{2,1,0:T(8,128)(2,1)}), bf16[16,112,128]{2,1,0:T(8,128)(2,1)}, u32[]{:S(2)}, u32[]{:S(2)}) async-start(bf16[16,112,128]{2,1,0:T(8,128)(2,1)} %add_convert_fusion.1), calls=%async_computation.1 | async-start | bytes 917504 | tf_op jit(solution)/shard_map/all_to_all | solution.py:550
  97.9 10.5 %copy-start.3 = (f32[4,197,384]{2,1,0:T(8,128)S(1)}, f32[4,197,384]{2,1,0:T(8,128)}, u32[]{:S(2)}) copy-start(f32[4,197,384]{2,1,0:T(8,128)} %copy-done.2) | copy-start | bytes 3631108
  101.5 8.6 %copy-start.1 = (f32[4,208,384]{2,1,0:T(8,128)S(1)}, f32[4,208,384]{2,1,0:T(8,128)}, u32[]{:S(2)}) copy-start(f32[4,208,384]{2,1,0:T(8,128)} %copy-done) | copy-start | bytes 3833860
  101.5 6.8 %collective-permute-start.17 = (bf16[24,1792]{1,0:T(8,128)(2,1)S(1)}, bf16[24,1792]{1,0:T(8,128)(2,1)S(1)}, u32[]{:S(2)}, u32[]{:S(2)}) collective-permute-start(bf16[24,1792]{1,0:T(8,128)(2,1)S(1)} %select_bitcast_fusion.5), channel_id=1, source_target_pairs={{0,8},{1,9},{2,10},{3,11},{4,12},{5,13},{6,14},{7,15},{8,0},{9,1},... | collective-permute-start | bytes 258056 | tf_op jit(solution)/shard_map/ppermute | solution.py:546
  108.3 7.5 %collective-permute-start.18 = (bf16[24,1792]{1,0:T(8,128)(2,1)S(1)}, bf16[24,1792]{1,0:T(8,128)(2,1)}, u32[]{:S(2)}, u32[]{:S(2)}) collective-permute-start(bf16[24,1792]{1,0:T(8,128)(2,1)S(1)} %fusion.6.own_ref), channel_id=1, source_target_pairs={{0,1},{1,0},{2,3},{3,2},{4,5},{5,4},{6,7},{7,6},{8,9},{9,8},{10,11... | collective-permute-start | bytes 258056 | tf_op jit(solution)/shard_map/ppermute | solution.py:546
